TPU v7x, 128 devices: a whole 4x4x4 slice. The times are simulated.
128 devices in a mesh: pipe: 2 (over core), tok: 64 (over y, z, x).
Axes of the slice: x: 4, y: 4, z: 4, core: 2. Of those that a mesh axis runs over, the one named last changes fastest.
Arguments:
- features: bfloat16 [2, 16384, 256], P(None, 'tok'), may hold values from -6 to 6
- coarse: bfloat16 [2, 4096, 256], P(None, 'tok'), may hold values from -6 to 6
- parent: int32 [2, 16384], P(None, 'tok'), may hold values from -1 to 4095, as said below
- counts: int32 [2, 64], replicated, may hold values from 1 to 256, 12288 in all within a row
- target: float32 [2, 16384], P(None, 'tok'), may hold values from -6 to 6
- gain_attn: float32 [2, 256], P('pipe'), may hold values from 0.25 to 1.75
- w_qkv: bfloat16 [2, 256, 768], P('pipe'), may hold values from -0.375 to 0.375
- w_out: bfloat16 [2, 256, 256], P('pipe'), may hold values from -0.375 to 0.375
- gain_mlp: float32 [2, 256], P('pipe'), may hold values from 0.25 to 1.75
- w_up: bfloat16 [2, 256, 1024], P('pipe'), may hold values from -0.375 to 0.375
- w_down: bfloat16 [2, 1024, 256], P('pipe'), may hold values from -0.1875 to 0.1875
- w_sdf: float32 [256], replicated, may hold values from -0.375 to 0.375
Outputs:
- loss: float32 [], replicated
- grad_sdf: float32 [256], replicated
- grad_gain_attn: float32 [2, 256], P('pipe')
- grad_qkv: float32 [2, 256, 768], P('pipe')
- grad_out: float32 [2, 256, 256], P('pipe')
- grad_gain_mlp: float32 [2, 256], P('pipe')
- grad_up: float32 [2, 256, 1024], P('pipe')
- grad_down: float32 [2, 1024, 256], P('pipe')
Inputs may be any that keep to these rules, and one draw needn't show every extreme that they name: parent never falls along the tokens of a micro-batch; the tokens of shard d (rows d * 256 to (d + 1) * 256 - 1) have parents d * 64 - 1 to (d + 1) * 64 - 1, the first token of every shard has parent d * 64 - 1, and every parent has a child.
All inputs are finite; a program needn't handle non-finite values.
Results may differ from a plain program's by a relative error of at most 0.005.
Values may be sent and summed in bfloat16 or wider, within the bound.
No kernel may reach another device: no remote copies, remote signals or barrier semaphores. Data moves between devices by JAX's collectives and lax.ppermute only.
A program may use at most 128 MiB of HBM per device.

v0:
```python
import math

import jax
import jax.numpy as jnp
from jax import lax
from jax.sharding import PartitionSpec as P

H = 8
WIN = 32


def from_behind(value, axis, steps):
    count = lax.axis_size(axis)
    initial, last = (max(0, -steps), min(count, count - steps))
    return lax.ppermute(value, axis, [(source, source + steps) for source in range(initial, last)])


def norm_gain(values, gain_vec):
    mean_sq = jnp.mean(values * values, axis=-1, keepdims=True)
    return values * lax.rsqrt(mean_sq + 1e-06) * gain_vec


def attend(packed, keys_ok):
    token_count = packed.shape[0]
    model_width = packed.shape[1] // 3
    head_size = model_width // H
    blocks = packed.reshape(token_count // WIN, WIN, 3, H, head_size)
    query_part = blocks[:, :, 0]
    key_part = blocks[:, :, 1]
    value_part = blocks[:, :, 2]
    scores = jnp.einsum(
        "wqhd,wkhd->whqk", query_part, key_part, preferred_element_type=jnp.float32
    ) * head_size ** (-0.5)
    allowed = keys_ok.reshape(token_count // WIN, 1, 1, WIN)
    scores = jnp.where(allowed, scores, -1e30)
    attn_weights = jax.nn.softmax(scores, axis=-1).astype(jnp.bfloat16)
    mixed_out = jnp.einsum(
        "whqk,wkhd->wqhd", attn_weights, value_part, preferred_element_type=jnp.float32
    )
    return mixed_out.reshape(token_count, model_width)


def matmul(left, right):
    return jnp.dot(left, right, preferred_element_type=jnp.float32)


def shards(
    features, coarse, parent, counts, target, gain_attn, w_qkv, w_out, gain_mlp, w_up, w_down, w_sdf
):
    pipe_section = lax.axis_index("pipe")
    device_idx = lax.axis_index("tok")
    rank_count = lax.axis_size("tok")
    micro_count, row_count, model_width = features.shape
    piece_rows = row_count // rank_count
    total_valid = 3 * row_count * rank_count // 4
    root_valid = math.sqrt(total_valid)
    first_section = pipe_section == 0
    gain_one = gain_attn[0]
    qkv_weight = w_qkv[0]
    out_weight = w_out[0]
    gain_two = gain_mlp[0]
    up_weight = w_up[0]
    down_weight = w_down[0]
    rim_row = from_behind(coarse[:, -1:, :], "tok", 1)
    parent_table = jnp.concatenate([rim_row, coarse], axis=1)
    local_parent = parent - device_idx * coarse.shape[1] + 1
    lifted = jnp.take_along_axis(parent_table, local_parent[:, :, None], axis=1)
    embedded = (features.astype(jnp.float32) + lifted.astype(jnp.float32)).astype(jnp.bfloat16)
    position = jnp.arange(row_count, dtype=jnp.int32)
    source = position // piece_rows
    window_pos = device_idx * piece_rows + position % piece_rows
    own_counts = jnp.take(counts, device_idx, axis=1)
    own_valid = position[None, :] < own_counts[:, None]
    window_valid = window_pos[None, :] < jnp.take(counts, source, axis=1)
    incoming = jnp.zeros((row_count, model_width), jnp.bfloat16)
    saved = []
    for clock_tick in range(micro_count + 1):
        early_mb = min(clock_tick, micro_count - 1)
        late_mb = max(clock_tick - 1, 0)
        block_in = jnp.where(first_section, embedded[early_mb], incoming)
        keys_ok = jnp.where(first_section, window_valid[early_mb], own_valid[late_mb])
        normed = norm_gain(block_in.astype(jnp.float32), gain_one).astype(jnp.bfloat16)
        packed = matmul(normed, qkv_weight).astype(jnp.bfloat16)
        packed_win = jnp.where(
            first_section,
            lax.all_to_all(packed, "tok", split_axis=0, concat_axis=0, tiled=True),
            packed,
        )
        mixed_win = attend(packed_win, keys_ok).astype(jnp.bfloat16)
        mixed_out = jnp.where(
            first_section,
            lax.all_to_all(mixed_win, "tok", split_axis=0, concat_axis=0, tiled=True),
            mixed_win,
        )
        after_attn = block_in.astype(jnp.float32) + matmul(mixed_out, out_weight)
        normed_two = norm_gain(after_attn, gain_two).astype(jnp.bfloat16)
        upward = matmul(normed_two, up_weight)
        hidden = jax.nn.gelu(upward).astype(jnp.bfloat16)
        block_out = (after_attn + matmul(hidden, down_weight)).astype(jnp.bfloat16)
        saved.append(
            (
                block_in,
                normed,
                packed_win,
                keys_ok,
                mixed_out,
                after_attn,
                normed_two,
                upward,
                hidden,
                block_out,
            )
        )
        if clock_tick < micro_count:
            incoming = from_behind(block_out, "pipe", 1)
    grad_totals = (
        jnp.zeros(gain_one.shape, jnp.float32),
        jnp.zeros(qkv_weight.shape, jnp.float32),
        jnp.zeros(out_weight.shape, jnp.float32),
        jnp.zeros(gain_two.shape, jnp.float32),
        jnp.zeros(up_weight.shape, jnp.float32),
        jnp.zeros(down_weight.shape, jnp.float32),
    )
    returned_grad = jnp.zeros((row_count, model_width), jnp.bfloat16)
    loss_total = jnp.zeros((), jnp.float32)
    sdf_total = jnp.zeros((model_width,), jnp.float32)
    for clock_tick in range(micro_count + 1):
        (
            block_in,
            normed,
            packed_win,
            keys_ok,
            mixed_out,
            after_attn,
            normed_two,
            upward,
            hidden,
            block_out,
        ) = saved[micro_count - clock_tick]
        late_mb = max(micro_count - 1 - clock_tick, 0)
        last_live = clock_tick < micro_count
        first_live = clock_tick >= 1
        out_float = block_out.astype(jnp.float32)
        predicted = jnp.sum(out_float * w_sdf, axis=-1)
        residue = jnp.where(own_valid[late_mb], predicted - target[late_mb], 0.0)
        slope_term = 2.0 * residue / root_valid
        head_grad = (slope_term[:, None] * w_sdf).astype(jnp.bfloat16)
        out_grad = jnp.where(first_section, returned_grad, head_grad)
        live_flag = jnp.where(first_section, first_live, last_live).astype(jnp.float32)
        grad_down = matmul(hidden.T, out_grad)
        hidden_grad = matmul(out_grad, down_weight.T).astype(jnp.bfloat16)
        gelu_back = jax.vjp(jax.nn.gelu, upward)[1]
        up_grad = gelu_back(hidden_grad.astype(jnp.float32))[0].astype(jnp.bfloat16)
        grad_up = matmul(normed_two.T, up_grad)
        normed_two_grad = matmul(up_grad, up_weight.T).astype(jnp.bfloat16)
        norm_back = jax.vjp(norm_gain, after_attn, gain_two)[1]
        attn_res_grad, grad_gain_two = norm_back(normed_two_grad.astype(jnp.float32))
        after_grad = out_grad.astype(jnp.float32) + attn_res_grad
        after_grad_low = after_grad.astype(jnp.bfloat16)
        grad_out = matmul(mixed_out.T, after_grad_low)
        mixed_grad = matmul(after_grad_low, out_weight.T).astype(jnp.bfloat16)
        mixed_grad_win = jnp.where(
            first_section,
            lax.all_to_all(mixed_grad, "tok", split_axis=0, concat_axis=0, tiled=True),
            mixed_grad,
        )
        attn_back = jax.vjp(lambda packed_in: attend(packed_in, keys_ok), packed_win)[1]
        packed_grad_win = attn_back(mixed_grad_win.astype(jnp.float32))[0]
        packed_grad = jnp.where(
            first_section,
            lax.all_to_all(packed_grad_win, "tok", split_axis=0, concat_axis=0, tiled=True),
            packed_grad_win,
        )
        grad_qkv = matmul(normed.T, packed_grad)
        normed_grad = matmul(packed_grad, qkv_weight.T).astype(jnp.bfloat16)
        in_back = jax.vjp(norm_gain, block_in.astype(jnp.float32), gain_one)[1]
        in_res_grad, grad_gain_one = in_back(normed_grad.astype(jnp.float32))
        in_grad = (after_grad + in_res_grad).astype(jnp.bfloat16)
        grad_terms = (
            grad_gain_one * live_flag,
            grad_qkv * live_flag,
            grad_out * live_flag,
            grad_gain_two * live_flag,
            grad_up * live_flag,
            grad_down * live_flag,
        )
        grad_totals = tuple((total + term for total, term in zip(grad_totals, grad_terms)))
        head_flag = jnp.where(first_section, 0.0, 1.0 if last_live else 0.0)
        loss_total = loss_total + head_flag * jnp.sum(residue * residue)
        sdf_total = sdf_total + head_flag * jnp.sum(slope_term[:, None] * out_float, axis=0)
        if clock_tick < micro_count:
            arriving = from_behind(in_grad, "pipe", -1)
            returned_grad = arriving
    grad_totals = lax.psum(grad_totals, "tok")
    loss_sum, grad_sdf = lax.psum((loss_total, sdf_total), ("pipe", "tok"))
    loss = loss_sum / (micro_count * total_valid)
    return (
        loss,
        grad_sdf,
        grad_totals[0][None],
        grad_totals[1][None],
        grad_totals[2][None],
        grad_totals[3][None],
        grad_totals[4][None],
        grad_totals[5][None],
    )


def solution(mesh):
    return jax.shard_map(
        shards,
        mesh=mesh,
        in_specs=(
            P(None, "tok", None),
            P(None, "tok", None),
            P(None, "tok"),
            P(),
            P(None, "tok"),
            P("pipe", None),
            P("pipe", None, None),
            P("pipe", None, None),
            P("pipe", None),
            P("pipe", None, None),
            P("pipe", None, None),
            P(),
        ),
        out_specs=(
            P(),
            P(),
            P("pipe", None),
            P("pipe", None, None),
            P("pipe", None, None),
            P("pipe", None),
            P("pipe", None, None),
            P("pipe", None, None),
        ),
        check_vma=False,
    )
```

profile of v0, /device:TPU:0, one launch (start us, length us, event | category | flops | bytes accessed | tf_op | source)
XLA Modules:
  0.0 585.1 jit_solution(10795170216960096335)
XLA Ops:
  19.9 11.1 %all-to-all-start = ((bf16[64,4,768]{2,1,0:T(4,128)(2,1)}), bf16[64,4,768]{2,1,0:T(4,128)(2,1)S(1)}, u32[]{:S(2)}, u32[]{:S(2)}) async-start(bf16[64,4,768]{2,1,0:T(4,128)(2,1)} %all_to_all.88), calls=%async_computation | async-start | bytes 786432 | tf_op jit(solution)/shard_map/all_to_all | solution.py:86
  33.0 9.8 %all-to-all-done = bf16[64,4,768]{2,1,0:T(4,128)(2,1)S(1)} async-done(((bf16[64,4,768]{2,1,0:T(4,128)(2,1)}), bf16[64,4,768]{2,1,0:T(4,128)(2,1)S(1)}, u32[]{:S(2)}, u32[]{:S(2)}) %all-to-all-start) | async-done | bytes 393248 | tf_op jit(solution)/shard_map/all_to_all | solution.py:86
  50.4 14.5 %all_to_all.132 = bf16[64,4,256]{2,1,0:T(4,128)(2,1)S(1)} all-to-all(bf16[64,4,256]{2,1,0:T(4,128)(2,1)S(1)} %convert_element_type.345), channel_id=1, replica_groups=mesh['pipe'=2,'tok'=64] {'tok'}, dimensions={0} | all-to-all | bytes 262144 | tf_op jit(solution)/shard_map/all_to_all | solution.py:92
  70.2 5.1 all-to-all-start.2
  75.4 12.5 %all-to-all-done.2 = bf16[64,4,768]{2,1,0:T(4,128)(2,1)S(1)} async-done(((bf16[64,4,768]{2,1,0:T(4,128)(2,1)}), bf16[64,4,768]{2,1,0:T(4,128)(2,1)S(1)}, u32[]{:S(2)}, u32[]{:S(2)}) %all-to-all-start.2) | async-done | bytes 393248 | tf_op jit(solution)/shard_map/all_to_all | solution.py:86
  99.5 4.7 all-to-all-start.3
  104.9 9.3 %all-to-all-done.3 = bf16[64,4,256]{2,1,0:T(4,128)(2,1)S(1)} async-done(((bf16[64,4,256]{2,1,0:T(4,128)(2,1)}), bf16[64,4,256]{2,1,0:T(4,128)(2,1)S(1)}, u32[]{:S(2)}, u32[]{:S(2)}) %all-to-all-start.3) | async-done | bytes 131104 | tf_op jit(solution)/shard_map/all_to_all | solution.py:92
  123.4 5.5 all-to-all-start.4
  133.9 6.7 %all-to-all-done.4 = bf16[64,4,768]{2,1,0:T(4,128)(2,1)S(1)} async-done(((bf16[64,4,768]{2,1,0:T(4,128)(2,1)}), bf16[64,4,768]{2,1,0:T(4,128)(2,1)S(1)}, u32[]{:S(2)}, u32[]{:S(2)}) %all-to-all-start.4) | async-done | bytes 393248 | tf_op jit(solution)/shard_map/all_to_all | solution.py:86
  157.9 9.9 %all-to-all-done.5 = bf16[64,4,256]{2,1,0:T(4,128)(2,1)S(1)} async-done(((bf16[64,4,256]{2,1,0:T(4,128)(2,1)}), bf16[64,4,256]{2,1,0:T(4,128)(2,1)S(1)}, u32[]{:S(2)}, u32[]{:S(2)}) %all-to-all-start.5) | async-done | bytes 131104 | tf_op jit(solution)/shard_map/all_to_all | solution.py:92
  175.5 5.1 all-to-all-start.6
  182.7 7.8 %all-to-all-done.6 = bf16[64,4,256]{2,1,0:T(4,128)(2,1)S(1)} async-done(((bf16[64,4,256]{2,1,0:T(4,128)(2,1)}), bf16[64,4,256]{2,1,0:T(4,128)(2,1)S(1)}, u32[]{:S(2)}, u32[]{:S(2)}) %all-to-all-start.6) | async-done | bytes 131104 | tf_op jit(solution)/shard_map/all_to_all | solution.py:164
  200.0 4.9 all-to-all-start.7
  209.6 6.7 %all-to-all-done.7 = bf16[64,4,768]{2,1,0:T(4,128)(2,1)S(1)} async-done(((bf16[64,4,768]{2,1,0:T(4,128)(2,1)}), bf16[64,4,768]{2,1,0:T(4,128)(2,1)S(1)}, u32[]{:S(2)}, u32[]{:S(2)}) %all-to-all-start.7) | async-done | bytes 393248 | tf_op jit(solution)/shard_map/all_to_all | solution.py:171
  234.8 4.9 all-to-all-start.8
  241.7 8.1 %all-to-all-done.8 = bf16[64,4,256]{2,1,0:T(4,128)(2,1)S(1)} async-done(((bf16[64,4,256]{2,1,0:T(4,128)(2,1)}), bf16[64,4,256]{2,1,0:T(4,128)(2,1)S(1)}, u32[]{:S(2)}, u32[]{:S(2)}) %all-to-all-start.8) | async-done | bytes 131104 | tf_op jit(solution)/shard_map/all_to_all | solution.py:164
  259.3 4.9 all-to-all-start.9
  270.3 6.5 %all-to-all-done.9 = bf16[64,4,768]{2,1,0:T(4,128)(2,1)S(1)} async-done(((bf16[64,4,768]{2,1,0:T(4,128)(2,1)}), bf16[64,4,768]{2,1,0:T(4,128)(2,1)S(1)}, u32[]{:S(2)}, u32[]{:S(2)}) %all-to-all-start.9) | async-done | bytes 393248 | tf_op jit(solution)/shard_map/all_to_all | solution.py:171
  288.6 5.0 all-to-all-start.10
  296.5 7.0 %all-to-all-done.10 = bf16[64,4,256]{2,1,0:T(4,128)(2,1)S(1)} async-done(((bf16[64,4,256]{2,1,0:T(4,128)(2,1)}), bf16[64,4,256]{2,1,0:T(4,128)(2,1)S(1)}, u32[]{:S(2)}, u32[]{:S(2)}) %all-to-all-start.10) | async-done | bytes 131104 | tf_op jit(solution)/shard_map/all_to_all | solution.py:164
  313.2 4.9 all-to-all-start.11
  322.3 7.3 %all-to-all-done.11 = bf16[64,4,768]{2,1,0:T(4,128)(2,1)S(1)} async-done(((bf16[64,4,768]{2,1,0:T(4,128)(2,1)}), bf16[64,4,768]{2,1,0:T(4,128)(2,1)S(1)}, u32[]{:S(2)}, u32[]{:S(2)}) %all-to-all-start.11) | async-done | bytes 393248 | tf_op jit(solution)/shard_map/all_to_all | solution.py:171
  333.0 63.4 %all-reduce.9 = (f32[]{:T(128)}, f32[256]{0:T(256)}) all-reduce(f32[]{:T(128)S(6)} %add.313, f32[256]{0:T(256)S(1)} %multiply_add_fusion), channel_id=1, replica_groups=mesh['pipe'=2,'tok'=64] {'pipe','tok'}, use_global_device_ids=true, to_apply=%region_18.19 | all-reduce | flops 257 | bytes 2056 | tf_op jit(solution)/shard_map/psum | solution.py:195
  397.5 174.4 %all-reduce.10 = (f32[1,256]{1,0:T(1,128)}, f32[1,256]{1,0:T(1,128)}) all-reduce(f32[1,256]{1,0:T(1,128)S(1)} %bitcast.359, f32[1,256]{1,0:T(1,128)S(1)} %bitcast.358), channel_id=1, replica_groups=mesh['pipe'=2,'tok'=64] {'tok'}, use_global_device_ids=true, to_apply=%region_34.35 | all-reduce | flops 512 | bytes 4096 | tf_op jit(solution)/shard_map/psum | solution.py:194
  (412 shorter events, 165.2 us)
Async XLA Ops:
  7.2 58.1 %copy-start = (bf16[1,256,1024]{2,1,0:T(8,128)(2,1)S(1)}, bf16[1,256,1024]{2,1,0:T(8,128)(2,1)}, u32[]{:S(2)}) copy-start(bf16[1,256,1024]{2,1,0:T(8,128)(2,1)} %param.21) | copy-start | bytes 1572868
  8.2 7.0 %collective-permute-start = (bf16[2,1,256]{2,0,1:T(2,128)(2,1)S(1)}, bf16[2,1,256]{2,0,1:T(2,128)(2,1)S(1)}, u32[]{:S(2)}, u32[]{:S(2)}) collective-permute-start(bf16[2,1,256]{2,0,1:T(2,128)(2,1)S(1)} %slice.100), channel_id=1, source_target_pairs={{0,1},{1,2},{2,3},{3,4},{4,5},{5,6},{6,7},{7,8},{8,9},{9,10},{10,1... | collective-permute-start | bytes 3080 | tf_op jit(solution)/shard_map/ppermute | solution.py:15
  18.5 102.5 %copy-start.8 = (bf16[2,256,256]{1,2,0:T(8,128)(2,1)}, bf16[2,256,256]{1,2,0:T(8,128)(2,1)S(1)}, u32[]{:S(2)}) copy-start(bf16[2,256,256]{1,2,0:T(8,128)(2,1)S(1)} %add_convert_fusion) | copy-start | bytes 786436
  19.9 22.9 %all-to-all-start = ((bf16[64,4,768]{2,1,0:T(4,128)(2,1)}), bf16[64,4,768]{2,1,0:T(4,128)(2,1)S(1)}, u32[]{:S(2)}, u32[]{:S(2)}) async-start(bf16[64,4,768]{2,1,0:T(4,128)(2,1)} %all_to_all.88), calls=%async_computation | async-start | bytes 786432 | tf_op jit(solution)/shard_map/all_to_all | solution.py:86
  66.6 2.3 collective-permute-start.1
  70.2 17.7 %all-to-all-start.2 = ((bf16[64,4,768]{2,1,0:T(4,128)(2,1)}), bf16[64,4,768]{2,1,0:T(4,128)(2,1)S(1)}, u32[]{:S(2)}, u32[]{:S(2)}) async-start(bf16[64,4,768]{2,1,0:T(4,128)(2,1)} %all_to_all.92), calls=%async_computation.2 | async-start | bytes 786432 | tf_op jit(solution)/shard_map/all_to_all | solution.py:86
  99.5 14.7 %all-to-all-start.3 = ((bf16[64,4,256]{2,1,0:T(4,128)(2,1)}), bf16[64,4,256]{2,1,0:T(4,128)(2,1)S(1)}, u32[]{:S(2)}, u32[]{:S(2)}) async-start(bf16[64,4,256]{2,1,0:T(4,128)(2,1)} %convert_element_type.355), calls=%async_computation.3 | async-start | bytes 262144 | tf_op jit(solution)/shard_map/all_to_all | solution.py:92
  117.7 3.3 collective-permute-start.2
  123.4 17.2 %all-to-all-start.4 = ((bf16[64,4,768]{2,1,0:T(4,128)(2,1)}), bf16[64,4,768]{2,1,0:T(4,128)(2,1)S(1)}, u32[]{:S(2)}, u32[]{:S(2)}) async-start(bf16[64,4,768]{2,1,0:T(4,128)(2,1)} %all_to_all.96), calls=%async_computation.4 | async-start | bytes 786432 | tf_op jit(solution)/shard_map/all_to_all | solution.py:86
  153.1 14.7 %all-to-all-start.5 = ((bf16[64,4,256]{2,1,0:T(4,128)(2,1)}), bf16[64,4,256]{2,1,0:T(4,128)(2,1)S(1)}, u32[]{:S(2)}, u32[]{:S(2)}) async-start(bf16[64,4,256]{2,1,0:T(4,128)(2,1)} %convert_element_type.365), calls=%async_computation.5 | async-start | bytes 262144 | tf_op jit(solution)/shard_map/all_to_all | solution.py:92
  175.5 15.0 %all-to-all-start.6 = ((bf16[64,4,256]{2,1,0:T(4,128)(2,1)}), bf16[64,4,256]{2,1,0:T(4,128)(2,1)S(1)}, u32[]{:S(2)}, u32[]{:S(2)}) async-start(bf16[64,4,256]{2,1,0:T(4,128)(2,1)} %all_to_all.100), calls=%async_computation.6 | async-start | bytes 262144 | tf_op jit(solution)/shard_map/all_to_all | solution.py:164
  200.0 16.3 %all-to-all-start.7 = ((bf16[64,4,768]{2,1,0:T(4,128)(2,1)}), bf16[64,4,768]{2,1,0:T(4,128)(2,1)S(1)}, u32[]{:S(2)}, u32[]{:S(2)}) async-start(bf16[64,4,768]{2,1,0:T(4,128)(2,1)} %all_to_all.103), calls=%async_computation.7 | async-start | bytes 786432 | tf_op jit(solution)/shard_map/all_to_all | solution.py:171
  223.3 5.1 collective-permute-start.3
  234.8 15.0 %all-to-all-start.8 = ((bf16[64,4,256]{2,1,0:T(4,128)(2,1)}), bf16[64,4,256]{2,1,0:T(4,128)(2,1)S(1)}, u32[]{:S(2)}, u32[]{:S(2)}) async-start(bf16[64,4,256]{2,1,0:T(4,128)(2,1)} %all_to_all.105), calls=%async_computation.8 | async-start | bytes 262144 | tf_op jit(solution)/shard_map/all_to_all | solution.py:164
  259.3 17.5 %all-to-all-start.9 = ((bf16[64,4,768]{2,1,0:T(4,128)(2,1)}), bf16[64,4,768]{2,1,0:T(4,128)(2,1)S(1)}, u32[]{:S(2)}, u32[]{:S(2)}) async-start(bf16[64,4,768]{2,1,0:T(4,128)(2,1)} %all_to_all.108), calls=%async_computation.9 | async-start | bytes 786432 | tf_op jit(solution)/shard_map/all_to_all | solution.py:171
  281.2 3.6 collective-permute-start.4
  288.6 14.9 %all-to-all-start.10 = ((bf16[64,4,256]{2,1,0:T(4,128)(2,1)}), bf16[64,4,256]{2,1,0:T(4,128)(2,1)S(1)}, u32[]{:S(2)}, u32[]{:S(2)}) async-start(bf16[64,4,256]{2,1,0:T(4,128)(2,1)} %all_to_all.110), calls=%async_computation.10 | async-start | bytes 262144 | tf_op jit(solution)/shard_map/all_to_all | solution.py:164
  313.2 16.5 %all-to-all-start.11 = ((bf16[64,4,768]{2,1,0:T(4,128)(2,1)}), bf16[64,4,768]{2,1,0:T(4,128)(2,1)S(1)}, u32[]{:S(2)}, u32[]{:S(2)}) async-start(bf16[64,4,768]{2,1,0:T(4,128)(2,1)} %all_to_all.113), calls=%async_computation.11 | async-start | bytes 786432 | tf_op jit(solution)/shard_map/all_to_all | solution.py:171
  318.1 253.7 %all-reduce.14.cloned.1.call-start = ((), (), s32[]{:S(2)}) async-start(), calls=%async_computation.12 | async-start | bytes 6291456 | tf_op jit(solution)/shard_map/psum | solution.py:194
  331.0 66.0 %copy-start.22 = (bf16[1,256,768]{2,1,0:T(8,128)(2,1)S(1)}, bf16[1,256,768]{2,1,0:T(8,128)(2,1)}, u32[]{:S(2)}) copy-start(bf16[1,256,768]{2,1,0:T(8,128)(2,1)} %param.18) | copy-start | bytes 1179652
  331.0 66.4 %copy-start.79 = (f32[256]{0:T(256)S(1)}, f32[256]{0:T(256)}, u32[]{:S(2)}) copy-start(f32[256]{0:T(256)} %get-tuple-element.19) | copy-start | bytes 3076
  331.0 66.4 %copy-start.80 = (f32[256]{0:T(256)S(1)}, f32[256]{0:T(256)}, u32[]{:S(2)}) copy-start(f32[256]{0:T(256)} %get-tuple-element.21) | copy-start | bytes 3076
  331.0 66.4 %copy-start.92 = (f32[256]{0:T(256)S(1)}, f32[256]{0:T(256)}, u32[]{:S(2)}) copy-start(f32[256]{0:T(256)} %get-tuple-element.25) | copy-start | bytes 3076
  331.1 66.4 %copy-start.93 = (f32[256]{0:T(256)S(1)}, f32[256]{0:T(256)}, u32[]{:S(2)}) copy-start(f32[256]{0:T(256)} %get-tuple-element.27) | copy-start | bytes 3076
  (97 other events, 529.3 us)
Sparse Core Ops, SparseCore 0:
  331.2 133.4 all-reduce.13
where the time goes:
time: 595 us; the launch traced here: 585 us
  blocking collectives  252 us (42%)
  waiting for transfers between devices  93.3 us (16%)
  starting transfers between devices  69.7 us (12%)
  local copies, waits for them, and re-layouts  66.5 us (11%)
  matrix products  62.2 us (10%)
  other arithmetic  21.1 us (4%)
  between operations  19.9 us (3%)
    psum x1, blocking collectives, shards(): grad_totals = lax.psum(grad_totals, 'tok')  174 us
    psum x1, blocking collectives, shards(): loss_sum, grad_sdf = lax.psum((loss_total, sdf_total), ('pipe', 'tok'))  63.4 us
    dot_general x36, matrix products, matmul(): return jnp.dot(left, right, preferred_element_type=jnp.float32)  41.8 us
    all_to_all x3, waiting for transfers between devices, shards(): lax.all_to_all(packed, 'tok', split_axis=0, concat_axis=0, tiled=True)  29 us
    all_to_all x3, waiting for transfers between devices, shards(): lax.all_to_all(mixed_grad, 'tok', split_axis=0, concat_axis=0, tiled=True)  22.9 us
    all_to_all x3, starting transfers between devices, shards(): lax.all_to_all(packed, 'tok', split_axis=0, concat_axis=0, tiled=True)  21.7 us
    all_to_all x3, waiting for transfers between devices, shards(): lax.all_to_all(packed_grad_win, 'tok', split_axis=0, concat_axis=0, tiled...  20.5 us
    all_to_all x2, waiting for transfers between devices, shards(): lax.all_to_all(mixed_win, 'tok', split_axis=0, concat_axis=0, tiled=True)  19.2 us
  transfers between devices with their start and end apart: 17, of which 13 were waited for; matrix products, arithmetic and copies ran while one was open for 7% of the time, Pallas kernels for 0%

commit v1 on v0

v1 whole, which is shorter than its diff:
```python
import functools
import math

import jax
import jax.numpy as jnp
from jax import lax
from jax.experimental import pallas as pl
from jax.experimental.pallas import tpu as pltpu
from jax.sharding import PartitionSpec as P

H = 8
WIN = 32
GROUP = 8
ROWS = 256
WIDTH = 256
FF = 1024
HEAD = WIDTH // H
EPS = 1e-06
CHUNK = 96
CHUNK_PAD = 104
SEND_ROWS = 40
BF = jnp.bfloat16
F32 = jnp.float32


def nn(a, b):
    return jnp.dot(a, b, preferred_element_type=F32)


def nt(a, b):
    return lax.dot_general(a, b, (((1,), (1,)), ((), ())), preferred_element_type=F32)


def tn(a, b):
    return lax.dot_general(a, b, (((0,), (0,)), ((), ())), preferred_element_type=F32)


def iota(shape, dim):
    return lax.broadcasted_iota(jnp.int32, shape, dim)


def split_two(value):
    high = value.astype(BF)
    low = (value - high.astype(F32)).astype(BF)
    return high, low


def embed_kernel(features_ref, coarse_ref, rim_ref, parent_ref, target_ref, out_ref):
    micro = lax.axis_index("pipe")
    shard = lax.axis_index("tok")
    local = parent_ref[pl.ds(micro, 1), :] - shard * coarse_ref.shape[1]
    own_hot = jnp.where(iota((64, ROWS), 0) == local, 1.0, 0.0).astype(BF)
    rim_hot = jnp.where((iota((16, ROWS), 0) == 0) & (local == -1), 1.0, 0.0).astype(BF)
    rim = jnp.broadcast_to(rim_ref[micro], (16, WIDTH))
    lifted = tn(own_hot, coarse_ref[micro]) + tn(rim_hot, rim)
    embedded = (features_ref[micro].astype(F32) + lifted).astype(BF)
    target = jnp.broadcast_to(target_ref[pl.ds(micro, 1), :], (8, ROWS))
    high = target.astype(BF).astype(F32)
    middle = (target - high).astype(BF).astype(F32)
    low = target - high - middle
    row = iota((8, ROWS), 0)
    extra = jnp.where(row == 0, high, jnp.where(row == 1, middle, jnp.where(row == 2, low, 0.0)))
    extra = extra.astype(BF)
    for part in range(GROUP):
        out_ref[part, 0:WIN, :] = embedded[part * WIN : (part + 1) * WIN]
        out_ref[part, WIN:SEND_ROWS, :] = extra


def group_max(values):
    lane = iota(values.shape, 1)
    for step in (1, 2, 4, 8, 16):
        ahead = pltpu.roll(values, values.shape[1] - step, 1)
        behind = pltpu.roll(values, step, 1)
        values = jnp.maximum(values, jnp.where((lane & step) == 0, ahead, behind))
    return values


def group_sum(values, same_head):
    high, low = split_two(values)
    return nn(high, same_head) + nn(low, same_head)


def step_kernel(
    counts_ref, received_ref, sdf_ref, gains_own_ref, gains_far_ref,
    qkv_own, qkv_far, out_own, out_far, up_own, up_far, down_own, down_far,
    keep_ref, send_ref,
    w_qkv, w_out, w_up, w_down,
    x_buf, inv_one, normed_buf, packed_buf, prob_buf, mixed_buf, after_buf, inv_two,
    normed_two_buf, slope_buf, hidden_buf, out_buf, mask_buf, grads, score_buf, dpacked_buf,
    load_sem, store_sem,
):
    micro = lax.axis_index("pipe")
    shard = lax.axis_index("tok")
    part = lax.rem(shard, GROUP)
    first = shard - part
    loads = []
    for number, (own, far, held) in enumerate(
        ((qkv_own, qkv_far, w_qkv), (out_own, out_far, w_out), (up_own, up_far, w_up), (down_own, down_far, w_down))
    ):
        loads.append(pltpu.make_async_copy(own.at[0], held.at[micro], load_sem.at[2 * number]))
        loads.append(pltpu.make_async_copy(far.at[0], held.at[1 - micro], load_sem.at[2 * number + 1]))
    for load in loads:
        load.start()

    own_is_first = micro == 0

    def gain(section, which):
        own = gains_own_ref[which : which + 1, :]
        far = gains_far_ref[which : which + 1, :]
        mine = own_is_first if section == 0 else jnp.logical_not(own_is_first)
        return jnp.where(mine, own, far)

    row_i = iota((ROWS, WIDTH), 0)
    col_i = iota((ROWS, WIDTH), 1)
    same_head = jnp.where(row_i // WIN == col_i // HEAD, 1.0, 0.0).astype(BF)
    swapped = row_i % WIN // 4 * WIN + row_i // WIN * 4 + row_i % 4
    swap = jnp.where(swapped == col_i, 1.0, 0.0).astype(BF)

    def exchange(value):
        return nn(swap, value).astype(BF)

    lane = iota((1, WIDTH), 1)
    key = lane % WIN
    count_of = [counts_ref[micro, first + s] for s in range(GROUP)]
    lane_count = jnp.zeros((1, WIDTH), jnp.int32)
    for s in range(GROUP):
        lane_count = jnp.where(key // 4 == s, count_of[s], lane_count)
    for w in range(GROUP):
        dilated = part * WIN + w * 4 + key % 4 < lane_count
        plain = part * WIN + key < count_of[w]
        mask_buf[0, w : w + 1, :] = jnp.where(dilated, 1.0, 0.0)
        mask_buf[1, w : w + 1, :] = jnp.where(plain, 1.0, 0.0)

    def expand(value):
        return jnp.concatenate([value] * H, axis=0) * same_head

    def window(value, w):
        return value[w * WIN : (w + 1) * WIN]

    def store_grad(section, block, value):
        for i in range(GROUP):
            slab = block * GROUP + i
            base = slab % 3 * WIN
            grads[section, slab // 3, base : base + WIN, :] = window(value, i).astype(BF)

    def store_wide(section, block, value):
        store_grad(section, block, value[:, :128])
        store_grad(section, block + 1, value[:, 128:])

    def forward(k):
        x = x_buf[k].astype(F32)
        inv = lax.rsqrt(jnp.mean(x * x, axis=-1, keepdims=True) + EPS)
        inv_one[k] = inv
        normed = (x * inv * gain(k, 0)).astype(BF)
        normed_buf[k] = normed
        if k == 0:
            loads[0].wait()
            loads[1].wait()
        for j in range(3):
            packed_buf[k, j] = nn(normed, w_qkv[k, :, j * WIDTH : (j + 1) * WIDTH]).astype(BF)
        for w in range(GROUP):
            rows = slice(w * WIN, (w + 1) * WIN)
            scores = nt(packed_buf[k, 0, rows, :], expand(packed_buf[k, 1, rows, :]))
            score_buf[rows, :] = jnp.where(mask_buf[k, w : w + 1, :] > 0.5, scores * HEAD**-0.5, -1e30)
        scores = score_buf[...]
        weights = jnp.exp(scores - group_max(scores))
        prob = weights / group_sum(weights, same_head)
        prob_buf[k] = prob
        prob_low = prob.astype(BF)
        for w in range(GROUP):
            rows = slice(w * WIN, (w + 1) * WIN)
            mixed_buf[k, rows, :] = nn(window(prob_low, w), expand(packed_buf[k, 2, rows, :])).astype(BF)
        if k == 0:
            loads[2].wait()
            loads[3].wait()
        after = x + nn(mixed_buf[k], w_out[k])
        after_buf[k] = after
        inv = lax.rsqrt(jnp.mean(after * after, axis=-1, keepdims=True) + EPS)
        inv_two[k] = inv
        normed_two = (after * inv * gain(k, 1)).astype(BF)
        normed_two_buf[k] = normed_two
        if k == 0:
            for load in loads[4:]:
                load.wait()
        total = after
        for j in range(4):
            cols = slice(j * WIDTH, (j + 1) * WIDTH)
            up = nn(normed_two, w_up[k, :, cols])
            root = math.sqrt(2.0 / math.pi)
            square = up * up
            bent = jnp.tanh(root * (up + 0.044715 * (square * up)))
            half = 0.5 * (1.0 + bent)
            hidden = (up * half).astype(BF)
            hidden_buf[k, j] = hidden
            slope_buf[k, j] = half + (0.5 * root) * up * (1.0 - bent * bent) * (1.0 + (3 * 0.044715) * square)
            total = total + nn(hidden, w_down[k, cols, :])
        return total.astype(BF)

    def norm_back(grad, value, inv, gain_row):
        gain_grad = jnp.sum(grad * value * inv, axis=0, keepdims=True)
        scaled = grad * gain_row
        inner = jnp.mean(scaled * value, axis=-1, keepdims=True)
        return inv * (scaled - value * (inv * inv * inner)), gain_grad

    def backward(k, out_grad):
        back = None
        for j in range(4):
            cols = slice(j * WIDTH, (j + 1) * WIDTH)
            store_wide(k, 16 + 2 * j, tn(hidden_buf[k, j], out_grad))
            hidden_grad = nt(out_grad, w_down[k, cols, :]).astype(BF)
            up_grad = (slope_buf[k, j] * hidden_grad.astype(F32)).astype(BF)
            store_wide(k, 8 + 2 * j, tn(normed_two_buf[k], up_grad))
            term = nt(up_grad, w_up[k, :, cols])
            back = term if back is None else back + term
        normed_two_grad = back.astype(BF).astype(F32)
        res_grad, gain_two_grad = norm_back(normed_two_grad, after_buf[k], inv_two[k], gain(k, 1))
        after_grad = out_grad.astype(F32) + res_grad
        after_low = after_grad.astype(BF)
        store_wide(k, 6, tn(mixed_buf[k], after_low))
        mixed_grad = nt(after_low, w_out[k]).astype(BF)
        for w in range(GROUP):
            rows = slice(w * WIN, (w + 1) * WIN)
            score_buf[rows, :] = nt(window(mixed_grad, w), expand(packed_buf[k, 2, rows, :]))
        prob = prob_buf[k]
        prob_low = prob.astype(BF)
        prob_grad = score_buf[...].astype(BF).astype(F32)
        flow = prob * prob_grad
        score_grad = ((flow - prob * group_sum(flow, same_head)) * HEAD**-0.5).astype(BF)

        def fold(value):
            total = None
            for h in range(H):
                piece = jnp.where(col_i[:WIN] // HEAD == h, window(value, h), 0.0)
                total = piece if total is None else total + piece
            return total

        for w in range(GROUP):
            rows = slice(w * WIN, (w + 1) * WIN)
            grad_w = window(score_grad, w)
            dpacked_buf[0, rows, :] = nn(grad_w, expand(packed_buf[k, 1, rows, :])).astype(BF)
            dpacked_buf[1, rows, :] = fold(tn(grad_w, packed_buf[k, 0, rows, :])).astype(BF)
            dpacked_buf[2, rows, :] = fold(tn(window(prob_low, w), window(mixed_grad, w))).astype(BF)
        back = None
        for j in range(3):
            piece = dpacked_buf[j]
            store_wide(k, 2 * j, tn(normed_buf[k], piece))
            term = nt(piece, w_qkv[k, :, j * WIDTH : (j + 1) * WIDTH])
            back = term if back is None else back + term
        normed_grad = back.astype(BF).astype(F32)
        in_res, gain_one_grad = norm_back(normed_grad, x_buf[k].astype(F32), inv_one[k], gain(k, 0))
        return (after_grad + in_res).astype(BF), gain_one_grad, gain_two_grad

    received = received_ref[:, 0:WIN, :].reshape(ROWS, WIDTH)
    x_buf[0] = exchange(received)
    x_buf[1] = exchange(forward(0))
    section_one = forward(1).astype(F32)

    pieces = []
    lane_w = iota((WIN, WIDTH), 1)
    row_w = iota((WIN, WIDTH), 0)
    valid_pieces = []
    for s in range(GROUP):
        parts = received_ref[s, WIN : WIN + 8, :].astype(F32)
        line = parts[0:1] + parts[1:2] + parts[2:3]
        chosen = jnp.where(lane_w == part * WIN + row_w, line, 0.0)
        pieces.append(jnp.sum(chosen, axis=-1, keepdims=True))
        valid_pieces.append(part * WIN + iota((WIN, 1), 0) < count_of[s])
    target = jnp.concatenate(pieces, axis=0)
    valid = jnp.concatenate([jnp.where(v, 1.0, 0.0) for v in valid_pieces], axis=0)
    sdf = sdf_ref[...]
    predicted = jnp.sum(section_one * sdf, axis=-1, keepdims=True)
    residue = jnp.where(valid > 0.5, predicted - target, 0.0)
    slope = 2.0 * residue / math.sqrt(3 * ROWS * 64 // 4)
    loss = jnp.sum(residue * residue, axis=0, keepdims=True)
    sdf_grad = jnp.sum(slope * section_one, axis=0, keepdims=True)
    head_grad = (slope * sdf).astype(BF)
    middle_grad, one_one, one_two = backward(1, head_grad)
    unused, zero_one, zero_two = backward(0, exchange(middle_grad))
    del unused
    loss_row = jnp.broadcast_to(loss, (1, 128))
    stat_row = iota((8, 128), 0)
    for k, (gain_one, gain_two) in enumerate(((zero_one, zero_two), (one_one, one_two))):
        lines = []
        for line in (gain_one, gain_two, sdf_grad):
            lines += [line[:, :128], line[:, 128:]]
        lines.append(loss_row)
        grads[k, :, CHUNK:CHUNK_PAD, :] = jnp.zeros((64, CHUNK_PAD - CHUNK, 128), BF)
        for c, line in enumerate(lines):
            high, low = split_two(line)
            both = jnp.where(stat_row == 0, high.astype(F32), jnp.where(stat_row == 1, low.astype(F32), 0.0))
            grads[k, c, CHUNK:CHUNK_PAD, :] = both.astype(BF)
    stores = [
        pltpu.make_async_copy(grads.at[micro], keep_ref, store_sem.at[0]),
        pltpu.make_async_copy(grads.at[1 - micro], send_ref, store_sem.at[1]),
    ]
    for store in stores:
        store.start()
    for store in stores:
        store.wait()


def add_kernel(keep_ref, far_ref, out_ref):
    for c in range(0, 64, 8):
        total = keep_ref[c : c + 8].astype(F32) + far_ref[c : c + 8].astype(F32)
        out_ref[c : c + 8, 0:CHUNK, :] = total[:, :CHUNK].astype(BF)
        stat = total[:, CHUNK : CHUNK + 1] + total[:, CHUNK + 1 : CHUNK + 2]
        out_ref[c : c + 8, CHUNK:CHUNK_PAD, :] = stat_rows(stat, (8, 8, 128), 1)


def stat_rows(stat, shape, dim):
    high, low = split_two(stat)
    row = iota(shape, dim)
    both = jnp.where(row == 0, high.astype(F32), jnp.where(row == 1, low.astype(F32), 0.0))
    return both.astype(BF)


def sum_kernel(in_ref, out_ref):
    total = in_ref[0].astype(F32)
    for c in range(1, 64):
        total = total + in_ref[c].astype(F32)
    stat = total[CHUNK : CHUNK + 1] + total[CHUNK + 1 : CHUNK + 2]
    main = total[:CHUNK].astype(BF)
    tail = stat_rows(stat, (8, 128), 0)
    for c in range(64):
        out_ref[c, 0:CHUNK, :] = main
        out_ref[c, CHUNK:CHUNK_PAD, :] = tail


def unpack_kernel(in_ref, loss_ref, sdf_ref, gain_one_ref, qkv_ref, out_ref, gain_two_ref, up_ref, down_ref):
    for block in range(24):
        for i in range(GROUP):
            slab = block * GROUP + i
            base = slab % 3 * WIN
            piece = in_ref[slab // 3, base : base + WIN, :].astype(F32)
            rows = slice(i * WIN, (i + 1) * WIN)
            if block < 6:
                qkv_ref[0, rows, block * 128 : (block + 1) * 128] = piece
            elif block < 8:
                out_ref[0, rows, (block - 6) * 128 : (block - 5) * 128] = piece
            elif block < 16:
                up_ref[0, rows, (block - 8) * 128 : (block - 7) * 128] = piece
            else:
                j, side = divmod(block - 16, 2)
                down_ref[0, j * 256 + i * WIN : j * 256 + (i + 1) * WIN, side * 128 : (side + 1) * 128] = piece
    lines = []
    for c in range(7):
        pair = in_ref[c, CHUNK:CHUNK_PAD, :].astype(F32)
        lines.append(pair[0:1] + pair[1:2])
    for ref, c in ((gain_one_ref, 0), (gain_two_ref, 2), (sdf_ref, 4)):
        ref[0:1, 0:128] = lines[c]
        ref[0:1, 128:256] = lines[c + 1]
    loss_ref[0:1, :] = lines[6] / (2 * 12288)


def swap_pipe(value):
    return lax.ppermute(value, "pipe", [(0, 1), (1, 0)])


VMEM = pl.BlockSpec(memory_space=pltpu.VMEM)
SMEM = pl.BlockSpec(memory_space=pltpu.SMEM)
ANY = pl.BlockSpec(memory_space=pl.ANY)


def shards(
    features, coarse, parent, counts, target, gain_attn, w_qkv, w_out, gain_mlp, w_up, w_down, w_sdf
):
    rank_count = lax.axis_size("tok")
    rim = lax.ppermute(coarse[:, -1:, :], "tok", [(i, i + 1) for i in range(rank_count - 1)])
    gains = jnp.concatenate([gain_attn, gain_mlp], axis=0)
    gains_far = swap_pipe(gains)
    qkv_far, out_far, up_far, down_far = (swap_pipe(w) for w in (w_qkv, w_out, w_up, w_down))
    outgoing = pl.pallas_call(
        embed_kernel,
        out_shape=jax.ShapeDtypeStruct((GROUP, SEND_ROWS, WIDTH), BF),
        in_specs=[VMEM] * 5,
        out_specs=VMEM,
        name="embed",
    )(features, coarse, rim, parent, target)
    groups = [[b * GROUP + i for i in range(GROUP)] for b in range(rank_count // GROUP)]
    received = lax.all_to_all(outgoing, "tok", 0, 0, axis_index_groups=groups, tiled=True)
    packet = jax.ShapeDtypeStruct((64, CHUNK_PAD, 128), BF)
    keep, send = pl.pallas_call(
        step_kernel,
        out_shape=(packet, packet),
        in_specs=[SMEM] + [VMEM] * 4 + [ANY] * 8,
        out_specs=(ANY, ANY),
        scratch_shapes=[
            pltpu.VMEM((2, WIDTH, 3 * WIDTH), BF),
            pltpu.VMEM((2, WIDTH, WIDTH), BF),
            pltpu.VMEM((2, WIDTH, FF), BF),
            pltpu.VMEM((2, FF, WIDTH), BF),
            pltpu.VMEM((2, ROWS, WIDTH), BF),
            pltpu.VMEM((2, ROWS, 1), F32),
            pltpu.VMEM((2, ROWS, WIDTH), BF),
            pltpu.VMEM((2, 3, ROWS, WIDTH), BF),
            pltpu.VMEM((2, ROWS, WIDTH), F32),
            pltpu.VMEM((2, ROWS, WIDTH), BF),
            pltpu.VMEM((2, ROWS, WIDTH), F32),
            pltpu.VMEM((2, ROWS, 1), F32),
            pltpu.VMEM((2, ROWS, WIDTH), BF),
            pltpu.VMEM((2, 4, ROWS, WIDTH), F32),
            pltpu.VMEM((2, 4, ROWS, WIDTH), BF),
            pltpu.VMEM((ROWS, WIDTH), BF),
            pltpu.VMEM((2, GROUP, WIDTH), F32),
            pltpu.VMEM((2, 64, CHUNK_PAD, 128), BF),
            pltpu.VMEM((ROWS, WIDTH), F32),
            pltpu.VMEM((3, ROWS, WIDTH), BF),
            pltpu.SemaphoreType.DMA((8,)),
            pltpu.SemaphoreType.DMA((2,)),
        ],
        name="step",
    )(counts, received, w_sdf[None], gains, gains_far, w_qkv, qkv_far, w_out, out_far, w_up, up_far, w_down, down_far)
    far = swap_pipe(send)
    total = pl.pallas_call(
        add_kernel, out_shape=packet, in_specs=[VMEM] * 2, out_specs=VMEM, name="add"
    )(keep, far)
    shares = lax.all_to_all(total, "tok", 0, 0, tiled=True)
    summed = pl.pallas_call(
        sum_kernel, out_shape=packet, in_specs=[VMEM], out_specs=VMEM, name="sum"
    )(shares)
    gathered = lax.all_to_all(summed, "tok", 0, 0, tiled=True)
    loss, sdf, gain_one, qkv, out, gain_two, up, down = pl.pallas_call(
        unpack_kernel,
        out_shape=(
            jax.ShapeDtypeStruct((1, 128), F32),
            jax.ShapeDtypeStruct((1, WIDTH), F32),
            jax.ShapeDtypeStruct((1, WIDTH), F32),
            jax.ShapeDtypeStruct((1, WIDTH, 3 * WIDTH), F32),
            jax.ShapeDtypeStruct((1, WIDTH, WIDTH), F32),
            jax.ShapeDtypeStruct((1, WIDTH), F32),
            jax.ShapeDtypeStruct((1, WIDTH, FF), F32),
            jax.ShapeDtypeStruct((1, FF, WIDTH), F32),
        ),
        in_specs=[VMEM],
        out_specs=(VMEM,) * 8,
        name="unpack",
    )(gathered)
    return loss[0, 0], sdf[0], gain_one, qkv, out, gain_two, up, down


def solution(mesh):
    return jax.shard_map(
        shards,
        mesh=mesh,
        in_specs=(
            P(None, "tok", None),
            P(None, "tok", None),
            P(None, "tok"),
            P(),
            P(None, "tok"),
            P("pipe", None),
            P("pipe", None, None),
            P("pipe", None, None),
            P("pipe", None),
            P("pipe", None, None),
            P("pipe", None, None),
            P(),
        ),
        out_specs=(
            P(),
            P(),
            P("pipe", None),
            P("pipe", None, None),
            P("pipe", None, None),
            P("pipe", None),
            P("pipe", None, None),
            P("pipe", None, None),
        ),
        check_vma=False,
    )
```

time: 595 us -> 121 us (0.20); the launches traced: 585 us -> 121 us
  blocking collectives: 252 us -> 66.1 us
  waiting for transfers between devices: 93.3 us -> 10.6 us
  local copies, waits for them, and re-layouts: 66.5 us -> 3.58 us
  matrix products: 62.2 us -> 0 us
  starting transfers between devices: 69.7 us -> 11.5 us
  Pallas kernels: 0 us -> 27.6 us
  other arithmetic: 21.1 us -> 0.71 us
  between operations: 19.9 us -> 0.74 us
    psum x2 -> x0, blocking collectives: 238 us -> none  [the longest x1 174 us: shards(): grad_totals = lax.psum(grad_totals, 'tok')]
    all_to_all x11 -> x1, waiting for transfers between devices: 91.5 us -> 4.64 us  [shards(): lax.all_to_all(outgoing, 'tok', 0, 0, axis_index_groups=groups, tiled=True)]
    dot_general x51 -> x0, matrix products: 54.6 us -> none  [the longest x36 41.8 us: matmul(): return jnp.dot(left, right, preferred_element_type=jnp.float32)]
    all_to_all x11 -> x1, starting transfers between devices: 60.9 us -> 6.44 us  [shards(): lax.all_to_all(outgoing, 'tok', 0, 0, axis_index_groups=groups, tiled=True)]
    all_to_all x1 -> x2, blocking collectives: 14.5 us -> 66.1 us  [the longest x1 35.8 us: shards(): shares = lax.all_to_all(total, 'tok', 0, 0, tiled=True)]
    pallas_call x0 -> x5, Pallas kernels: none -> 27.6 us  [the longest x1 15.8 us: shards(): pl.pallas_call(step_kernel, out_shape=(packet, packet), in_specs=[SMEM] +...]
    all_to_all x26 -> x0, local copies, waits for them, and re-layouts: 14.3 us -> none  [the longest x5 6.58 us: shards(): lax.all_to_all(packed_grad_win, 'tok', split_axis=0, concat_axis=0, tiled...]
    unnamed x219 -> x18, local copies, waits for them, and re-layouts: 16.6 us -> 2.86 us
  transfers between devices with their start and end apart: 17 -> 8, of which waited for: 13 -> 4; matrix products, arithmetic and copies ran while one was open for 7% -> 1% of each run, Pallas kernels for 0% -> 2%
where the time goes in v1:
time: 121 us
  blocking collectives  66.1 us (55%)
  Pallas kernels  27.6 us (23%)
  starting transfers between devices  11.5 us (10%)
  waiting for transfers between devices  10.6 us (9%)
  local copies, waits for them, and re-layouts  3.58 us (3%)
    all_to_all x1, blocking collectives, shards(): shares = lax.all_to_all(total, 'tok', 0, 0, tiled=True)  35.8 us
    all_to_all x1, blocking collectives, shards(): gathered = lax.all_to_all(summed, 'tok', 0, 0, tiled=True)  30.3 us
    pallas_call x1, Pallas kernels, shards(): pl.pallas_call(step_kernel, out_shape=(packet, packet), in_specs=[SMEM] +...  15.8 us
    all_to_all x1, starting transfers between devices, shards(): lax.all_to_all(outgoing, 'tok', 0, 0, axis_index_groups=groups, tiled=True)  6.44 us
    all_to_all x1, waiting for transfers between devices, shards(): lax.all_to_all(outgoing, 'tok', 0, 0, axis_index_groups=groups, tiled=True)  4.64 us
    ppermute x6, waiting for transfers between devices, swap_pipe(): return lax.ppermute(value, 'pipe', [(0, 1), (1, 0)])  4.63 us
    pallas_call x1, Pallas kernels, shards(): pl.pallas_call(add_kernel, out_shape=packet, in_specs=[VMEM] * 2, out_spe...  3.64 us
    ppermute x1, starting transfers between devices, shards(): lax.ppermute(coarse[:, -1:, :], 'tok', [(i, i + 1) for i in range(rank_co...  3.49 us
  transfers between devices with their start and end apart: 8, of which 4 were waited for; matrix products, arithmetic and copies ran while one was open for 1% of the time, Pallas kernels for 2%

profile of v1, /device:TPU:0, one launch (start us, length us, event | category | flops | bytes accessed | tf_op | source)
XLA Modules:
  0.0 120.7 jit_solution(15233409301848160185)
XLA Ops:
  0.7 0.5 collective-permute-start.5
  1.3 0.7 slice.6
  2.0 3.5 %collective-permute-start = (bf16[2,1,256]{2,1,0:T(2,128)(2,1)S(1)}, bf16[2,1,256]{2,1,0:T(2,128)(2,1)S(1)}, u32[]{:S(2)}, u32[]{:S(2)}) collective-permute-start(bf16[2,1,256]{2,1,0:T(2,128)(2,1)S(1)} %slice.6), channel_id=1, source_target_pairs={{0,1},{1,2},{2,3},{3,4},{4,5},{5,6},{6,7},{7,8},{8,9},{9,10},{10,1... | collective-permute-start | bytes 3080 | tf_op jit(solution)/shard_map/ppermute | solution.py:368
  5.5 1.3 %collective-permute-done.rim_ref = bf16[2,1,256]{2,1,0:T(2,128)(2,1)S(1)} collective-permute-done((bf16[2,1,256]{2,1,0:T(2,128)(2,1)S(1)}, bf16[2,1,256]{2,1,0:T(2,128)(2,1)S(1)}, u32[]{:S(2)}, u32[]{:S(2)}) %collective-permute-start) | collective-permute-done | bytes 1056 | tf_op jit(solution)/shard_map/ppermute | solution.py:368
  6.8 0.6 copy-done.7
  7.4 1.9 %embed.1 = bf16[8,40,256]{2,1,0:T(8,128)(2,1)} custom-call(bf16[2,256,256]{2,1,0:T(8,128)(2,1)} %features_ref.1, bf16[2,64,256]{2,1,0:T(8,128)(2,1)} %coarse_ref.1, bf16[2,1,256]{2,1,0:T(2,128)(2,1)} %copy-done.7, s32[2,256]{1,0:T(2,128)} %parent_ref.1, f32[2,256]{1,0:T(2,128)} %target_ref.1), custom_call_target="tpu_custom_call" | custom-call | tf_op jit(solution)/shard_map/embed/pallas_call | solution.py:372
  9.4 6.4 %all-to-all-start = ((bf16[8,40,256]{2,1,0:T(8,128)(2,1)}), bf16[8,40,256]{2,1,0:T(8,128)(2,1)S(1)}, u32[]{:S(2)}, u32[]{:S(2)}) async-start(bf16[8,40,256]{2,1,0:T(8,128)(2,1)} %embed.1), calls=%async_computation | async-start | bytes 327680 | tf_op jit(solution)/shard_map/all_to_all | solution.py:380
  15.8 0.7 pad_maximum_fusion.gains_own_ref
  16.5 0.6 collective-permute-start.1
  17.1 0.8 collective-permute-done.1.gains_far_ref
  17.9 4.6 %all-to-all-done.received_ref = bf16[8,40,256]{2,1,0:T(8,128)(2,1)S(1)} async-done(((bf16[8,40,256]{2,1,0:T(8,128)(2,1)}), bf16[8,40,256]{2,1,0:T(8,128)(2,1)S(1)}, u32[]{:S(2)}, u32[]{:S(2)}) %all-to-all-start) | async-done | bytes 163872 | tf_op jit(solution)/shard_map/all_to_all | solution.py:380
  22.6 0.6 copy-done.1
  23.2 0.1 copy-done.4
  23.4 0.2 copy-done.2
  23.5 0.2 copy-done.3
  23.7 15.8 %step.1 = (bf16[64,104,128]{2,1,0:T(8,128)(2,1)}, bf16[64,104,128]{2,1,0:T(8,128)(2,1)}) custom-call(s32[2,64]{1,0:T(2,128)} %counts_ref.1, bf16[8,40,256]{2,1,0:T(8,128)(2,1)} %copy-done.1, f32[1,256]{1,0:T(1,128)} %bitcast.4, f32[2,256]{1,0:T(2,128)} %copy-done.6, f32[2,256]{1,0:T(2,128)} %copy-done.8, bf16[1,256,768]{2,1,0:T(8,128)(2,1)} %qkv_own.1, ...), custom_call_target="tpu_custom_call" | custom-call | tf_op jit(solution)/shard_map/step/pallas_call | solution.py:382
  39.6 0.3 collective-permute-start.6
  39.8 3.8 %collective-permute-done.6.far_ref = bf16[64,104,128]{2,1,0:T(8,128)(2,1)S(1)} collective-permute-done((bf16[64,104,128]{2,1,0:T(8,128)(2,1)}, bf16[64,104,128]{2,1,0:T(8,128)(2,1)S(1)}, u32[]{:S(2)}, u32[]{:S(2)}) %collective-permute-start.6) | collective-permute-done | bytes 1703968 | tf_op jit(solution)/shard_map/ppermute | solution.py:356
  43.6 1.2 copy-done
  44.8 3.6 %add.1 = bf16[64,104,128]{2,1,0:T(8,128)(2,1)} custom-call(bf16[64,104,128]{2,1,0:T(8,128)(2,1)} %get-tuple-element.18.keep_ref, bf16[64,104,128]{2,1,0:T(8,128)(2,1)} %copy-done), custom_call_target="tpu_custom_call" | custom-call | tf_op jit(solution)/shard_map/add/pallas_call | solution.py:414
  48.5 35.8 %all_to_all.15.in_ref = bf16[64,104,128]{2,1,0:T(8,128)(2,1)} all-to-all(bf16[64,104,128]{2,1,0:T(8,128)(2,1)} %add.1), channel_id=1, replica_groups=mesh['pipe'=2,'tok'=64] {'tok'}, dimensions={0} | all-to-all | bytes 3407872 | tf_op jit(solution)/shard_map/all_to_all | solution.py:417
  84.3 3.0 %sum.1 = bf16[64,104,128]{2,1,0:T(8,128)(2,1)} custom-call(bf16[64,104,128]{2,1,0:T(8,128)(2,1)} %all_to_all.15.in_ref), custom_call_target="tpu_custom_call" | custom-call | tf_op jit(solution)/shard_map/sum/pallas_call | solution.py:418
  87.2 30.3 %all_to_all.16.in_ref = bf16[64,104,128]{2,1,0:T(8,128)(2,1)} all-to-all(bf16[64,104,128]{2,1,0:T(8,128)(2,1)} %sum.1), channel_id=1, replica_groups=mesh['pipe'=2,'tok'=64] {'tok'}, dimensions={0} | all-to-all | bytes 3407872 | tf_op jit(solution)/shard_map/all_to_all | solution.py:421
  117.5 3.2 %unpack.1 = (f32[1,128]{1,0:T(1,128)}, f32[1,256]{1,0:T(1,128)}, f32[1,256]{1,0:T(1,128)}, f32[1,256,768]{2,1,0:T(8,128)}, f32[1,256,256]{2,1,0:T(8,128)}, /*ind...) custom-call(bf16[64,104,128]{2,1,0:T(8,128)(2,1)} %all_to_all.16.in_ref), custom_call_target="tpu_custom_call" | custom-call | tf_op jit(solution)/shard_map/unpack/pallas_call | solution.py:422
  (19 shorter events, 0.2 us)
Async XLA Ops:
  0.6 21.9 %collective-permute-start.4 = (bf16[1,256,1024]{2,1,0:T(8,128)(2,1)}, bf16[1,256,1024]{2,1,0:T(8,128)(2,1)S(1)}, u32[]{:S(2)}, u32[]{:S(2)}) collective-permute-start(bf16[1,256,1024]{2,1,0:T(8,128)(2,1)} %up_own.1), channel_id=1, source_target_pairs={{0,64},{64,0},{1,65},{65,1},{2,66},{66,2},{3,67},{67,3},{4,68},{68... | collective-permute-start | bytes 1572872 | tf_op jit(solution)/shard_map/ppermute | solution.py:356
  0.7 21.9 %collective-permute-start.5 = (bf16[1,1024,256]{2,1,0:T(8,128)(2,1)}, bf16[1,1024,256]{2,1,0:T(8,128)(2,1)S(1)}, u32[]{:S(2)}, u32[]{:S(2)}) collective-permute-start(bf16[1,1024,256]{2,1,0:T(8,128)(2,1)} %down_own.1), channel_id=1, source_target_pairs={{0,64},{64,0},{1,65},{65,1},{2,66},{66,2},{3,67},{67,3},{4,68},{68... | collective-permute-start | bytes 1572872 | tf_op jit(solution)/shard_map/ppermute | solution.py:356
  1.2 21.3 %collective-permute-start.2 = (bf16[1,256,768]{2,1,0:T(8,128)(2,1)}, bf16[1,256,768]{2,1,0:T(8,128)(2,1)S(1)}, u32[]{:S(2)}, u32[]{:S(2)}) collective-permute-start(bf16[1,256,768]{2,1,0:T(8,128)(2,1)} %qkv_own.1), channel_id=1, source_target_pairs={{0,64},{64,0},{1,65},{65,1},{2,66},{66,2},{3,67},{67,3},{4,68},{68... | collective-permute-start | bytes 1179656 | tf_op jit(solution)/shard_map/ppermute | solution.py:356
  2.0 4.8 %collective-permute-start = (bf16[2,1,256]{2,1,0:T(2,128)(2,1)S(1)}, bf16[2,1,256]{2,1,0:T(2,128)(2,1)S(1)}, u32[]{:S(2)}, u32[]{:S(2)}) collective-permute-start(bf16[2,1,256]{2,1,0:T(2,128)(2,1)S(1)} %slice.6), channel_id=1, source_target_pairs={{0,1},{1,2},{2,3},{3,4},{4,5},{5,6},{6,7},{7,8},{8,9},{9,10},{10,1... | collective-permute-start | bytes 3080 | tf_op jit(solution)/shard_map/ppermute | solution.py:368
  6.8 0.6 copy-start.7
  9.4 13.2 %all-to-all-start = ((bf16[8,40,256]{2,1,0:T(8,128)(2,1)}), bf16[8,40,256]{2,1,0:T(8,128)(2,1)S(1)}, u32[]{:S(2)}, u32[]{:S(2)}) async-start(bf16[8,40,256]{2,1,0:T(8,128)(2,1)} %embed.1), calls=%async_computation | async-start | bytes 327680 | tf_op jit(solution)/shard_map/all_to_all | solution.py:380
  15.8 2.1 %collective-permute-start.3 = (bf16[1,256,256]{2,1,0:T(8,128)(2,1)}, bf16[1,256,256]{2,1,0:T(8,128)(2,1)S(1)}, u32[]{:S(2)}, u32[]{:S(2)}) collective-permute-start(bf16[1,256,256]{2,1,0:T(8,128)(2,1)} %out_own.1), channel_id=1, source_target_pairs={{0,64},{64,0},{1,65},{65,1},{2,66},{66,2},{3,67},{67,3},{4,68},{68... | collective-permute-start | bytes 393224 | tf_op jit(solution)/shard_map/ppermute | solution.py:356
  16.5 6.1 %copy-start.6 = (f32[2,256]{1,0:T(2,128)}, f32[2,256]{1,0:T(2,128)S(1)}, u32[]{:S(2)}) copy-start(f32[2,256]{1,0:T(2,128)S(1)} %pad_maximum_fusion.gains_own_ref) | copy-start | bytes 6148
  16.5 1.4 %collective-permute-start.1 = (f32[2,256]{1,0:T(2,128)S(1)}, f32[2,256]{1,0:T(2,128)S(1)}, u32[]{:S(2)}, u32[]{:S(2)}) collective-permute-start(f32[2,256]{1,0:T(2,128)S(1)} %pad_maximum_fusion.gains_own_ref), channel_id=1, source_target_pairs={{0,64},{64,0},{1,65},{65,1},{2,66},{66,2},{3,67},{67,3},{4,68},{68... | collective-permute-start | bytes 6152 | tf_op jit(solution)/shard_map/ppermute | solution.py:356
  17.9 4.7 %copy-start.8 = (f32[2,256]{1,0:T(2,128)}, f32[2,256]{1,0:T(2,128)S(1)}, u32[]{:S(2)}) copy-start(f32[2,256]{1,0:T(2,128)S(1)} %collective-permute-done.1.gains_far_ref) | copy-start | bytes 6148
  17.9 4.7 %copy-start.5 = (bf16[1,256,256]{2,1,0:T(8,128)(2,1)}, bf16[1,256,256]{2,1,0:T(8,128)(2,1)S(1)}, u32[]{:S(2)}) copy-start(bf16[1,256,256]{2,1,0:T(8,128)(2,1)S(1)} %collective-permute-done.3.out_far) | copy-start | bytes 393220
  22.6 0.7 copy-start.1
  22.6 0.8 copy-start.4
  22.6 1.0 copy-start.2
  22.6 1.1 copy-start.3
  39.6 4.1 %collective-permute-start.6 = (bf16[64,104,128]{2,1,0:T(8,128)(2,1)}, bf16[64,104,128]{2,1,0:T(8,128)(2,1)S(1)}, u32[]{:S(2)}, u32[]{:S(2)}) collective-permute-start(bf16[64,104,128]{2,1,0:T(8,128)(2,1)} %get-tuple-element.19), channel_id=1, source_target_pairs={{0,64},{64,0},{1,65},{65,1},{2,66},{66,2},{3,67},{67,3},{4,68},{68... | collective-permute-start | bytes 5111816 | tf_op jit(solution)/shard_map/ppermute | solution.py:356
  43.6 1.2 copy-start

commit v2 on v1

--- a/solution.py
+++ b/solution.py
@@ -45,15 +45,33 @@
     return high, low
 
 
-def embed_kernel(features_ref, coarse_ref, rim_ref, parent_ref, target_ref, out_ref):
+def embed_kernel(
+    features_hbm, coarse_hbm, rim_ref, parent_hbm, target_hbm, out_ref,
+    features_ref, coarse_ref, parent_ref, target_ref, load_sem,
+):
     micro = lax.axis_index("pipe")
     shard = lax.axis_index("tok")
-    local = parent_ref[pl.ds(micro, 1), :] - shard * coarse_ref.shape[1]
+    loads = [
+        pltpu.make_async_copy(source, held, load_sem.at[number])
+        for number, (source, held) in enumerate(
+            (
+                (features_hbm.at[micro], features_ref),
+                (coarse_hbm.at[micro], coarse_ref),
+                (parent_hbm, parent_ref),
+                (target_hbm, target_ref),
+            )
+        )
+    ]
+    for load in loads:
+        load.start()
+    for load in loads:
+        load.wait()
+    local = parent_ref[pl.ds(micro, 1), :] - shard * 64
     own_hot = jnp.where(iota((64, ROWS), 0) == local, 1.0, 0.0).astype(BF)
     rim_hot = jnp.where((iota((16, ROWS), 0) == 0) & (local == -1), 1.0, 0.0).astype(BF)
     rim = jnp.broadcast_to(rim_ref[micro], (16, WIDTH))
-    lifted = tn(own_hot, coarse_ref[micro]) + tn(rim_hot, rim)
-    embedded = (features_ref[micro].astype(F32) + lifted).astype(BF)
+    lifted = tn(own_hot, coarse_ref[...]) + tn(rim_hot, rim)
+    embedded = (features_ref[...].astype(F32) + lifted).astype(BF)
     target = jnp.broadcast_to(target_ref[pl.ds(micro, 1), :], (8, ROWS))
     high = target.astype(BF).astype(F32)
     middle = (target - high).astype(BF).astype(F32)
@@ -81,13 +99,13 @@
 
 
 def step_kernel(
-    counts_ref, received_ref, sdf_ref, gains_own_ref, gains_far_ref,
+    counts_hbm, received_ref, gain_far_one, gain_far_two, sdf_hbm, gain_own_one_hbm, gain_own_two_hbm,
     qkv_own, qkv_far, out_own, out_far, up_own, up_far, down_own, down_far,
     keep_ref, send_ref,
     w_qkv, w_out, w_up, w_down,
     x_buf, inv_one, normed_buf, packed_buf, prob_buf, mixed_buf, after_buf, inv_two,
-    normed_two_buf, slope_buf, hidden_buf, out_buf, mask_buf, grads, score_buf, dpacked_buf,
-    load_sem, store_sem,
+    normed_two_buf, slope_buf, hidden_buf, mask_buf, grads, score_buf, dpacked_buf,
+    sdf_ref, gain_own_one, gain_own_two, counts_ref, load_sem, store_sem,
 ):
     micro = lax.axis_index("pipe")
     shard = lax.axis_index("tok")
@@ -99,14 +117,27 @@
     ):
         loads.append(pltpu.make_async_copy(own.at[0], held.at[micro], load_sem.at[2 * number]))
         loads.append(pltpu.make_async_copy(far.at[0], held.at[1 - micro], load_sem.at[2 * number + 1]))
-    for load in loads:
+    small = [
+        pltpu.make_async_copy(source, held, load_sem.at[8 + number])
+        for number, (source, held) in enumerate(
+            (
+                (sdf_hbm, sdf_ref),
+                (gain_own_one_hbm, gain_own_one),
+                (gain_own_two_hbm, gain_own_two),
+                (counts_hbm, counts_ref),
+            )
+        )
+    ]
+    for load in small + loads:
         load.start()
+    for load in small:
+        load.wait()
 
     own_is_first = micro == 0
 
     def gain(section, which):
-        own = gains_own_ref[which : which + 1, :]
-        far = gains_far_ref[which : which + 1, :]
+        own = (gain_own_one, gain_own_two)[which][...]
+        far = (gain_far_one, gain_far_two)[which][...]
         mine = own_is_first if section == 0 else jnp.logical_not(own_is_first)
         return jnp.where(mine, own, far)
 
@@ -287,7 +318,9 @@
         grads[k, :, CHUNK:CHUNK_PAD, :] = jnp.zeros((64, CHUNK_PAD - CHUNK, 128), BF)
         for c, line in enumerate(lines):
             high, low = split_two(line)
-            both = jnp.where(stat_row == 0, high.astype(F32), jnp.where(stat_row == 1, low.astype(F32), 0.0))
+            both = jnp.where(
+                stat_row == 2 * micro, high.astype(F32), jnp.where(stat_row == 2 * micro + 1, low.astype(F32), 0.0)
+            )
             grads[k, c, CHUNK:CHUNK_PAD, :] = both.astype(BF)
     stores = [
         pltpu.make_async_copy(grads.at[micro], keep_ref, store_sem.at[0]),
@@ -299,34 +332,17 @@
         store.wait()
 
 
-def add_kernel(keep_ref, far_ref, out_ref):
-    for c in range(0, 64, 8):
-        total = keep_ref[c : c + 8].astype(F32) + far_ref[c : c + 8].astype(F32)
-        out_ref[c : c + 8, 0:CHUNK, :] = total[:, :CHUNK].astype(BF)
-        stat = total[:, CHUNK : CHUNK + 1] + total[:, CHUNK + 1 : CHUNK + 2]
-        out_ref[c : c + 8, CHUNK:CHUNK_PAD, :] = stat_rows(stat, (8, 8, 128), 1)
-
-
-def stat_rows(stat, shape, dim):
-    high, low = split_two(stat)
-    row = iota(shape, dim)
-    both = jnp.where(row == 0, high.astype(F32), jnp.where(row == 1, low.astype(F32), 0.0))
-    return both.astype(BF)
-
-
-def sum_kernel(in_ref, out_ref):
-    total = in_ref[0].astype(F32)
-    for c in range(1, 64):
-        total = total + in_ref[c].astype(F32)
-    stat = total[CHUNK : CHUNK + 1] + total[CHUNK + 1 : CHUNK + 2]
-    main = total[:CHUNK].astype(BF)
-    tail = stat_rows(stat, (8, 128), 0)
-    for c in range(64):
-        out_ref[c, 0:CHUNK, :] = main
-        out_ref[c, CHUNK:CHUNK_PAD, :] = tail
-
-
-def unpack_kernel(in_ref, loss_ref, sdf_ref, gain_one_ref, qkv_ref, out_ref, gain_two_ref, up_ref, down_ref):
+def unpack_kernel(
+    in_ref, loss_ref, sdf_ref, gain_one_ref, qkv_hbm, out_hbm, gain_two_ref, up_hbm, down_hbm,
+    qkv_ref, out_ref, up_ref, down_ref, store_sem,
+):
+    stores = []
+
+    def store(source, target):
+        copy = pltpu.make_async_copy(source, target, store_sem.at[len(stores)])
+        copy.start()
+        stores.append(copy)
+
     for block in range(24):
         for i in range(GROUP):
             slab = block * GROUP + i
@@ -334,14 +350,23 @@
             piece = in_ref[slab // 3, base : base + WIN, :].astype(F32)
             rows = slice(i * WIN, (i + 1) * WIN)
             if block < 6:
-                qkv_ref[0, rows, block * 128 : (block + 1) * 128] = piece
+                qkv_ref[rows, block * 128 : (block + 1) * 128] = piece
             elif block < 8:
-                out_ref[0, rows, (block - 6) * 128 : (block - 5) * 128] = piece
+                out_ref[rows, (block - 6) * 128 : (block - 5) * 128] = piece
             elif block < 16:
-                up_ref[0, rows, (block - 8) * 128 : (block - 7) * 128] = piece
+                up_ref[rows, (block - 8) * 128 : (block - 7) * 128] = piece
             else:
                 j, side = divmod(block - 16, 2)
-                down_ref[0, j * 256 + i * WIN : j * 256 + (i + 1) * WIN, side * 128 : (side + 1) * 128] = piece
+                down_ref[j * 256 + i * WIN : j * 256 + (i + 1) * WIN, side * 128 : (side + 1) * 128] = piece
+        if block == 5:
+            store(qkv_ref, qkv_hbm.at[0])
+        elif block == 7:
+            store(out_ref, out_hbm.at[0])
+        elif block == 15:
+            store(up_ref, up_hbm.at[0])
+        elif block > 15 and block % 2 == 1:
+            rows = slice((block - 17) // 2 * 256, (block - 15) // 2 * 256)
+            store(down_ref.at[rows], down_hbm.at[0, rows])
     lines = []
     for c in range(7):
         pair = in_ref[c, CHUNK:CHUNK_PAD, :].astype(F32)
@@ -350,6 +375,12 @@
         ref[0:1, 0:128] = lines[c]
         ref[0:1, 128:256] = lines[c + 1]
     loss_ref[0:1, :] = lines[6] / (2 * 12288)
+    for copy in stores:
+        copy.wait()
+
+
+def fix(value):
+    return pltpu.with_memory_space_constraint(value, pltpu.HBM)
 
 
 def swap_pipe(value):
@@ -357,8 +388,8 @@
 
 
 VMEM = pl.BlockSpec(memory_space=pltpu.VMEM)
-SMEM = pl.BlockSpec(memory_space=pltpu.SMEM)
 ANY = pl.BlockSpec(memory_space=pl.ANY)
+HBM = pl.BlockSpec(memory_space=pltpu.HBM)
 
 
 def shards(
@@ -366,23 +397,30 @@
 ):
     rank_count = lax.axis_size("tok")
     rim = lax.ppermute(coarse[:, -1:, :], "tok", [(i, i + 1) for i in range(rank_count - 1)])
-    gains = jnp.concatenate([gain_attn, gain_mlp], axis=0)
-    gains_far = swap_pipe(gains)
+    gains_far = [swap_pipe(g) for g in (gain_attn, gain_mlp)]
     qkv_far, out_far, up_far, down_far = (swap_pipe(w) for w in (w_qkv, w_out, w_up, w_down))
     outgoing = pl.pallas_call(
         embed_kernel,
         out_shape=jax.ShapeDtypeStruct((GROUP, SEND_ROWS, WIDTH), BF),
-        in_specs=[VMEM] * 5,
+        in_specs=[HBM, HBM, VMEM, HBM, HBM],
         out_specs=VMEM,
+        scratch_shapes=[
+            pltpu.VMEM((ROWS, WIDTH), BF),
+            pltpu.VMEM((64, WIDTH), BF),
+            pltpu.VMEM((2, ROWS), jnp.int32),
+            pltpu.VMEM((2, ROWS), F32),
+            pltpu.SemaphoreType.DMA((4,)),
+        ],
         name="embed",
-    )(features, coarse, rim, parent, target)
+        compiler_params=pltpu.CompilerParams(vmem_limit_bytes=4 * 2**20),
+    )(fix(features), fix(coarse), rim, fix(parent), fix(target))
     groups = [[b * GROUP + i for i in range(GROUP)] for b in range(rank_count // GROUP)]
     received = lax.all_to_all(outgoing, "tok", 0, 0, axis_index_groups=groups, tiled=True)
     packet = jax.ShapeDtypeStruct((64, CHUNK_PAD, 128), BF)
     keep, send = pl.pallas_call(
         step_kernel,
         out_shape=(packet, packet),
-        in_specs=[SMEM] + [VMEM] * 4 + [ANY] * 8,
+        in_specs=[HBM] + [VMEM] * 3 + [HBM] * 3 + [HBM, ANY] * 4,
         out_specs=(ANY, ANY),
         scratch_shapes=[
             pltpu.VMEM((2, WIDTH, 3 * WIDTH), BF),
@@ -400,25 +438,32 @@
             pltpu.VMEM((2, ROWS, WIDTH), BF),
             pltpu.VMEM((2, 4, ROWS, WIDTH), F32),
             pltpu.VMEM((2, 4, ROWS, WIDTH), BF),
-            pltpu.VMEM((ROWS, WIDTH), BF),
             pltpu.VMEM((2, GROUP, WIDTH), F32),
             pltpu.VMEM((2, 64, CHUNK_PAD, 128), BF),
             pltpu.VMEM((ROWS, WIDTH), F32),
             pltpu.VMEM((3, ROWS, WIDTH), BF),
-            pltpu.SemaphoreType.DMA((8,)),
+            pltpu.VMEM((1, WIDTH), F32),
+            pltpu.VMEM((1, WIDTH), F32),
+            pltpu.VMEM((1, WIDTH), F32),
+            pltpu.SMEM((2, 64), jnp.int32),
+            pltpu.SemaphoreType.DMA((12,)),
             pltpu.SemaphoreType.DMA((2,)),
         ],
         name="step",
-    )(counts, received, w_sdf[None], gains, gains_far, w_qkv, qkv_far, w_out, out_far, w_up, up_far, w_down, down_far)
+        compiler_params=pltpu.CompilerParams(vmem_limit_bytes=32 * 2**20),
+    )(fix(counts), received, *gains_far, fix(w_sdf[None]), fix(gain_attn), fix(gain_mlp), fix(w_qkv), qkv_far, fix(w_out), out_far, fix(w_up), up_far, fix(w_down), down_far)
     far = swap_pipe(send)
-    total = pl.pallas_call(
-        add_kernel, out_shape=packet, in_specs=[VMEM] * 2, out_specs=VMEM, name="add"
-    )(keep, far)
+    total = (keep.astype(F32) + far.astype(F32)).astype(BF)
     shares = lax.all_to_all(total, "tok", 0, 0, tiled=True)
-    summed = pl.pallas_call(
-        sum_kernel, out_shape=packet, in_specs=[VMEM], out_specs=VMEM, name="sum"
-    )(shares)
-    gathered = lax.all_to_all(summed, "tok", 0, 0, tiled=True)
+    summed = jnp.sum(shares.astype(F32), axis=0)
+    stat = jnp.sum(summed[CHUNK : CHUNK + 4], axis=0, keepdims=True)
+    high = lax.reduce_precision(stat, 8, 7)
+    row = iota((CHUNK_PAD, 128), 0)
+    tail = jnp.where(row == CHUNK, high, jnp.where(row == CHUNK + 1, stat - high, 0.0))
+    summed = jnp.where(row < CHUNK, summed, tail).astype(BF)
+    gathered = lax.all_to_all(
+        jnp.broadcast_to(summed[None], (rank_count, CHUNK_PAD, 128)), "tok", 0, 0, tiled=True
+    )
     loss, sdf, gain_one, qkv, out, gain_two, up, down = pl.pallas_call(
         unpack_kernel,
         out_shape=(
@@ -432,8 +477,16 @@
             jax.ShapeDtypeStruct((1, FF, WIDTH), F32),
         ),
         in_specs=[VMEM],
-        out_specs=(VMEM,) * 8,
+        out_specs=(VMEM, VMEM, VMEM, HBM, HBM, VMEM, HBM, HBM),
+        scratch_shapes=[
+            pltpu.VMEM((WIDTH, 3 * WIDTH), F32),
+            pltpu.VMEM((WIDTH, WIDTH), F32),
+            pltpu.VMEM((WIDTH, FF), F32),
+            pltpu.VMEM((FF, WIDTH), F32),
+            pltpu.SemaphoreType.DMA((7,)),
+        ],
         name="unpack",
+        compiler_params=pltpu.CompilerParams(vmem_limit_bytes=16 * 2**20),
     )(gathered)
     return loss[0, 0], sdf[0], gain_one, qkv, out, gain_two, up, down
 

time: 121 us -> 110 us (0.909)
  blocking collectives: 66.1 us -> 29.7 us
  waiting for transfers between devices: 10.6 us -> 37.2 us
  Pallas kernels: 27.6 us -> 17.8 us
  starting transfers between devices: 11.5 us -> 20.8 us
  local copies, waits for them, and re-layouts: 3.58 us -> 0.92 us
  other arithmetic: 0.71 us -> 2.06 us
    all_to_all x2 -> x1, blocking collectives: 66.1 us -> 29.7 us  [shards(): lax.all_to_all(jnp.broadcast_to(summed[None], (rank_count, CHUNK_PAD, 128...]
    all_to_all x0 -> x1, waiting for transfers between devices: none -> 26.4 us  [shards(): shares = lax.all_to_all(total, 'tok', 0, 0, tiled=True)]
    all_to_all x0 -> x1, starting transfers between devices: none -> 9.24 us  [shards(): shares = lax.all_to_all(total, 'tok', 0, 0, tiled=True)]
    pallas_call x3 -> x1, Pallas kernels: 22.5 us -> 13.6 us  [shards(): pl.pallas_call(step_kernel, out_shape=(packet, packet), in_specs=[HBM] +...]
    unnamed x18 -> x0, local copies, waits for them, and re-layouts: 2.86 us -> none
    convert_element_type x0 -> x2, other arithmetic: none -> 1.76 us  [the longest x1 1.65 us: shards(): total = (keep.astype(F32) + far.astype(F32)).astype(BF)]
    ppermute x6 -> x7, waiting for transfers between devices: 4.63 us -> 5.69 us  [swap_pipe(): return lax.ppermute(value, 'pipe', [(0, 1), (1, 0)])]
  transfers between devices with their start and end apart: 8 -> 10, of which waited for: 4 -> 6; matrix products, arithmetic and copies ran while one was open for 1% -> 1% of each run, Pallas kernels for 2% -> 2%
where the time goes in v2:
time: 110 us; the launch traced here: 109 us
  waiting for transfers between devices  37.2 us (34%)
  blocking collectives  29.7 us (27%)
  starting transfers between devices  20.8 us (19%)
  Pallas kernels  17.8 us (16%)
  other arithmetic  2.06 us (2%)
    all_to_all x1, blocking collectives, shards(): lax.all_to_all(jnp.broadcast_to(summed[None], (rank_count, CHUNK_PAD, 128...  29.7 us
    all_to_all x1, waiting for transfers between devices, shards(): shares = lax.all_to_all(total, 'tok', 0, 0, tiled=True)  26.4 us
    pallas_call x1, Pallas kernels, shards(): pl.pallas_call(step_kernel, out_shape=(packet, packet), in_specs=[HBM] +...  13.6 us
    all_to_all x1, starting transfers between devices, shards(): shares = lax.all_to_all(total, 'tok', 0, 0, tiled=True)  9.24 us
    all_to_all x1, starting transfers between devices, shards(): lax.all_to_all(outgoing, 'tok', 0, 0, axis_index_groups=groups, tiled=True)  6.45 us
    ppermute x7, waiting for transfers between devices, swap_pipe(): return lax.ppermute(value, 'pipe', [(0, 1), (1, 0)])  5.69 us
    all_to_all x1, waiting for transfers between devices, shards(): lax.all_to_all(outgoing, 'tok', 0, 0, axis_index_groups=groups, tiled=True)  3.82 us
    ppermute x1, starting transfers between devices, shards(): lax.ppermute(coarse[:, -1:, :], 'tok', [(i, i + 1) for i in range(rank_co...  3.49 us
  transfers between devices with their start and end apart: 10, of which 6 were waited for; matrix products, arithmetic and copies ran while one was open for 1% of the time, Pallas kernels for 2%

profile of v2, /device:TPU:0, one launch (start us, length us, event | category | flops | bytes accessed | tf_op | source)
XLA Modules:
  0.0 109.2 jit_solution(9466347266286571180)
XLA Ops:
  0.6 0.1 collective-permute-start.5
  0.7 0.5 collective-permute-start.6
  1.2 0.1 collective-permute-start.3
  1.3 0.7 slice.9
  2.0 3.5 %collective-permute-start = (bf16[2,1,256]{2,1,0:T(2,128)(2,1)S(1)}, bf16[2,1,256]{2,1,0:T(2,128)(2,1)S(1)}, u32[]{:S(2)}, u32[]{:S(2)}) collective-permute-start(bf16[2,1,256]{2,1,0:T(2,128)(2,1)S(1)} %slice.9), channel_id=1, source_target_pairs={{0,1},{1,2},{2,3},{3,4},{4,5},{5,6},{6,7},{7,8},{8,9},{9,10},{10,1... | collective-permute-start | bytes 3080 | tf_op jit(solution)/shard_map/ppermute | solution.py:399
  5.5 1.3 %collective-permute-done.rim_ref = bf16[2,1,256]{2,1,0:T(2,128)(2,1)S(1)} collective-permute-done((bf16[2,1,256]{2,1,0:T(2,128)(2,1)S(1)}, bf16[2,1,256]{2,1,0:T(2,128)(2,1)S(1)}, u32[]{:S(2)}, u32[]{:S(2)}) %collective-permute-start) | collective-permute-done | bytes 1056 | tf_op jit(solution)/shard_map/ppermute | solution.py:399
  6.8 1.9 %embed.1 = bf16[8,40,256]{2,1,0:T(8,128)(2,1)} custom-call(bf16[2,256,256]{2,1,0:T(8,128)(2,1)} %features_hbm.1, bf16[2,64,256]{2,1,0:T(8,128)(2,1)} %coarse_hbm.1, bf16[2,1,256]{2,1,0:T(2,128)(2,1)S(1)} %collective-permute-done.rim_ref, s32[2,256]{1,0:T(2,128)} %parent_hbm.1, f32[2,256]{1,0:T(2,128)} %target_hbm.1), custom_call_target="tpu_custom_call" | custom-call | tf_op jit(solution)/shard_map/embed/pallas_call | solution.py:402
  8.7 6.5 %all-to-all-start = ((bf16[8,40,256]{2,1,0:T(8,128)(2,1)}), bf16[8,40,256]{2,1,0:T(8,128)(2,1)S(1)}, u32[]{:S(2)}, u32[]{:S(2)}) async-start(bf16[8,40,256]{2,1,0:T(8,128)(2,1)} %embed.1), calls=%async_computation | async-start | bytes 327680 | tf_op jit(solution)/shard_map/all_to_all | solution.py:418
  15.2 0.5 collective-permute-start.1
  15.7 1.0 collective-permute-done.1.gain_far_one
  16.7 0.3 collective-permute-start.2
  17.0 1.0 collective-permute-done.2.gain_far_two
  18.1 3.8 %all-to-all-done.received_ref = bf16[8,40,256]{2,1,0:T(8,128)(2,1)S(1)} async-done(((bf16[8,40,256]{2,1,0:T(8,128)(2,1)}), bf16[8,40,256]{2,1,0:T(8,128)(2,1)S(1)}, u32[]{:S(2)}, u32[]{:S(2)}) %all-to-all-start) | async-done | bytes 163872 | tf_op jit(solution)/shard_map/all_to_all | solution.py:418
  21.9 13.6 %step.1 = (bf16[64,104,128]{2,1,0:T(8,128)(2,1)S(1)}, bf16[64,104,128]{2,1,0:T(8,128)(2,1)S(1)}) custom-call(s32[2,64]{1,0:T(2,128)} %counts_hbm.1, bf16[8,40,256]{2,1,0:T(8,128)(2,1)S(1)} %all-to-all-done.received_ref, f32[1,256]{1,0:T(1,128)S(1)} %collective-permute-done.1.gain_far_one, f32[1,256]{1,0:T(1,128)S(1)} %collective-permute-done.2.gain_far_two, ...), custom_call_target="tpu_custom_call" | custom-call | tf_op jit(solution)/shard_map/step/pallas_call | solution.py:420
  35.5 0.1 collective-permute-start.7
  35.6 3.6 %collective-permute-done.7 = bf16[64,104,128]{2,1,0:T(8,128)(2,1)S(1)} collective-permute-done((bf16[64,104,128]{2,1,0:T(8,128)(2,1)S(1)}, bf16[64,104,128]{2,1,0:T(8,128)(2,1)S(1)}, u32[]{:S(2)}, u32[]{:S(2)}) %collective-permute-start.7) | collective-permute-done | bytes 1703968 | tf_op jit(solution)/shard_map/ppermute | solution.py:387
  39.2 1.7 %add_convert_fusion = bf16[64,104,128]{2,1,0:T(8,128)(2,1)} fusion(bf16[64,104,128]{2,1,0:T(8,128)(2,1)S(1)} %collective-permute-done.7, bf16[64,104,128]{2,1,0:T(8,128)(2,1)S(1)} %get-tuple-element.18), kind=kLoop, calls=%fused_computation.1 | loop fusion | flops 3407872 | bytes 5111808 | tf_op jit(solution)/shard_map/convert_element_type | solution.py:456
  40.9 9.2 %all-to-all-start.1 = ((bf16[64,104,128]{2,1,0:T(8,128)(2,1)}), bf16[64,104,128]{2,1,0:T(8,128)(2,1)S(1)}, u32[]{:S(2)}, u32[]{:S(2)}) async-start(bf16[64,104,128]{2,1,0:T(8,128)(2,1)} %add_convert_fusion), calls=%async_computation.1 | async-start | bytes 3407872 | tf_op jit(solution)/shard_map/all_to_all | solution.py:457
  50.1 26.4 %all-to-all-done.1 = bf16[64,104,128]{2,1,0:T(8,128)(2,1)S(1)} async-done(((bf16[64,104,128]{2,1,0:T(8,128)(2,1)}), bf16[64,104,128]{2,1,0:T(8,128)(2,1)S(1)}, u32[]{:S(2)}, u32[]{:S(2)}) %all-to-all-start.1) | async-done | bytes 1703968 | tf_op jit(solution)/shard_map/all_to_all | solution.py:457
  76.6 0.3 convert_reduce_fusion
  76.9 0.1 select_convert_fusion
  77.0 0.2 broadcast_in_dim.34
  77.2 29.7 %all_to_all.15.in_ref = bf16[64,104,128]{2,1,0:T(8,128)(2,1)S(1)} all-to-all(bf16[64,104,128]{2,1,0:T(8,128)(2,1)S(1)} %broadcast_in_dim.34), channel_id=1, replica_groups=mesh['pipe'=2,'tok'=64] {'tok'}, dimensions={0} | all-to-all | bytes 3407872 | tf_op jit(solution)/shard_map/all_to_all | solution.py:464
  106.9 2.3 %unpack.1 = (f32[1,128]{1,0:T(1,128)}, f32[1,256]{1,0:T(1,128)}, f32[1,256]{1,0:T(1,128)}, f32[1,256,768]{2,1,0:T(8,128)}, f32[1,256,256]{2,1,0:T(8,128)}, /*ind...) custom-call(bf16[64,104,128]{2,1,0:T(8,128)(2,1)S(1)} %all_to_all.15.in_ref), custom_call_target="tpu_custom_call" | custom-call | tf_op jit(solution)/shard_map/unpack/pallas_call | solution.py:467
  (9 shorter events, 0.1 us)
Async XLA Ops:
  0.6 21.3 %collective-permute-start.5 = (bf16[1,256,1024]{2,1,0:T(8,128)(2,1)}, bf16[1,256,1024]{2,1,0:T(8,128)(2,1)S(1)}, u32[]{:S(2)}, u32[]{:S(2)}) collective-permute-start(bf16[1,256,1024]{2,1,0:T(8,128)(2,1)} %up_own.1), channel_id=1, source_target_pairs={{0,64},{64,0},{1,65},{65,1},{2,66},{66,2},{3,67},{67,3},{4,68},{68... | collective-permute-start | bytes 1572872 | tf_op jit(solution)/shard_map/ppermute | solution.py:387
  0.7 21.2 %collective-permute-start.6 = (bf16[1,1024,256]{2,1,0:T(8,128)(2,1)}, bf16[1,1024,256]{2,1,0:T(8,128)(2,1)S(1)}, u32[]{:S(2)}, u32[]{:S(2)}) collective-permute-start(bf16[1,1024,256]{2,1,0:T(8,128)(2,1)} %down_own.1), channel_id=1, source_target_pairs={{0,64},{64,0},{1,65},{65,1},{2,66},{66,2},{3,67},{67,3},{4,68},{68... | collective-permute-start | bytes 1572872 | tf_op jit(solution)/shard_map/ppermute | solution.py:387
  1.2 20.7 %collective-permute-start.3 = (bf16[1,256,768]{2,1,0:T(8,128)(2,1)}, bf16[1,256,768]{2,1,0:T(8,128)(2,1)S(1)}, u32[]{:S(2)}, u32[]{:S(2)}) collective-permute-start(bf16[1,256,768]{2,1,0:T(8,128)(2,1)} %qkv_own.1), channel_id=1, source_target_pairs={{0,64},{64,0},{1,65},{65,1},{2,66},{66,2},{3,67},{67,3},{4,68},{68... | collective-permute-start | bytes 1179656 | tf_op jit(solution)/shard_map/ppermute | solution.py:387
  2.0 4.8 %collective-permute-start = (bf16[2,1,256]{2,1,0:T(2,128)(2,1)S(1)}, bf16[2,1,256]{2,1,0:T(2,128)(2,1)S(1)}, u32[]{:S(2)}, u32[]{:S(2)}) collective-permute-start(bf16[2,1,256]{2,1,0:T(2,128)(2,1)S(1)} %slice.9), channel_id=1, source_target_pairs={{0,1},{1,2},{2,3},{3,4},{4,5},{5,6},{6,7},{7,8},{8,9},{9,10},{10,1... | collective-permute-start | bytes 3080 | tf_op jit(solution)/shard_map/ppermute | solution.py:399
  8.7 13.2 %all-to-all-start = ((bf16[8,40,256]{2,1,0:T(8,128)(2,1)}), bf16[8,40,256]{2,1,0:T(8,128)(2,1)S(1)}, u32[]{:S(2)}, u32[]{:S(2)}) async-start(bf16[8,40,256]{2,1,0:T(8,128)(2,1)} %embed.1), calls=%async_computation | async-start | bytes 327680 | tf_op jit(solution)/shard_map/all_to_all | solution.py:418
  15.1 2.9 %collective-permute-start.4 = (bf16[1,256,256]{2,1,0:T(8,128)(2,1)}, bf16[1,256,256]{2,1,0:T(8,128)(2,1)S(1)}, u32[]{:S(2)}, u32[]{:S(2)}) collective-permute-start(bf16[1,256,256]{2,1,0:T(8,128)(2,1)} %out_own.1), channel_id=1, source_target_pairs={{0,64},{64,0},{1,65},{65,1},{2,66},{66,2},{3,67},{67,3},{4,68},{68... | collective-permute-start | bytes 393224 | tf_op jit(solution)/shard_map/ppermute | solution.py:387
  15.2 1.5 %collective-permute-start.1 = (f32[1,256]{1,0:T(1,128)}, f32[1,256]{1,0:T(1,128)S(1)}, u32[]{:S(2)}, u32[]{:S(2)}) collective-permute-start(f32[1,256]{1,0:T(1,128)} %gain_own_one_hbm.1), channel_id=1, source_target_pairs={{0,64},{64,0},{1,65},{65,1},{2,66},{66,2},{3,67},{67,3},{4,68},{68... | collective-permute-start | bytes 3080 | tf_op jit(solution)/shard_map/ppermute | solution.py:387
  16.7 1.4 %collective-permute-start.2 = (f32[1,256]{1,0:T(1,128)}, f32[1,256]{1,0:T(1,128)S(1)}, u32[]{:S(2)}, u32[]{:S(2)}) collective-permute-start(f32[1,256]{1,0:T(1,128)} %gain_own_two_hbm.1), channel_id=1, source_target_pairs={{0,64},{64,0},{1,65},{65,1},{2,66},{66,2},{3,67},{67,3},{4,68},{68... | collective-permute-start | bytes 3080 | tf_op jit(solution)/shard_map/ppermute | solution.py:387
  35.5 3.7 %collective-permute-start.7 = (bf16[64,104,128]{2,1,0:T(8,128)(2,1)S(1)}, bf16[64,104,128]{2,1,0:T(8,128)(2,1)S(1)}, u32[]{:S(2)}, u32[]{:S(2)}) collective-permute-start(bf16[64,104,128]{2,1,0:T(8,128)(2,1)S(1)} %get-tuple-element.19), channel_id=1, source_target_pairs={{0,64},{64,0},{1,65},{65,1},{2,66},{66,2},{3,67},{67,3},{4,68},{68... | collective-permute-start | bytes 5111816 | tf_op jit(solution)/shard_map/ppermute | solution.py:387
  40.9 35.7 %all-to-all-start.1 = ((bf16[64,104,128]{2,1,0:T(8,128)(2,1)}), bf16[64,104,128]{2,1,0:T(8,128)(2,1)S(1)}, u32[]{:S(2)}, u32[]{:S(2)}) async-start(bf16[64,104,128]{2,1,0:T(8,128)(2,1)} %add_convert_fusion), calls=%async_computation.1 | async-start | bytes 3407872 | tf_op jit(solution)/shard_map/all_to_all | solution.py:457

commit v3 on v2

--- a/solution.py
+++ b/solution.py
@@ -16,8 +16,10 @@
 FF = 1024
 HEAD = WIDTH // H
 EPS = 1e-06
-CHUNK = 96
-CHUNK_PAD = 104
+CHUNK = 80
+CHUNK_PAD = 88
+SLAB = 16
+STAT_AT = 49
 SEND_ROWS = 40
 BF = jnp.bfloat16
 F32 = jnp.float32
@@ -85,12 +87,16 @@
 
 
 def group_max(values):
-    lane = iota(values.shape, 1)
-    for step in (1, 2, 4, 8, 16):
-        ahead = pltpu.roll(values, values.shape[1] - step, 1)
-        behind = pltpu.roll(values, step, 1)
-        values = jnp.maximum(values, jnp.where((lane & step) == 0, ahead, behind))
-    return values
+    halves = []
+    for side in range(2):
+        half = values[:, side * 128 : (side + 1) * 128]
+        lane = iota((1, 128), 1)
+        for step in (1, 2, 4, 8, 16):
+            ahead = pltpu.roll(half, 128 - step, 1)
+            behind = pltpu.roll(half, step, 1)
+            half = jnp.maximum(half, jnp.where((lane & step) == 0, ahead, behind))
+        halves.append(half)
+    return jnp.concatenate(halves, axis=1)
 
 
 def group_sum(values, same_head):
@@ -168,15 +174,43 @@
     def window(value, w):
         return value[w * WIN : (w + 1) * WIN]
 
-    def store_grad(section, block, value):
-        for i in range(GROUP):
-            slab = block * GROUP + i
-            base = slab % 3 * WIN
-            grads[section, slab // 3, base : base + WIN, :] = window(value, i).astype(BF)
-
-    def store_wide(section, block, value):
-        store_grad(section, block, value[:, :128])
-        store_grad(section, block + 1, value[:, 128:])
+    def store_grad(stream, place, value):
+        for i in range(ROWS // SLAB):
+            slab = place * (ROWS // SLAB) + i
+            base = slab % 5 * SLAB
+            grads[stream, slab // 5, base : base + SLAB, :] = value[i * SLAB : (i + 1) * SLAB].astype(BF)
+
+    def store_wide(stream, place, value):
+        store_grad(stream, place, value[:, :128])
+        store_grad(stream, place + 1, value[:, 128:])
+
+    stat_row = iota((8, 128), 0)
+    for stream in range(2):
+        grads[stream, :, CHUNK:CHUNK_PAD, :] = jnp.zeros((64, CHUNK_PAD - CHUNK, 128), BF)
+
+    def store_stats(stream, lines):
+        halves = []
+        for line in lines:
+            halves += [line[:, i : i + 128] for i in range(0, line.shape[1], 128)]
+        for c, line in enumerate(halves):
+            high, low = split_two(line)
+            both = jnp.where(
+                stat_row == 2 * micro, high.astype(F32), jnp.where(stat_row == 2 * micro + 1, low.astype(F32), 0.0)
+            )
+            grads[stream, STAT_AT + c, CHUNK:CHUNK_PAD, :] = both.astype(BF)
+
+    stores = []
+
+    def send_out(stream, first_chunk, last_chunk):
+        number = len(stores)
+        chunks = pl.ds(first_chunk, last_chunk - first_chunk)
+        copies = [
+            pltpu.make_async_copy(grads.at[stream, chunks], ref.at[chunks], store_sem.at[number])
+            for ref in (keep_ref, send_ref)
+        ]
+        stores.append(copies[0])
+        pl.when(micro == stream)(copies[0].start)
+        pl.when(micro != stream)(copies[1].start)
 
     def forward(k):
         x = x_buf[k].astype(F32)
@@ -219,11 +253,11 @@
             up = nn(normed_two, w_up[k, :, cols])
             root = math.sqrt(2.0 / math.pi)
             square = up * up
-            bent = jnp.tanh(root * (up + 0.044715 * (square * up)))
-            half = 0.5 * (1.0 + bent)
+            half = 0.5 * jnp.tanh(up * (root + (root * 0.044715) * square)) + 0.5
             hidden = (up * half).astype(BF)
             hidden_buf[k, j] = hidden
-            slope_buf[k, j] = half + (0.5 * root) * up * (1.0 - bent * bent) * (1.0 + (3 * 0.044715) * square)
+            bend = up * (2 * root + (6 * root * 0.044715) * square)
+            slope_buf[k, j] = half * (1.0 + bend * (1.0 - half))
             total = total + nn(hidden, w_down[k, cols, :])
         return total.astype(BF)
 
@@ -233,21 +267,33 @@
         inner = jnp.mean(scaled * value, axis=-1, keepdims=True)
         return inv * (scaled - value * (inv * inv * inner)), gain_grad
 
-    def backward(k, out_grad):
+    def backward(k, out_grad, slope, pulled):
         back = None
-        for j in range(4):
+        down_lines = []
+        places = {0: 6, 1: 10, 2: 0, 3: 2} if k == 0 else {0: 0, 1: 2, 2: 4, 3: 6}
+        for j in (2, 3, 0, 1):
             cols = slice(j * WIDTH, (j + 1) * WIDTH)
-            store_wide(k, 16 + 2 * j, tn(hidden_buf[k, j], out_grad))
-            hidden_grad = nt(out_grad, w_down[k, cols, :]).astype(BF)
-            up_grad = (slope_buf[k, j] * hidden_grad.astype(F32)).astype(BF)
-            store_wide(k, 8 + 2 * j, tn(normed_two_buf[k], up_grad))
+            if k == 0:
+                stream, place = (1, 12 + 2 * j) if j >= 2 else (0, 4 + 4 * j)
+                out_low = out_grad.astype(BF)
+                store_wide(stream, place, tn(hidden_buf[k, j], out_low))
+                hidden_grad = nt(out_low, w_down[k, cols, :]).astype(BF).astype(F32)
+            else:
+                down_lines.append(jnp.sum(hidden_buf[k, j].astype(F32) * slope, axis=0, keepdims=True))
+                hidden_grad = slope * pulled[j]
+            up_grad = (slope_buf[k, j] * hidden_grad).astype(BF)
+            store_wide(k, places[j], tn(normed_two_buf[k], up_grad))
             term = nt(up_grad, w_up[k, :, cols])
             back = term if back is None else back + term
+            if k == 0 and j == 3:
+                send_out(1, 51, 64)
+        if k == 0:
+            send_out(0, 0, 38)
         normed_two_grad = back.astype(BF).astype(F32)
         res_grad, gain_two_grad = norm_back(normed_two_grad, after_buf[k], inv_two[k], gain(k, 1))
-        after_grad = out_grad.astype(F32) + res_grad
+        after_grad = out_grad + res_grad
         after_low = after_grad.astype(BF)
-        store_wide(k, 6, tn(mixed_buf[k], after_low))
+        store_wide(k, 12 if k == 0 else 8, tn(mixed_buf[k], after_low))
         mixed_grad = nt(after_low, w_out[k]).astype(BF)
         for w in range(GROUP):
             rows = slice(w * WIN, (w + 1) * WIN)
@@ -256,7 +302,7 @@
         prob_low = prob.astype(BF)
         prob_grad = score_buf[...].astype(BF).astype(F32)
         flow = prob * prob_grad
-        score_grad = ((flow - prob * group_sum(flow, same_head)) * HEAD**-0.5).astype(BF)
+        score_grad = (flow - prob * group_sum(flow, same_head)) * HEAD**-0.5
 
         def fold(value):
             total = None
@@ -267,19 +313,19 @@
 
         for w in range(GROUP):
             rows = slice(w * WIN, (w + 1) * WIN)
-            grad_w = window(score_grad, w)
+            grad_w = jnp.where(mask_buf[k, w : w + 1, :] > 0.5, window(score_grad, w), 0.0).astype(BF)
             dpacked_buf[0, rows, :] = nn(grad_w, expand(packed_buf[k, 1, rows, :])).astype(BF)
             dpacked_buf[1, rows, :] = fold(tn(grad_w, packed_buf[k, 0, rows, :])).astype(BF)
             dpacked_buf[2, rows, :] = fold(tn(window(prob_low, w), window(mixed_grad, w))).astype(BF)
         back = None
         for j in range(3):
             piece = dpacked_buf[j]
-            store_wide(k, 2 * j, tn(normed_buf[k], piece))
+            store_wide(k, (14 if k == 0 else 10) + 2 * j, tn(normed_buf[k], piece))
             term = nt(piece, w_qkv[k, :, j * WIDTH : (j + 1) * WIDTH])
             back = term if back is None else back + term
         normed_grad = back.astype(BF).astype(F32)
         in_res, gain_one_grad = norm_back(normed_grad, x_buf[k].astype(F32), inv_one[k], gain(k, 0))
-        return (after_grad + in_res).astype(BF), gain_one_grad, gain_two_grad
+        return (after_grad + in_res).astype(BF), gain_one_grad, gain_two_grad, down_lines[2:] + down_lines[:2]
 
     received = received_ref[:, 0:WIN, :].reshape(ROWS, WIDTH)
     x_buf[0] = exchange(received)
@@ -304,38 +350,31 @@
     slope = 2.0 * residue / math.sqrt(3 * ROWS * 64 // 4)
     loss = jnp.sum(residue * residue, axis=0, keepdims=True)
     sdf_grad = jnp.sum(slope * section_one, axis=0, keepdims=True)
-    head_grad = (slope * sdf).astype(BF)
-    middle_grad, one_one, one_two = backward(1, head_grad)
-    unused, zero_one, zero_two = backward(0, exchange(middle_grad))
-    del unused
+    high = sdf.astype(BF).astype(F32)
+    middle = (sdf - high).astype(BF).astype(F32)
+    row = iota((16, WIDTH), 0)
+    parts = jnp.where(row == 0, high, jnp.where(row == 1, middle, jnp.where(row == 2, sdf - high - middle, 0.0)))
+    parts = parts.astype(BF)
+    pulled = [
+        jnp.sum(nt(parts, w_down[1, j * WIDTH : (j + 1) * WIDTH, :]), axis=0, keepdims=True) for j in range(4)
+    ]
     loss_row = jnp.broadcast_to(loss, (1, 128))
-    stat_row = iota((8, 128), 0)
-    for k, (gain_one, gain_two) in enumerate(((zero_one, zero_two), (one_one, one_two))):
-        lines = []
-        for line in (gain_one, gain_two, sdf_grad):
-            lines += [line[:, :128], line[:, 128:]]
-        lines.append(loss_row)
-        grads[k, :, CHUNK:CHUNK_PAD, :] = jnp.zeros((64, CHUNK_PAD - CHUNK, 128), BF)
-        for c, line in enumerate(lines):
-            high, low = split_two(line)
-            both = jnp.where(
-                stat_row == 2 * micro, high.astype(F32), jnp.where(stat_row == 2 * micro + 1, low.astype(F32), 0.0)
-            )
-            grads[k, c, CHUNK:CHUNK_PAD, :] = both.astype(BF)
-    stores = [
-        pltpu.make_async_copy(grads.at[micro], keep_ref, store_sem.at[0]),
-        pltpu.make_async_copy(grads.at[1 - micro], send_ref, store_sem.at[1]),
-    ]
-    for store in stores:
-        store.start()
+    middle_grad, gain_one, gain_two, down_lines = backward(1, slope * sdf, slope, pulled)
+    store_stats(1, [gain_one, gain_two, sdf_grad, loss_row] + down_lines)
+    send_out(1, 0, 51)
+    unused, gain_one, gain_two, none = backward(0, exchange(middle_grad).astype(F32), None, None)
+    del unused, none
+    store_stats(0, [gain_one, gain_two, sdf_grad, loss_row])
+    send_out(0, 38, 64)
     for store in stores:
         store.wait()
 
 
 def unpack_kernel(
-    in_ref, loss_ref, sdf_ref, gain_one_ref, qkv_hbm, out_hbm, gain_two_ref, up_hbm, down_hbm,
+    in_ref, moved_ref, sdf_row_ref, loss_ref, sdf_ref, gain_one_ref, qkv_hbm, out_hbm, gain_two_ref, up_hbm, down_hbm,
     qkv_ref, out_ref, up_ref, down_ref, store_sem,
 ):
+    micro = lax.axis_index("pipe")
     stores = []
 
     def store(source, target):
@@ -343,34 +382,52 @@
         copy.start()
         stores.append(copy)
 
-    for block in range(24):
-        for i in range(GROUP):
-            slab = block * GROUP + i
-            base = slab % 3 * WIN
-            piece = in_ref[slab // 3, base : base + WIN, :].astype(F32)
-            rows = slice(i * WIN, (i + 1) * WIN)
-            if block < 6:
-                qkv_ref[rows, block * 128 : (block + 1) * 128] = piece
-            elif block < 8:
-                out_ref[rows, (block - 6) * 128 : (block - 5) * 128] = piece
-            elif block < 16:
-                up_ref[rows, (block - 8) * 128 : (block - 7) * 128] = piece
-            else:
-                j, side = divmod(block - 16, 2)
-                down_ref[j * 256 + i * WIN : j * 256 + (i + 1) * WIN, side * 128 : (side + 1) * 128] = piece
-        if block == 5:
-            store(qkv_ref, qkv_hbm.at[0])
-        elif block == 7:
-            store(out_ref, out_hbm.at[0])
-        elif block == 15:
-            store(up_ref, up_hbm.at[0])
-        elif block > 15 and block % 2 == 1:
-            rows = slice((block - 17) // 2 * 256, (block - 15) // 2 * 256)
-            store(down_ref.at[rows], down_hbm.at[0, rows])
+    def wide(source, first_chunk, place, target, base):
+        for side in range(2):
+            for i in range(ROWS // SLAB):
+                slab = (place + side) * (ROWS // SLAB) + i
+                low = slab % 5 * SLAB
+                piece = source[slab // 5 - first_chunk, low : low + SLAB, :].astype(F32)
+                target(i, side, piece, base)
+
+    def into(ref, base):
+        def put(i, side, piece, low):
+            ref[low + i * SLAB : low + (i + 1) * SLAB, base + side * 128 : base + (side + 1) * 128] = piece
+
+        return put
+
+    def section(up_at, out_at, qkv_at):
+        for j in range(4):
+            wide(in_ref, 0, up_at[j], into(up_ref, j * WIDTH), 0)
+        wide(in_ref, 0, out_at, into(out_ref, 0), 0)
+        for j in range(3):
+            wide(in_ref, 0, qkv_at + 2 * j, into(qkv_ref, j * WIDTH), 0)
+
     lines = []
-    for c in range(7):
-        pair = in_ref[c, CHUNK:CHUNK_PAD, :].astype(F32)
+    for c in range(15):
+        pair = in_ref[STAT_AT + c, CHUNK:CHUNK_PAD, :].astype(F32)
         lines.append(pair[0:1] + pair[1:2])
+
+    @pl.when(micro == 0)
+    def _():
+        section((6, 10, 0, 2), 12, 14)
+        for j, place in ((0, 4), (1, 8)):
+            wide(in_ref, 0, place, into(down_ref, 0), j * WIDTH)
+        for j in (2, 3):
+            wide(moved_ref, 51, 12 + 2 * j, into(down_ref, 0), j * WIDTH)
+
+    @pl.when(micro == 1)
+    def _():
+        section((0, 2, 4, 6), 8, 10)
+        diagonal = iota((128, 128), 0) == iota((128, 128), 1)
+        for c in range(8):
+            column = jnp.sum(jnp.where(diagonal, lines[7 + c], 0.0), axis=1, keepdims=True)
+            down_ref[c * 128 : (c + 1) * 128, :] = column * sdf_row_ref[...]
+
+    store(qkv_ref, qkv_hbm.at[0])
+    store(out_ref, out_hbm.at[0])
+    store(up_ref, up_hbm.at[0])
+    store(down_ref, down_hbm.at[0])
     for ref, c in ((gain_one_ref, 0), (gain_two_ref, 2), (sdf_ref, 4)):
         ref[0:1, 0:128] = lines[c]
         ref[0:1, 128:256] = lines[c + 1]
@@ -447,7 +504,7 @@
             pltpu.VMEM((1, WIDTH), F32),
             pltpu.SMEM((2, 64), jnp.int32),
             pltpu.SemaphoreType.DMA((12,)),
-            pltpu.SemaphoreType.DMA((2,)),
+            pltpu.SemaphoreType.DMA((4,)),
         ],
         name="step",
         compiler_params=pltpu.CompilerParams(vmem_limit_bytes=32 * 2**20),
@@ -464,6 +521,7 @@
     gathered = lax.all_to_all(
         jnp.broadcast_to(summed[None], (rank_count, CHUNK_PAD, 128)), "tok", 0, 0, tiled=True
     )
+    moved = lax.ppermute(gathered[51:64], "pipe", [(1, 0)])
     loss, sdf, gain_one, qkv, out, gain_two, up, down = pl.pallas_call(
         unpack_kernel,
         out_shape=(
@@ -476,7 +534,7 @@
             jax.ShapeDtypeStruct((1, WIDTH, FF), F32),
             jax.ShapeDtypeStruct((1, FF, WIDTH), F32),
         ),
-        in_specs=[VMEM],
+        in_specs=[VMEM, VMEM, VMEM],
         out_specs=(VMEM, VMEM, VMEM, HBM, HBM, VMEM, HBM, HBM),
         scratch_shapes=[
             pltpu.VMEM((WIDTH, 3 * WIDTH), F32),
@@ -487,7 +545,7 @@
         ],
         name="unpack",
         compiler_params=pltpu.CompilerParams(vmem_limit_bytes=16 * 2**20),
-    )(gathered)
+    )(gathered, moved, fix(w_sdf[None]))
     return loss[0, 0], sdf[0], gain_one, qkv, out, gain_two, up, down
 
 

time: 110 us -> 109 us (level)
  blocking collectives: 29.7 us -> 26.6 us
  starting transfers between devices: 20.8 us -> 22.1 us
  waiting for transfers between devices: 37.2 us -> 36.1 us
    all_to_all x1, blocking collectives: 29.7 us -> 26.6 us  [shards(): lax.all_to_all(jnp.broadcast_to(summed[None], (rank_count, CHUNK_PAD, 128...]
    all_to_all x1, waiting for transfers between devices: 26.4 us -> 23.5 us  [shards(): shares = lax.all_to_all(total, 'tok', 0, 0, tiled=True)]
    ppermute x0 -> x1, waiting for transfers between devices: none -> 2.17 us  [shards(): moved = lax.ppermute(gathered[51:64], 'pipe', [(1, 0)])]
    ppermute x0 -> x1, starting transfers between devices: none -> 1.29 us  [shards(): moved = lax.ppermute(gathered[51:64], 'pipe', [(1, 0)])]
  transfers between devices with their start and end apart: 10 -> 11, of which waited for: 6 -> 7; matrix products, arithmetic and copies ran while one was open for 1% -> 1% of each run, Pallas kernels for 2% -> 2%
where the time goes in v3:
time: 109 us; the launch traced here: 107 us
  waiting for transfers between devices  36.1 us (33%)
  blocking collectives  26.6 us (24%)
  starting transfers between devices  22.1 us (20%)
  Pallas kernels  18.9 us (17%)
  other arithmetic  1.87 us (2%)
    all_to_all x1, blocking collectives, shards(): lax.all_to_all(jnp.broadcast_to(summed[None], (rank_count, CHUNK_PAD, 128...  26.6 us
    all_to_all x1, waiting for transfers between devices, shards(): shares = lax.all_to_all(total, 'tok', 0, 0, tiled=True)  23.5 us
    pallas_call x1, Pallas kernels, shards(): pl.pallas_call(step_kernel, out_shape=(packet, packet), in_specs=[HBM] +...  13.8 us
    all_to_all x1, starting transfers between devices, shards(): shares = lax.all_to_all(total, 'tok', 0, 0, tiled=True)  9.24 us
    all_to_all x1, starting transfers between devices, shards(): lax.all_to_all(outgoing, 'tok', 0, 0, axis_index_groups=groups, tiled=True)  6.45 us
    ppermute x7, waiting for transfers between devices, swap_pipe(): return lax.ppermute(value, 'pipe', [(0, 1), (1, 0)])  5.32 us
    all_to_all x1, waiting for transfers between devices, shards(): lax.all_to_all(outgoing, 'tok', 0, 0, axis_index_groups=groups, tiled=True)  3.82 us
    ppermute x1, starting transfers between devices, shards(): lax.ppermute(coarse[:, -1:, :], 'tok', [(i, i + 1) for i in range(rank_co...  3.49 us
  transfers between devices with their start and end apart: 11, of which 7 were waited for; matrix products, arithmetic and copies ran while one was open for 1% of the time, Pallas kernels for 2%

profile of v3, /device:TPU:0, one launch (start us, length us, event | category | flops | bytes accessed | tf_op | source)
XLA Modules:
  0.0 107.3 jit_solution(13576247217526867368)
XLA Ops:
  0.7 0.5 collective-permute-start.6
  1.2 0.1 collective-permute-start.3
  1.3 0.7 slice.12
  2.0 3.5 %collective-permute-start = (bf16[2,1,256]{2,1,0:T(2,128)(2,1)S(1)}, bf16[2,1,256]{2,1,0:T(2,128)(2,1)S(1)}, u32[]{:S(2)}, u32[]{:S(2)}) collective-permute-start(bf16[2,1,256]{2,1,0:T(2,128)(2,1)S(1)} %slice.12), channel_id=1, source_target_pairs={{0,1},{1,2},{2,3},{3,4},{4,5},{5,6},{6,7},{7,8},{8,9},{9,10},{10,1... | collective-permute-start | bytes 3080 | tf_op jit(solution)/shard_map/ppermute | solution.py:456
  5.5 1.3 %collective-permute-done.rim_ref = bf16[2,1,256]{2,1,0:T(2,128)(2,1)S(1)} collective-permute-done((bf16[2,1,256]{2,1,0:T(2,128)(2,1)S(1)}, bf16[2,1,256]{2,1,0:T(2,128)(2,1)S(1)}, u32[]{:S(2)}, u32[]{:S(2)}) %collective-permute-start) | collective-permute-done | bytes 1056 | tf_op jit(solution)/shard_map/ppermute | solution.py:456
  6.8 1.9 %embed.1 = bf16[8,40,256]{2,1,0:T(8,128)(2,1)} custom-call(bf16[2,256,256]{2,1,0:T(8,128)(2,1)} %features_hbm.1, bf16[2,64,256]{2,1,0:T(8,128)(2,1)} %coarse_hbm.1, bf16[2,1,256]{2,1,0:T(2,128)(2,1)S(1)} %collective-permute-done.rim_ref, s32[2,256]{1,0:T(2,128)} %parent_hbm.1, f32[2,256]{1,0:T(2,128)} %target_hbm.1), custom_call_target="tpu_custom_call" | custom-call | tf_op jit(solution)/shard_map/embed/pallas_call | solution.py:459
  8.7 6.5 %all-to-all-start = ((bf16[8,40,256]{2,1,0:T(8,128)(2,1)}), bf16[8,40,256]{2,1,0:T(8,128)(2,1)S(1)}, u32[]{:S(2)}, u32[]{:S(2)}) async-start(bf16[8,40,256]{2,1,0:T(8,128)(2,1)} %embed.1), calls=%async_computation | async-start | bytes 327680 | tf_op jit(solution)/shard_map/all_to_all | solution.py:475
  15.2 0.5 collective-permute-start.1
  15.7 1.0 collective-permute-done.1.gain_far_one
  16.7 0.3 collective-permute-start.2
  17.0 1.0 collective-permute-done.2.gain_far_two
  18.1 3.8 %all-to-all-done.received_ref = bf16[8,40,256]{2,1,0:T(8,128)(2,1)S(1)} async-done(((bf16[8,40,256]{2,1,0:T(8,128)(2,1)}), bf16[8,40,256]{2,1,0:T(8,128)(2,1)S(1)}, u32[]{:S(2)}, u32[]{:S(2)}) %all-to-all-start) | async-done | bytes 163872 | tf_op jit(solution)/shard_map/all_to_all | solution.py:475
  21.9 13.8 %step.1 = (bf16[64,88,128]{2,1,0:T(8,128)(2,1)S(1)}, bf16[64,88,128]{2,1,0:T(8,128)(2,1)S(1)}) custom-call(s32[2,64]{1,0:T(2,128)} %counts_hbm.1, bf16[8,40,256]{2,1,0:T(8,128)(2,1)S(1)} %all-to-all-done.received_ref, f32[1,256]{1,0:T(1,128)S(1)} %collective-permute-done.1.gain_far_one, f32[1,256]{1,0:T(1,128)S(1)} %collective-permute-done.2.gain_far_two, ...), custom_call_target="tpu_custom_call" | custom-call | tf_op jit(solution)/shard_map/step/pallas_call | solution.py:477
  35.8 3.2 %collective-permute-done.7 = bf16[64,88,128]{2,1,0:T(8,128)(2,1)S(1)} collective-permute-done((bf16[64,88,128]{2,1,0:T(8,128)(2,1)S(1)}, bf16[64,88,128]{2,1,0:T(8,128)(2,1)S(1)}, u32[]{:S(2)}, u32[]{:S(2)}) %collective-permute-start.7) | collective-permute-done | bytes 1441824 | tf_op jit(solution)/shard_map/ppermute | solution.py:444
  39.0 1.5 %add_convert_fusion = bf16[64,88,128]{2,1,0:T(8,128)(2,1)} fusion(bf16[64,88,128]{2,1,0:T(8,128)(2,1)S(1)} %collective-permute-done.7, bf16[64,88,128]{2,1,0:T(8,128)(2,1)S(1)} %get-tuple-element.18), kind=kLoop, calls=%fused_computation.1 | loop fusion | flops 2883584 | bytes 4325376 | tf_op jit(solution)/shard_map/convert_element_type | solution.py:513
  40.5 9.2 %all-to-all-start.1 = ((bf16[64,88,128]{2,1,0:T(8,128)(2,1)}), bf16[64,88,128]{2,1,0:T(8,128)(2,1)S(1)}, u32[]{:S(2)}, u32[]{:S(2)}) async-start(bf16[64,88,128]{2,1,0:T(8,128)(2,1)} %add_convert_fusion), calls=%async_computation.1 | async-start | bytes 2883584 | tf_op jit(solution)/shard_map/all_to_all | solution.py:514
  49.8 23.5 %all-to-all-done.1 = bf16[64,88,128]{2,1,0:T(8,128)(2,1)S(1)} async-done(((bf16[64,88,128]{2,1,0:T(8,128)(2,1)}), bf16[64,88,128]{2,1,0:T(8,128)(2,1)S(1)}, u32[]{:S(2)}, u32[]{:S(2)}) %all-to-all-start.1) | async-done | bytes 1441824 | tf_op jit(solution)/shard_map/all_to_all | solution.py:514
  73.3 0.2 convert_reduce_fusion
  73.5 0.1 select_convert_fusion
  73.6 0.2 broadcast_in_dim.35
  73.8 26.6 %all_to_all.15.in_ref = bf16[64,88,128]{2,1,0:T(8,128)(2,1)S(1)} all-to-all(bf16[64,88,128]{2,1,0:T(8,128)(2,1)S(1)} %broadcast_in_dim.35), channel_id=1, replica_groups=mesh['pipe'=2,'tok'=64] {'tok'}, dimensions={0} | all-to-all | bytes 2883584 | tf_op jit(solution)/shard_map/all_to_all | solution.py:521
  100.4 1.3 %collective-permute-start.8 = (bf16[13,88,128]{2,1,0:T(8,128)(2,1)S(1)}, bf16[13,88,128]{2,1,0:T(8,128)(2,1)S(1)}, u32[]{:S(2)}, u32[]{:S(2)}) collective-permute-start(bf16[13,88,128]{2,1,0:T(8,128)(2,1)S(1)} %slice.17), channel_id=1, source_target_pairs={{64,0},{65,1},{66,2},{67,3},{68,4},{69,5},{70,6},{71,7},{72,8},{73... | collective-permute-start | bytes 878600 | tf_op jit(solution)/shard_map/ppermute | solution.py:524
  101.7 2.2 %collective-permute-done.8.moved_ref = bf16[13,88,128]{2,1,0:T(8,128)(2,1)S(1)} collective-permute-done((bf16[13,88,128]{2,1,0:T(8,128)(2,1)S(1)}, bf16[13,88,128]{2,1,0:T(8,128)(2,1)S(1)}, u32[]{:S(2)}, u32[]{:S(2)}) %collective-permute-start.8) | collective-permute-done | bytes 292896 | tf_op jit(solution)/shard_map/ppermute | solution.py:524
  103.9 3.2 %unpack.1 = (f32[1,128]{1,0:T(1,128)}, f32[1,256]{1,0:T(1,128)}, f32[1,256]{1,0:T(1,128)}, f32[1,256,768]{2,1,0:T(8,128)}, f32[1,256,256]{2,1,0:T(8,128)}, /*ind...) custom-call(bf16[64,88,128]{2,1,0:T(8,128)(2,1)S(1)} %all_to_all.15.in_ref, ...), custom_call_target="tpu_custom_call" | custom-call | tf_op jit(solution)/shard_map/unpack/pallas_call | solution.py:525
  (12 shorter events, 0.2 us)
Async XLA Ops:
  0.6 21.3 %collective-permute-start.5 = (bf16[1,256,1024]{2,1,0:T(8,128)(2,1)}, bf16[1,256,1024]{2,1,0:T(8,128)(2,1)S(1)}, u32[]{:S(2)}, u32[]{:S(2)}) collective-permute-start(bf16[1,256,1024]{2,1,0:T(8,128)(2,1)} %up_own.1), channel_id=1, source_target_pairs={{0,64},{64,0},{1,65},{65,1},{2,66},{66,2},{3,67},{67,3},{4,68},{68... | collective-permute-start | bytes 1572872 | tf_op jit(solution)/shard_map/ppermute | solution.py:444
  0.7 21.2 %collective-permute-start.6 = (bf16[1,1024,256]{2,1,0:T(8,128)(2,1)}, bf16[1,1024,256]{2,1,0:T(8,128)(2,1)S(1)}, u32[]{:S(2)}, u32[]{:S(2)}) collective-permute-start(bf16[1,1024,256]{2,1,0:T(8,128)(2,1)} %down_own.1), channel_id=1, source_target_pairs={{0,64},{64,0},{1,65},{65,1},{2,66},{66,2},{3,67},{67,3},{4,68},{68... | collective-permute-start | bytes 1572872 | tf_op jit(solution)/shard_map/ppermute | solution.py:444
  1.2 20.7 %collective-permute-start.3 = (bf16[1,256,768]{2,1,0:T(8,128)(2,1)}, bf16[1,256,768]{2,1,0:T(8,128)(2,1)S(1)}, u32[]{:S(2)}, u32[]{:S(2)}) collective-permute-start(bf16[1,256,768]{2,1,0:T(8,128)(2,1)} %qkv_own.1), channel_id=1, source_target_pairs={{0,64},{64,0},{1,65},{65,1},{2,66},{66,2},{3,67},{67,3},{4,68},{68... | collective-permute-start | bytes 1179656 | tf_op jit(solution)/shard_map/ppermute | solution.py:444
  2.0 4.8 %collective-permute-start = (bf16[2,1,256]{2,1,0:T(2,128)(2,1)S(1)}, bf16[2,1,256]{2,1,0:T(2,128)(2,1)S(1)}, u32[]{:S(2)}, u32[]{:S(2)}) collective-permute-start(bf16[2,1,256]{2,1,0:T(2,128)(2,1)S(1)} %slice.12), channel_id=1, source_target_pairs={{0,1},{1,2},{2,3},{3,4},{4,5},{5,6},{6,7},{7,8},{8,9},{9,10},{10,1... | collective-permute-start | bytes 3080 | tf_op jit(solution)/shard_map/ppermute | solution.py:456
  8.7 13.2 %all-to-all-start = ((bf16[8,40,256]{2,1,0:T(8,128)(2,1)}), bf16[8,40,256]{2,1,0:T(8,128)(2,1)S(1)}, u32[]{:S(2)}, u32[]{:S(2)}) async-start(bf16[8,40,256]{2,1,0:T(8,128)(2,1)} %embed.1), calls=%async_computation | async-start | bytes 327680 | tf_op jit(solution)/shard_map/all_to_all | solution.py:475
  15.1 2.9 %collective-permute-start.4 = (bf16[1,256,256]{2,1,0:T(8,128)(2,1)}, bf16[1,256,256]{2,1,0:T(8,128)(2,1)S(1)}, u32[]{:S(2)}, u32[]{:S(2)}) collective-permute-start(bf16[1,256,256]{2,1,0:T(8,128)(2,1)} %out_own.1), channel_id=1, source_target_pairs={{0,64},{64,0},{1,65},{65,1},{2,66},{66,2},{3,67},{67,3},{4,68},{68... | collective-permute-start | bytes 393224 | tf_op jit(solution)/shard_map/ppermute | solution.py:444
  15.2 1.5 %collective-permute-start.1 = (f32[1,256]{1,0:T(1,128)}, f32[1,256]{1,0:T(1,128)S(1)}, u32[]{:S(2)}, u32[]{:S(2)}) collective-permute-start(f32[1,256]{1,0:T(1,128)} %gain_own_one_hbm.1), channel_id=1, source_target_pairs={{0,64},{64,0},{1,65},{65,1},{2,66},{66,2},{3,67},{67,3},{4,68},{68... | collective-permute-start | bytes 3080 | tf_op jit(solution)/shard_map/ppermute | solution.py:444
  16.7 1.4 %collective-permute-start.2 = (f32[1,256]{1,0:T(1,128)}, f32[1,256]{1,0:T(1,128)S(1)}, u32[]{:S(2)}, u32[]{:S(2)}) collective-permute-start(f32[1,256]{1,0:T(1,128)} %gain_own_two_hbm.1), channel_id=1, source_target_pairs={{0,64},{64,0},{1,65},{65,1},{2,66},{66,2},{3,67},{67,3},{4,68},{68... | collective-permute-start | bytes 3080 | tf_op jit(solution)/shard_map/ppermute | solution.py:444
  35.7 3.3 %collective-permute-start.7 = (bf16[64,88,128]{2,1,0:T(8,128)(2,1)S(1)}, bf16[64,88,128]{2,1,0:T(8,128)(2,1)S(1)}, u32[]{:S(2)}, u32[]{:S(2)}) collective-permute-start(bf16[64,88,128]{2,1,0:T(8,128)(2,1)S(1)} %get-tuple-element.19), channel_id=1, source_target_pairs={{0,64},{64,0},{1,65},{65,1},{2,66},{66,2},{3,67},{67,3},{4,68},{68... | collective-permute-start | bytes 4325384 | tf_op jit(solution)/shard_map/ppermute | solution.py:444
  40.5 32.7 %all-to-all-start.1 = ((bf16[64,88,128]{2,1,0:T(8,128)(2,1)}), bf16[64,88,128]{2,1,0:T(8,128)(2,1)S(1)}, u32[]{:S(2)}, u32[]{:S(2)}) async-start(bf16[64,88,128]{2,1,0:T(8,128)(2,1)} %add_convert_fusion), calls=%async_computation.1 | async-start | bytes 2883584 | tf_op jit(solution)/shard_map/all_to_all | solution.py:514
  100.4 3.5 %collective-permute-start.8 = (bf16[13,88,128]{2,1,0:T(8,128)(2,1)S(1)}, bf16[13,88,128]{2,1,0:T(8,128)(2,1)S(1)}, u32[]{:S(2)}, u32[]{:S(2)}) collective-permute-start(bf16[13,88,128]{2,1,0:T(8,128)(2,1)S(1)} %slice.17), channel_id=1, source_target_pairs={{64,0},{65,1},{66,2},{67,3},{68,4},{69,5},{70,6},{71,7},{72,8},{73... | collective-permute-start | bytes 878600 | tf_op jit(solution)/shard_map/ppermute | solution.py:524

commit v4 on v3

--- a/solution.py
+++ b/solution.py
@@ -7,6 +7,7 @@
 from jax.experimental import pallas as pl
 from jax.experimental.pallas import tpu as pltpu
 from jax.sharding import PartitionSpec as P
+
 
 H = 8
 WIN = 32
@@ -19,7 +20,7 @@
 CHUNK = 80
 CHUNK_PAD = 88
 SLAB = 16
-STAT_AT = 49
+STAT_AT = 25
 SEND_ROWS = 40
 BF = jnp.bfloat16
 F32 = jnp.float32
@@ -86,17 +87,15 @@
         out_ref[part, WIN:SEND_ROWS, :] = extra
 
 
-def group_max(values):
+def group_max(values, same_head):
+    lane = iota((1, 128), 1)
     halves = []
     for side in range(2):
         half = values[:, side * 128 : (side + 1) * 128]
-        lane = iota((1, 128), 1)
         for step in (1, 2, 4, 8, 16):
-            ahead = pltpu.roll(half, 128 - step, 1)
-            behind = pltpu.roll(half, step, 1)
-            half = jnp.maximum(half, jnp.where((lane & step) == 0, ahead, behind))
-        halves.append(half)
-    return jnp.concatenate(halves, axis=1)
+            half = jnp.maximum(half, pltpu.roll(half, step, 1))
+        halves.append(jnp.where(lane % WIN == WIN - 1, half, 0.0))
+    return group_sum(jnp.concatenate(halves, axis=1), same_head)
 
 
 def group_sum(values, same_head):
@@ -162,10 +161,14 @@
     lane_count = jnp.zeros((1, WIDTH), jnp.int32)
     for s in range(GROUP):
         lane_count = jnp.where(key // 4 == s, count_of[s], lane_count)
+    fills = ([], [])
     for w in range(GROUP):
         dilated = part * WIN + w * 4 + key % 4 < lane_count
         plain = part * WIN + key < count_of[w]
         mask_buf[0, w : w + 1, :] = jnp.where(dilated, 1.0, 0.0)
+        most = functools.reduce(jnp.maximum, count_of)
+        fills[0].append(jnp.where(part * WIN + w * 4 < most, -1e30, 0.0))
+        fills[1].append(jnp.where(part * WIN < count_of[w], -1e30, 0.0))
         mask_buf[1, w : w + 1, :] = jnp.where(plain, 1.0, 0.0)
 
     def expand(value):
@@ -226,9 +229,9 @@
         for w in range(GROUP):
             rows = slice(w * WIN, (w + 1) * WIN)
             scores = nt(packed_buf[k, 0, rows, :], expand(packed_buf[k, 1, rows, :]))
-            score_buf[rows, :] = jnp.where(mask_buf[k, w : w + 1, :] > 0.5, scores * HEAD**-0.5, -1e30)
+            score_buf[rows, :] = jnp.where(mask_buf[k, w : w + 1, :] > 0.5, scores * HEAD**-0.5, fills[k][w])
         scores = score_buf[...]
-        weights = jnp.exp(scores - group_max(scores))
+        weights = jnp.exp(scores - group_max(scores, same_head))
         prob = weights / group_sum(weights, same_head)
         prob_buf[k] = prob
         prob_low = prob.astype(BF)
@@ -270,11 +273,10 @@
     def backward(k, out_grad, slope, pulled):
         back = None
         down_lines = []
-        places = {0: 6, 1: 10, 2: 0, 3: 2} if k == 0 else {0: 0, 1: 2, 2: 4, 3: 6}
         for j in (2, 3, 0, 1):
             cols = slice(j * WIDTH, (j + 1) * WIDTH)
             if k == 0:
-                stream, place = (1, 12 + 2 * j) if j >= 2 else (0, 4 + 4 * j)
+                stream, place = (1, 12 + 2 * j) if j >= 2 else (0, 16 + 2 * j)
                 out_low = out_grad.astype(BF)
                 store_wide(stream, place, tn(hidden_buf[k, j], out_low))
                 hidden_grad = nt(out_low, w_down[k, cols, :]).astype(BF).astype(F32)
@@ -282,18 +284,19 @@
                 down_lines.append(jnp.sum(hidden_buf[k, j].astype(F32) * slope, axis=0, keepdims=True))
                 hidden_grad = slope * pulled[j]
             up_grad = (slope_buf[k, j] * hidden_grad).astype(BF)
-            store_wide(k, places[j], tn(normed_two_buf[k], up_grad))
+            store_wide(k, 2 * j, tn(normed_two_buf[k], up_grad))
             term = nt(up_grad, w_up[k, :, cols])
             back = term if back is None else back + term
             if k == 0 and j == 3:
                 send_out(1, 51, 64)
         if k == 0:
-            send_out(0, 0, 38)
+            send_out(0, 0, 25)
+            send_out(0, 52, 64)
         normed_two_grad = back.astype(BF).astype(F32)
         res_grad, gain_two_grad = norm_back(normed_two_grad, after_buf[k], inv_two[k], gain(k, 1))
         after_grad = out_grad + res_grad
         after_low = after_grad.astype(BF)
-        store_wide(k, 12 if k == 0 else 8, tn(mixed_buf[k], after_low))
+        store_wide(k, 8, tn(mixed_buf[k], after_low))
         mixed_grad = nt(after_low, w_out[k]).astype(BF)
         for w in range(GROUP):
             rows = slice(w * WIN, (w + 1) * WIN)
@@ -304,23 +307,29 @@
         flow = prob * prob_grad
         score_grad = (flow - prob * group_sum(flow, same_head)) * HEAD**-0.5
 
-        def fold(value):
-            total = None
-            for h in range(H):
-                piece = jnp.where(col_i[:WIN] // HEAD == h, window(value, h), 0.0)
-                total = piece if total is None else total + piece
-            return total
+        lane_head = iota((WIN, 128), 1) // HEAD
+
+        def fold(left, right):
+            halves = []
+            for side in range(2):
+                cols = slice(side * 128, (side + 1) * 128)
+                value = tn(left[:, cols], right[:, cols])
+                total = window(value, 3)
+                for h in range(3):
+                    total = jnp.where(lane_head == h, window(value, h), total)
+                halves.append(total.astype(BF))
+            return jnp.concatenate(halves, axis=1)
 
         for w in range(GROUP):
             rows = slice(w * WIN, (w + 1) * WIN)
             grad_w = jnp.where(mask_buf[k, w : w + 1, :] > 0.5, window(score_grad, w), 0.0).astype(BF)
             dpacked_buf[0, rows, :] = nn(grad_w, expand(packed_buf[k, 1, rows, :])).astype(BF)
-            dpacked_buf[1, rows, :] = fold(tn(grad_w, packed_buf[k, 0, rows, :])).astype(BF)
-            dpacked_buf[2, rows, :] = fold(tn(window(prob_low, w), window(mixed_grad, w))).astype(BF)
+            dpacked_buf[1, rows, :] = fold(grad_w, packed_buf[k, 0, rows, :])
+            dpacked_buf[2, rows, :] = fold(window(prob_low, w), window(mixed_grad, w))
         back = None
         for j in range(3):
             piece = dpacked_buf[j]
-            store_wide(k, (14 if k == 0 else 10) + 2 * j, tn(normed_buf[k], piece))
+            store_wide(k, 10 + 2 * j, tn(normed_buf[k], piece))
             term = nt(piece, w_qkv[k, :, j * WIDTH : (j + 1) * WIDTH])
             back = term if back is None else back + term
         normed_grad = back.astype(BF).astype(F32)
@@ -365,13 +374,22 @@
     unused, gain_one, gain_two, none = backward(0, exchange(middle_grad).astype(F32), None, None)
     del unused, none
     store_stats(0, [gain_one, gain_two, sdf_grad, loss_row])
-    send_out(0, 38, 64)
+    send_out(0, 25, 52)
     for store in stores:
         store.wait()
 
 
+def wide(source, first_chunk, place, ref, row, col, slabs=range(ROWS // SLAB)):
+    for side in range(2):
+        for i in slabs:
+            slab = (place + side) * (ROWS // SLAB) + i
+            low = slab % 5 * SLAB
+            piece = source[slab // 5 - first_chunk, low : low + SLAB, :].astype(F32)
+            ref[row + i * SLAB : row + (i + 1) * SLAB, col + side * 128 : col + (side + 1) * 128] = piece
+
+
 def unpack_kernel(
-    in_ref, moved_ref, sdf_row_ref, loss_ref, sdf_ref, gain_one_ref, qkv_hbm, out_hbm, gain_two_ref, up_hbm, down_hbm,
+    in_ref, sdf_row_ref, loss_ref, sdf_ref, gain_one_ref, qkv_hbm, out_hbm, gain_two_ref, up_hbm, down_hbm,
     qkv_ref, out_ref, up_ref, down_ref, store_sem,
 ):
     micro = lax.axis_index("pipe")
@@ -382,58 +400,53 @@
         copy.start()
         stores.append(copy)
 
-    def wide(source, first_chunk, place, target, base):
-        for side in range(2):
-            for i in range(ROWS // SLAB):
-                slab = (place + side) * (ROWS // SLAB) + i
-                low = slab % 5 * SLAB
-                piece = source[slab // 5 - first_chunk, low : low + SLAB, :].astype(F32)
-                target(i, side, piece, base)
-
-    def into(ref, base):
-        def put(i, side, piece, low):
-            ref[low + i * SLAB : low + (i + 1) * SLAB, base + side * 128 : base + (side + 1) * 128] = piece
-
-        return put
-
-    def section(up_at, out_at, qkv_at):
-        for j in range(4):
-            wide(in_ref, 0, up_at[j], into(up_ref, j * WIDTH), 0)
-        wide(in_ref, 0, out_at, into(out_ref, 0), 0)
-        for j in range(3):
-            wide(in_ref, 0, qkv_at + 2 * j, into(qkv_ref, j * WIDTH), 0)
-
+    for ref, target, place, count in ((up_ref, up_hbm, 0, 4), (out_ref, out_hbm, 8, 1), (qkv_ref, qkv_hbm, 10, 3)):
+        for quarter in range(4):
+            for j in range(count):
+                wide(in_ref, 0, place + 2 * j, ref, 0, j * WIDTH, range(4 * quarter, 4 * quarter + 4))
+            rows = pl.ds(quarter * 64, 64)
+            store(ref.at[rows], target.at[0, rows])
     lines = []
     for c in range(15):
         pair = in_ref[STAT_AT + c, CHUNK:CHUNK_PAD, :].astype(F32)
         lines.append(pair[0:1] + pair[1:2])
+    for ref, c in ((gain_one_ref, 0), (gain_two_ref, 2), (sdf_ref, 4)):
+        ref[0:1, 0:128] = lines[c]
+        ref[0:1, 128:256] = lines[c + 1]
+    loss_ref[0:1, :] = lines[6] / (2 * 12288)
 
     @pl.when(micro == 0)
     def _():
-        section((6, 10, 0, 2), 12, 14)
-        for j, place in ((0, 4), (1, 8)):
-            wide(in_ref, 0, place, into(down_ref, 0), j * WIDTH)
-        for j in (2, 3):
-            wide(moved_ref, 51, 12 + 2 * j, into(down_ref, 0), j * WIDTH)
+        for j in range(2):
+            wide(in_ref, 0, 16 + 2 * j, down_ref, j * WIDTH, 0)
 
     @pl.when(micro == 1)
     def _():
-        section((0, 2, 4, 6), 8, 10)
         diagonal = iota((128, 128), 0) == iota((128, 128), 1)
         for c in range(8):
             column = jnp.sum(jnp.where(diagonal, lines[7 + c], 0.0), axis=1, keepdims=True)
             down_ref[c * 128 : (c + 1) * 128, :] = column * sdf_row_ref[...]
 
-    store(qkv_ref, qkv_hbm.at[0])
-    store(out_ref, out_hbm.at[0])
-    store(up_ref, up_hbm.at[0])
-    store(down_ref, down_hbm.at[0])
-    for ref, c in ((gain_one_ref, 0), (gain_two_ref, 2), (sdf_ref, 4)):
-        ref[0:1, 0:128] = lines[c]
-        ref[0:1, 128:256] = lines[c + 1]
-    loss_ref[0:1, :] = lines[6] / (2 * 12288)
+    for quarter in range(4):
+        rows = pl.ds(quarter * WIDTH, WIDTH)
+        store(down_ref.at[rows], down_hbm.at[0, rows])
     for copy in stores:
         copy.wait()
+
+
+def finish_kernel(moved_hbm, down_in, down_out, moved_ref, half_ref, sem):
+    del down_in
+
+    @pl.when(lax.axis_index("pipe") == 0)
+    def _():
+        load = pltpu.make_async_copy(moved_hbm, moved_ref, sem.at[0])
+        load.start()
+        load.wait()
+        for j in range(2):
+            wide(moved_ref, 51, 16 + 2 * j, half_ref, j * WIDTH, 0)
+        store = pltpu.make_async_copy(half_ref, down_out.at[0, pl.ds(2 * WIDTH, 2 * WIDTH)], sem.at[1])
+        store.start()
+        store.wait()
 
 
 def fix(value):
@@ -454,8 +467,11 @@
 ):
     rank_count = lax.axis_size("tok")
     rim = lax.ppermute(coarse[:, -1:, :], "tok", [(i, i + 1) for i in range(rank_count - 1)])
-    gains_far = [swap_pipe(g) for g in (gain_attn, gain_mlp)]
-    qkv_far, out_far, up_far, down_far = (swap_pipe(w) for w in (w_qkv, w_out, w_up, w_down))
+    arrived = []
+    for value in (gain_attn, gain_mlp, w_qkv, w_out, w_up, w_down):
+        arrived.append(swap_pipe(value))
+    gains_far = arrived[:2]
+    qkv_far, out_far, up_far, down_far = arrived[2:]
     outgoing = pl.pallas_call(
         embed_kernel,
         out_shape=jax.ShapeDtypeStruct((GROUP, SEND_ROWS, WIDTH), BF),
@@ -504,7 +520,7 @@
             pltpu.VMEM((1, WIDTH), F32),
             pltpu.SMEM((2, 64), jnp.int32),
             pltpu.SemaphoreType.DMA((12,)),
-            pltpu.SemaphoreType.DMA((4,)),
+            pltpu.SemaphoreType.DMA((5,)),
         ],
         name="step",
         compiler_params=pltpu.CompilerParams(vmem_limit_bytes=32 * 2**20),
@@ -534,18 +550,32 @@
             jax.ShapeDtypeStruct((1, WIDTH, FF), F32),
             jax.ShapeDtypeStruct((1, FF, WIDTH), F32),
         ),
-        in_specs=[VMEM, VMEM, VMEM],
+        in_specs=[VMEM, VMEM],
         out_specs=(VMEM, VMEM, VMEM, HBM, HBM, VMEM, HBM, HBM),
         scratch_shapes=[
             pltpu.VMEM((WIDTH, 3 * WIDTH), F32),
             pltpu.VMEM((WIDTH, WIDTH), F32),
             pltpu.VMEM((WIDTH, FF), F32),
             pltpu.VMEM((FF, WIDTH), F32),
-            pltpu.SemaphoreType.DMA((7,)),
+            pltpu.SemaphoreType.DMA((16,)),
         ],
         name="unpack",
         compiler_params=pltpu.CompilerParams(vmem_limit_bytes=16 * 2**20),
-    )(gathered, moved, fix(w_sdf[None]))
+    )(gathered, fix(w_sdf[None]))
+    down = pl.pallas_call(
+        finish_kernel,
+        out_shape=jax.ShapeDtypeStruct((1, FF, WIDTH), F32),
+        in_specs=[ANY, HBM],
+        out_specs=HBM,
+        scratch_shapes=[
+            pltpu.VMEM((13, CHUNK_PAD, 128), BF),
+            pltpu.VMEM((2 * WIDTH, WIDTH), F32),
+            pltpu.SemaphoreType.DMA((2,)),
+        ],
+        input_output_aliases={1: 0},
+        name="finish",
+        compiler_params=pltpu.CompilerParams(vmem_limit_bytes=16 * 2**20),
+    )(moved, down)
     return loss[0, 0], sdf[0], gain_one, qkv, out, gain_two, up, down
 
 

time: 109 us -> 107 us (0.982)
  waiting for transfers between devices: 36.1 us -> 33.9 us
    ppermute x1, waiting for transfers between devices: 2.17 us -> 0.01 us  [shards(): moved = lax.ppermute(gathered[51:64], 'pipe', [(1, 0)])]
  transfers between devices with their start and end apart: 11 -> 11, of which waited for: 7 -> 6; matrix products, arithmetic and copies ran while one was open for 1% -> 1% of each run, Pallas kernels for 2% -> 5%
where the time goes in v4:
time: 107 us; the launch traced here: 105 us
  waiting for transfers between devices  33.9 us (32%)
  blocking collectives  26.6 us (25%)
  starting transfers between devices  22.2 us (21%)
  Pallas kernels  19 us (18%)
  other arithmetic  1.87 us (2%)
    all_to_all x1, blocking collectives, shards(): lax.all_to_all(jnp.broadcast_to(summed[None], (rank_count, CHUNK_PAD, 128...  26.6 us
    all_to_all x1, waiting for transfers between devices, shards(): shares = lax.all_to_all(total, 'tok', 0, 0, tiled=True)  23.5 us
    pallas_call x1, Pallas kernels, shards(): pl.pallas_call(step_kernel, out_shape=(packet, packet), in_specs=[HBM] +...  13.2 us
    all_to_all x1, starting transfers between devices, shards(): shares = lax.all_to_all(total, 'tok', 0, 0, tiled=True)  9.24 us
    all_to_all x1, starting transfers between devices, shards(): lax.all_to_all(outgoing, 'tok', 0, 0, axis_index_groups=groups, tiled=True)  6.45 us
    ppermute x7, waiting for transfers between devices, swap_pipe(): return lax.ppermute(value, 'pipe', [(0, 1), (1, 0)])  5.32 us
    all_to_all x1, waiting for transfers between devices, shards(): lax.all_to_all(outgoing, 'tok', 0, 0, axis_index_groups=groups, tiled=True)  3.82 us
    ppermute x1, starting transfers between devices, shards(): lax.ppermute(coarse[:, -1:, :], 'tok', [(i, i + 1) for i in range(rank_co...  3.49 us
  transfers between devices with their start and end apart: 11, of which 6 were waited for; matrix products, arithmetic and copies ran while one was open for 1% of the time, Pallas kernels for 5%

profile of v4, /device:TPU:0, one launch (start us, length us, event | category | flops | bytes accessed | tf_op | source)
XLA Modules:
  0.0 105.5 jit_solution(475233621749381495)
XLA Ops:
  0.7 0.5 collective-permute-start.6
  1.3 0.7 slice.12
  2.0 3.5 %collective-permute-start = (bf16[2,1,256]{2,1,0:T(2,128)(2,1)S(1)}, bf16[2,1,256]{2,1,0:T(2,128)(2,1)S(1)}, u32[]{:S(2)}, u32[]{:S(2)}) collective-permute-start(bf16[2,1,256]{2,1,0:T(2,128)(2,1)S(1)} %slice.12), channel_id=1, source_target_pairs={{0,1},{1,2},{2,3},{3,4},{4,5},{5,6},{6,7},{7,8},{8,9},{9,10},{10,1... | collective-permute-start | bytes 3080 | tf_op jit(solution)/shard_map/ppermute | solution.py:469
  5.5 1.3 %collective-permute-done.rim_ref = bf16[2,1,256]{2,1,0:T(2,128)(2,1)S(1)} collective-permute-done((bf16[2,1,256]{2,1,0:T(2,128)(2,1)S(1)}, bf16[2,1,256]{2,1,0:T(2,128)(2,1)S(1)}, u32[]{:S(2)}, u32[]{:S(2)}) %collective-permute-start) | collective-permute-done | bytes 1056 | tf_op jit(solution)/shard_map/ppermute | solution.py:469
  6.8 1.9 %embed.1 = bf16[8,40,256]{2,1,0:T(8,128)(2,1)} custom-call(bf16[2,256,256]{2,1,0:T(8,128)(2,1)} %features_hbm.1, bf16[2,64,256]{2,1,0:T(8,128)(2,1)} %coarse_hbm.1, bf16[2,1,256]{2,1,0:T(2,128)(2,1)S(1)} %collective-permute-done.rim_ref, s32[2,256]{1,0:T(2,128)} %parent_hbm.1, f32[2,256]{1,0:T(2,128)} %target_hbm.1), custom_call_target="tpu_custom_call" | custom-call | tf_op jit(solution)/shard_map/embed/pallas_call | solution.py:475
  8.7 6.5 %all-to-all-start = ((bf16[8,40,256]{2,1,0:T(8,128)(2,1)}), bf16[8,40,256]{2,1,0:T(8,128)(2,1)S(1)}, u32[]{:S(2)}, u32[]{:S(2)}) async-start(bf16[8,40,256]{2,1,0:T(8,128)(2,1)} %embed.1), calls=%async_computation | async-start | bytes 327680 | tf_op jit(solution)/shard_map/all_to_all | solution.py:491
  15.2 0.5 collective-permute-start.1
  15.7 1.0 collective-permute-done.1.gain_far_one
  16.7 0.3 collective-permute-start.2
  17.0 1.0 collective-permute-done.2.gain_far_two
  18.1 3.8 %all-to-all-done.received_ref = bf16[8,40,256]{2,1,0:T(8,128)(2,1)S(1)} async-done(((bf16[8,40,256]{2,1,0:T(8,128)(2,1)}), bf16[8,40,256]{2,1,0:T(8,128)(2,1)S(1)}, u32[]{:S(2)}, u32[]{:S(2)}) %all-to-all-start) | async-done | bytes 163872 | tf_op jit(solution)/shard_map/all_to_all | solution.py:491
  21.9 13.2 %step.1 = (bf16[64,88,128]{2,1,0:T(8,128)(2,1)S(1)}, bf16[64,88,128]{2,1,0:T(8,128)(2,1)S(1)}) custom-call(s32[2,64]{1,0:T(2,128)} %counts_hbm.1, bf16[8,40,256]{2,1,0:T(8,128)(2,1)S(1)} %all-to-all-done.received_ref, f32[1,256]{1,0:T(1,128)S(1)} %collective-permute-done.1.gain_far_one, f32[1,256]{1,0:T(1,128)S(1)} %collective-permute-done.2.gain_far_two, ...), custom_call_target="tpu_custom_call" | custom-call | tf_op jit(solution)/shard_map/step/pallas_call | solution.py:493
  35.1 0.3 collective-permute-start.7
  35.4 3.2 %collective-permute-done.7 = bf16[64,88,128]{2,1,0:T(8,128)(2,1)S(1)} collective-permute-done((bf16[64,88,128]{2,1,0:T(8,128)(2,1)S(1)}, bf16[64,88,128]{2,1,0:T(8,128)(2,1)S(1)}, u32[]{:S(2)}, u32[]{:S(2)}) %collective-permute-start.7) | collective-permute-done | bytes 1441824 | tf_op jit(solution)/shard_map/ppermute | solution.py:457
  38.6 1.5 %add_convert_fusion = bf16[64,88,128]{2,1,0:T(8,128)(2,1)} fusion(bf16[64,88,128]{2,1,0:T(8,128)(2,1)S(1)} %collective-permute-done.7, bf16[64,88,128]{2,1,0:T(8,128)(2,1)S(1)} %get-tuple-element.18), kind=kLoop, calls=%fused_computation.1 | loop fusion | flops 2883584 | bytes 4325376 | tf_op jit(solution)/shard_map/convert_element_type | solution.py:529
  40.1 9.2 %all-to-all-start.1 = ((bf16[64,88,128]{2,1,0:T(8,128)(2,1)}), bf16[64,88,128]{2,1,0:T(8,128)(2,1)S(1)}, u32[]{:S(2)}, u32[]{:S(2)}) async-start(bf16[64,88,128]{2,1,0:T(8,128)(2,1)} %add_convert_fusion), calls=%async_computation.1 | async-start | bytes 2883584 | tf_op jit(solution)/shard_map/all_to_all | solution.py:530
  49.4 23.5 %all-to-all-done.1 = bf16[64,88,128]{2,1,0:T(8,128)(2,1)S(1)} async-done(((bf16[64,88,128]{2,1,0:T(8,128)(2,1)}), bf16[64,88,128]{2,1,0:T(8,128)(2,1)S(1)}, u32[]{:S(2)}, u32[]{:S(2)}) %all-to-all-start.1) | async-done | bytes 1441824 | tf_op jit(solution)/shard_map/all_to_all | solution.py:530
  72.8 0.2 convert_reduce_fusion
  73.1 0.1 select_convert_fusion
  73.2 0.2 broadcast_in_dim.35
  73.4 26.6 %all_to_all.15.in_ref = bf16[64,88,128]{2,1,0:T(8,128)(2,1)S(1)} all-to-all(bf16[64,88,128]{2,1,0:T(8,128)(2,1)S(1)} %broadcast_in_dim.35), channel_id=1, replica_groups=mesh['pipe'=2,'tok'=64] {'tok'}, dimensions={0} | all-to-all | bytes 2883584 | tf_op jit(solution)/shard_map/all_to_all | solution.py:537
  100.0 1.3 %collective-permute-start.8 = (bf16[13,88,128]{2,1,0:T(8,128)(2,1)S(1)}, bf16[13,88,128]{2,1,0:T(8,128)(2,1)S(1)}, u32[]{:S(2)}, u32[]{:S(2)}) collective-permute-start(bf16[13,88,128]{2,1,0:T(8,128)(2,1)S(1)} %slice.17), channel_id=1, source_target_pairs={{64,0},{65,1},{66,2},{67,3},{68,4},{69,5},{70,6},{71,7},{72,8},{73... | collective-permute-start | bytes 878600 | tf_op jit(solution)/shard_map/ppermute | solution.py:540
  101.3 3.1 %unpack.1 = (f32[1,128]{1,0:T(1,128)}, f32[1,256]{1,0:T(1,128)}, f32[1,256]{1,0:T(1,128)}, f32[1,256,768]{2,1,0:T(8,128)}, f32[1,256,256]{2,1,0:T(8,128)}, /*ind...) custom-call(bf16[64,88,128]{2,1,0:T(8,128)(2,1)S(1)} %all_to_all.15.in_ref, f32[1,256]{1,0:T(1,128)} %bitcast.5), custom_call_target="tpu_custom_call" | custom-call | tf_op jit(solution)/shard_map/unpack/pallas_call | solution.py:541
  104.4 0.9 finish.1
  (13 shorter events, 0.3 us)
Async XLA Ops:
  0.6 21.3 %collective-permute-start.5 = (bf16[1,256,1024]{2,1,0:T(8,128)(2,1)}, bf16[1,256,1024]{2,1,0:T(8,128)(2,1)S(1)}, u32[]{:S(2)}, u32[]{:S(2)}) collective-permute-start(bf16[1,256,1024]{2,1,0:T(8,128)(2,1)} %up_own.1), channel_id=1, source_target_pairs={{0,64},{64,0},{1,65},{65,1},{2,66},{66,2},{3,67},{67,3},{4,68},{68... | collective-permute-start | bytes 1572872 | tf_op jit(solution)/shard_map/ppermute | solution.py:457
  0.7 21.2 %collective-permute-start.6 = (bf16[1,1024,256]{2,1,0:T(8,128)(2,1)}, bf16[1,1024,256]{2,1,0:T(8,128)(2,1)S(1)}, u32[]{:S(2)}, u32[]{:S(2)}) collective-permute-start(bf16[1,1024,256]{2,1,0:T(8,128)(2,1)} %down_own.1), channel_id=1, source_target_pairs={{0,64},{64,0},{1,65},{65,1},{2,66},{66,2},{3,67},{67,3},{4,68},{68... | collective-permute-start | bytes 1572872 | tf_op jit(solution)/shard_map/ppermute | solution.py:457
  1.2 20.7 %collective-permute-start.3 = (bf16[1,256,768]{2,1,0:T(8,128)(2,1)}, bf16[1,256,768]{2,1,0:T(8,128)(2,1)S(1)}, u32[]{:S(2)}, u32[]{:S(2)}) collective-permute-start(bf16[1,256,768]{2,1,0:T(8,128)(2,1)} %qkv_own.1), channel_id=1, source_target_pairs={{0,64},{64,0},{1,65},{65,1},{2,66},{66,2},{3,67},{67,3},{4,68},{68... | collective-permute-start | bytes 1179656 | tf_op jit(solution)/shard_map/ppermute | solution.py:457
  2.0 4.8 %collective-permute-start = (bf16[2,1,256]{2,1,0:T(2,128)(2,1)S(1)}, bf16[2,1,256]{2,1,0:T(2,128)(2,1)S(1)}, u32[]{:S(2)}, u32[]{:S(2)}) collective-permute-start(bf16[2,1,256]{2,1,0:T(2,128)(2,1)S(1)} %slice.12), channel_id=1, source_target_pairs={{0,1},{1,2},{2,3},{3,4},{4,5},{5,6},{6,7},{7,8},{8,9},{9,10},{10,1... | collective-permute-start | bytes 3080 | tf_op jit(solution)/shard_map/ppermute | solution.py:469
  8.7 13.2 %all-to-all-start = ((bf16[8,40,256]{2,1,0:T(8,128)(2,1)}), bf16[8,40,256]{2,1,0:T(8,128)(2,1)S(1)}, u32[]{:S(2)}, u32[]{:S(2)}) async-start(bf16[8,40,256]{2,1,0:T(8,128)(2,1)} %embed.1), calls=%async_computation | async-start | bytes 327680 | tf_op jit(solution)/shard_map/all_to_all | solution.py:491
  15.1 2.9 %collective-permute-start.4 = (bf16[1,256,256]{2,1,0:T(8,128)(2,1)}, bf16[1,256,256]{2,1,0:T(8,128)(2,1)S(1)}, u32[]{:S(2)}, u32[]{:S(2)}) collective-permute-start(bf16[1,256,256]{2,1,0:T(8,128)(2,1)} %out_own.1), channel_id=1, source_target_pairs={{0,64},{64,0},{1,65},{65,1},{2,66},{66,2},{3,67},{67,3},{4,68},{68... | collective-permute-start | bytes 393224 | tf_op jit(solution)/shard_map/ppermute | solution.py:457
  15.2 1.5 %collective-permute-start.1 = (f32[1,256]{1,0:T(1,128)}, f32[1,256]{1,0:T(1,128)S(1)}, u32[]{:S(2)}, u32[]{:S(2)}) collective-permute-start(f32[1,256]{1,0:T(1,128)} %gain_own_one_hbm.1), channel_id=1, source_target_pairs={{0,64},{64,0},{1,65},{65,1},{2,66},{66,2},{3,67},{67,3},{4,68},{68... | collective-permute-start | bytes 3080 | tf_op jit(solution)/shard_map/ppermute | solution.py:457
  16.7 1.4 %collective-permute-start.2 = (f32[1,256]{1,0:T(1,128)}, f32[1,256]{1,0:T(1,128)S(1)}, u32[]{:S(2)}, u32[]{:S(2)}) collective-permute-start(f32[1,256]{1,0:T(1,128)} %gain_own_two_hbm.1), channel_id=1, source_target_pairs={{0,64},{64,0},{1,65},{65,1},{2,66},{66,2},{3,67},{67,3},{4,68},{68... | collective-permute-start | bytes 3080 | tf_op jit(solution)/shard_map/ppermute | solution.py:457
  35.1 3.5 %collective-permute-start.7 = (bf16[64,88,128]{2,1,0:T(8,128)(2,1)S(1)}, bf16[64,88,128]{2,1,0:T(8,128)(2,1)S(1)}, u32[]{:S(2)}, u32[]{:S(2)}) collective-permute-start(bf16[64,88,128]{2,1,0:T(8,128)(2,1)S(1)} %get-tuple-element.19), channel_id=1, source_target_pairs={{0,64},{64,0},{1,65},{65,1},{2,66},{66,2},{3,67},{67,3},{4,68},{68... | collective-permute-start | bytes 4325384 | tf_op jit(solution)/shard_map/ppermute | solution.py:457
  40.1 32.7 %all-to-all-start.1 = ((bf16[64,88,128]{2,1,0:T(8,128)(2,1)}), bf16[64,88,128]{2,1,0:T(8,128)(2,1)S(1)}, u32[]{:S(2)}, u32[]{:S(2)}) async-start(bf16[64,88,128]{2,1,0:T(8,128)(2,1)} %add_convert_fusion), calls=%async_computation.1 | async-start | bytes 2883584 | tf_op jit(solution)/shard_map/all_to_all | solution.py:530
  100.0 4.4 %collective-permute-start.8 = (bf16[13,88,128]{2,1,0:T(8,128)(2,1)S(1)}, bf16[13,88,128]{2,1,0:T(8,128)(2,1)S(1)}, u32[]{:S(2)}, u32[]{:S(2)}) collective-permute-start(bf16[13,88,128]{2,1,0:T(8,128)(2,1)S(1)} %slice.17), channel_id=1, source_target_pairs={{64,0},{65,1},{66,2},{67,3},{68,4},{69,5},{70,6},{71,7},{72,8},{73... | collective-permute-start | bytes 878600 | tf_op jit(solution)/shard_map/ppermute | solution.py:540

commit v5 on v4

--- a/solution.py
+++ b/solution.py
@@ -49,7 +49,7 @@
 
 
 def embed_kernel(
-    features_hbm, coarse_hbm, rim_ref, parent_hbm, target_hbm, out_ref,
+    features_hbm, coarse_hbm, parent_hbm, target_hbm, out_ref, rim_hot_ref,
     features_ref, coarse_ref, parent_ref, target_ref, load_sem,
 ):
     micro = lax.axis_index("pipe")
@@ -71,10 +71,8 @@
         load.wait()
     local = parent_ref[pl.ds(micro, 1), :] - shard * 64
     own_hot = jnp.where(iota((64, ROWS), 0) == local, 1.0, 0.0).astype(BF)
-    rim_hot = jnp.where((iota((16, ROWS), 0) == 0) & (local == -1), 1.0, 0.0).astype(BF)
-    rim = jnp.broadcast_to(rim_ref[micro], (16, WIDTH))
-    lifted = tn(own_hot, coarse_ref[...]) + tn(rim_hot, rim)
-    embedded = (features_ref[...].astype(F32) + lifted).astype(BF)
+    rim_hot_ref[...] = jnp.where((iota((16, ROWS), 0) == 0) & (local == -1), 1.0, 0.0).astype(BF)
+    embedded = (features_ref[...].astype(F32) + tn(own_hot, coarse_ref[...])).astype(BF)
     target = jnp.broadcast_to(target_ref[pl.ds(micro, 1), :], (8, ROWS))
     high = target.astype(BF).astype(F32)
     middle = (target - high).astype(BF).astype(F32)
@@ -85,6 +83,15 @@
     for part in range(GROUP):
         out_ref[part, 0:WIN, :] = embedded[part * WIN : (part + 1) * WIN]
         out_ref[part, WIN:SEND_ROWS, :] = extra
+
+
+def rim_kernel(embedded_ref, rim_hot_ref, rim_ref, out_ref):
+    rim = jnp.broadcast_to(rim_ref[lax.axis_index("pipe")], (16, WIDTH))
+    lifted = tn(rim_hot_ref[...], rim)
+    for part in range(GROUP):
+        rows = slice(part * WIN, (part + 1) * WIN)
+        out_ref[part, 0:WIN, :] = (embedded_ref[part, 0:WIN, :].astype(F32) + lifted[rows]).astype(BF)
+        out_ref[part, WIN:SEND_ROWS, :] = embedded_ref[part, WIN:SEND_ROWS, :]
 
 
 def group_max(values, same_head):
@@ -400,12 +407,6 @@
         copy.start()
         stores.append(copy)
 
-    for ref, target, place, count in ((up_ref, up_hbm, 0, 4), (out_ref, out_hbm, 8, 1), (qkv_ref, qkv_hbm, 10, 3)):
-        for quarter in range(4):
-            for j in range(count):
-                wide(in_ref, 0, place + 2 * j, ref, 0, j * WIDTH, range(4 * quarter, 4 * quarter + 4))
-            rows = pl.ds(quarter * 64, 64)
-            store(ref.at[rows], target.at[0, rows])
     lines = []
     for c in range(15):
         pair = in_ref[STAT_AT + c, CHUNK:CHUNK_PAD, :].astype(F32)
@@ -427,9 +428,17 @@
             column = jnp.sum(jnp.where(diagonal, lines[7 + c], 0.0), axis=1, keepdims=True)
             down_ref[c * 128 : (c + 1) * 128, :] = column * sdf_row_ref[...]
 
-    for quarter in range(4):
-        rows = pl.ds(quarter * WIDTH, WIDTH)
-        store(down_ref.at[rows], down_hbm.at[0, rows])
+    store(down_ref.at[pl.ds(0, 2 * WIDTH)], down_hbm.at[0, pl.ds(0, 2 * WIDTH)])
+    rows = pl.ds(2 * WIDTH, 2 * WIDTH)
+    last = pltpu.make_async_copy(down_ref.at[rows], down_hbm.at[0, rows], store_sem.at[13])
+    pl.when(micro == 1)(last.start)
+    for ref, target, place, count in ((up_ref, up_hbm, 0, 4), (out_ref, out_hbm, 8, 1), (qkv_ref, qkv_hbm, 10, 3)):
+        for quarter in range(4):
+            for j in range(count):
+                wide(in_ref, 0, place + 2 * j, ref, 0, j * WIDTH, range(4 * quarter, 4 * quarter + 4))
+            rows = pl.ds(quarter * 64, 64)
+            store(ref.at[rows], target.at[0, rows])
+    pl.when(micro == 1)(last.wait)
     for copy in stores:
         copy.wait()
 
@@ -472,11 +481,14 @@
         arrived.append(swap_pipe(value))
     gains_far = arrived[:2]
     qkv_far, out_far, up_far, down_far = arrived[2:]
-    outgoing = pl.pallas_call(
+    embedded, rim_hot = pl.pallas_call(
         embed_kernel,
-        out_shape=jax.ShapeDtypeStruct((GROUP, SEND_ROWS, WIDTH), BF),
-        in_specs=[HBM, HBM, VMEM, HBM, HBM],
-        out_specs=VMEM,
+        out_shape=(
+            jax.ShapeDtypeStruct((GROUP, SEND_ROWS, WIDTH), BF),
+            jax.ShapeDtypeStruct((16, ROWS), BF),
+        ),
+        in_specs=[HBM] * 4,
+        out_specs=(VMEM, VMEM),
         scratch_shapes=[
             pltpu.VMEM((ROWS, WIDTH), BF),
             pltpu.VMEM((64, WIDTH), BF),
@@ -486,7 +498,15 @@
         ],
         name="embed",
         compiler_params=pltpu.CompilerParams(vmem_limit_bytes=4 * 2**20),
-    )(fix(features), fix(coarse), rim, fix(parent), fix(target))
+    )(fix(features), fix(coarse), fix(parent), fix(target))
+    outgoing = pl.pallas_call(
+        rim_kernel,
+        out_shape=jax.ShapeDtypeStruct((GROUP, SEND_ROWS, WIDTH), BF),
+        in_specs=[VMEM] * 3,
+        out_specs=VMEM,
+        name="add_rim",
+        compiler_params=pltpu.CompilerParams(vmem_limit_bytes=4 * 2**20),
+    )(embedded, rim_hot, rim)
     groups = [[b * GROUP + i for i in range(GROUP)] for b in range(rank_count // GROUP)]
     received = lax.all_to_all(outgoing, "tok", 0, 0, axis_index_groups=groups, tiled=True)
     packet = jax.ShapeDtypeStruct((64, CHUNK_PAD, 128), BF)
@@ -557,7 +577,7 @@
             pltpu.VMEM((WIDTH, WIDTH), F32),
             pltpu.VMEM((WIDTH, FF), F32),
             pltpu.VMEM((FF, WIDTH), F32),
-            pltpu.SemaphoreType.DMA((16,)),
+            pltpu.SemaphoreType.DMA((14,)),
         ],
         name="unpack",
         compiler_params=pltpu.CompilerParams(vmem_limit_bytes=16 * 2**20),

time: 107 us -> 106 us (level)
  waiting for transfers between devices: 33.9 us -> 32.7 us
    ppermute x1, waiting for transfers between devices: 1.29 us -> 0.1 us  [shards(): lax.ppermute(coarse[:, -1:, :], 'tok', [(i, i + 1) for i in range(rank_co...]
where the time goes in v5:
time: 106 us; the launch traced here: 104 us
  waiting for transfers between devices  32.7 us (31%)
  blocking collectives  26.6 us (25%)
  starting transfers between devices  22.2 us (21%)
  Pallas kernels  19.1 us (18%)
  other arithmetic  1.86 us (2%)
    all_to_all x1, blocking collectives, shards(): lax.all_to_all(jnp.broadcast_to(summed[None], (rank_count, CHUNK_PAD, 128...  26.6 us
    all_to_all x1, waiting for transfers between devices, shards(): shares = lax.all_to_all(total, 'tok', 0, 0, tiled=True)  23.5 us
    pallas_call x1, Pallas kernels, shards(): pl.pallas_call(step_kernel, out_shape=(packet, packet), in_specs=[HBM] +...  13.2 us
    all_to_all x1, starting transfers between devices, shards(): shares = lax.all_to_all(total, 'tok', 0, 0, tiled=True)  9.23 us
    all_to_all x1, starting transfers between devices, shards(): lax.all_to_all(outgoing, 'tok', 0, 0, axis_index_groups=groups, tiled=True)  6.44 us
    ppermute x7, waiting for transfers between devices, swap_pipe(): return lax.ppermute(value, 'pipe', [(0, 1), (1, 0)])  5.32 us
    all_to_all x1, waiting for transfers between devices, shards(): lax.all_to_all(outgoing, 'tok', 0, 0, axis_index_groups=groups, tiled=True)  3.82 us
    ppermute x1, starting transfers between devices, shards(): lax.ppermute(coarse[:, -1:, :], 'tok', [(i, i + 1) for i in range(rank_co...  3.49 us
  transfers between devices with their start and end apart: 11, of which 6 were waited for; matrix products, arithmetic and copies ran while one was open for 1% of the time, Pallas kernels for 5%

profile of v5, /device:TPU:0, one launch (start us, length us, event | category | flops | bytes accessed | tf_op | source)
XLA Modules:
  0.0 104.3 jit_solution(1551928366508747083)
XLA Ops:
  0.7 0.5 collective-permute-start.6
  1.3 0.7 slice.12
  2.0 3.5 %collective-permute-start = (bf16[2,1,256]{2,1,0:T(2,128)(2,1)S(1)}, bf16[2,1,256]{2,1,0:T(2,128)(2,1)S(1)}, u32[]{:S(2)}, u32[]{:S(2)}) collective-permute-start(bf16[2,1,256]{2,1,0:T(2,128)(2,1)S(1)} %slice.12), channel_id=1, source_target_pairs={{0,1},{1,2},{2,3},{3,4},{4,5},{5,6},{6,7},{7,8},{8,9},{9,10},{10,1... | collective-permute-start | bytes 3080 | tf_op jit(solution)/shard_map/ppermute | solution.py:478
  5.5 1.2 %embed.1 = (bf16[8,40,256]{2,1,0:T(8,128)(2,1)S(1)}, bf16[16,256]{1,0:T(8,128)(2,1)S(1)}) custom-call(bf16[2,256,256]{2,1,0:T(8,128)(2,1)} %features_hbm.1, bf16[2,64,256]{2,1,0:T(8,128)(2,1)} %coarse_hbm.1, s32[2,256]{1,0:T(2,128)} %parent_hbm.1, f32[2,256]{1,0:T(2,128)} %target_hbm.1), custom_call_target="tpu_custom_call" | custom-call | tf_op jit(solution)/shard_map/embed/pallas_call | solution.py:484
  6.7 0.1 collective-permute-done.rim_ref
  6.8 0.9 add_rim.1
  7.7 6.4 %all-to-all-start = ((bf16[8,40,256]{2,1,0:T(8,128)(2,1)}), bf16[8,40,256]{2,1,0:T(8,128)(2,1)S(1)}, u32[]{:S(2)}, u32[]{:S(2)}) async-start(bf16[8,40,256]{2,1,0:T(8,128)(2,1)} %add_rim.1), calls=%async_computation | async-start | bytes 327680 | tf_op jit(solution)/shard_map/all_to_all | solution.py:511
  14.2 0.5 collective-permute-start.1
  14.7 1.0 %collective-permute-done.1.gain_far_one = f32[1,256]{1,0:T(1,128)S(1)} collective-permute-done((f32[1,256]{1,0:T(1,128)}, f32[1,256]{1,0:T(1,128)S(1)}, u32[]{:S(2)}, u32[]{:S(2)}) %collective-permute-start.1) | collective-permute-done | bytes 1056 | tf_op jit(solution)/shard_map/ppermute | solution.py:466
  15.7 0.3 collective-permute-start.2
  16.0 1.0 %collective-permute-done.2.gain_far_two = f32[1,256]{1,0:T(1,128)S(1)} collective-permute-done((f32[1,256]{1,0:T(1,128)}, f32[1,256]{1,0:T(1,128)S(1)}, u32[]{:S(2)}, u32[]{:S(2)}) %collective-permute-start.2) | collective-permute-done | bytes 1056 | tf_op jit(solution)/shard_map/ppermute | solution.py:466
  17.1 3.8 %all-to-all-done.received_ref = bf16[8,40,256]{2,1,0:T(8,128)(2,1)S(1)} async-done(((bf16[8,40,256]{2,1,0:T(8,128)(2,1)}), bf16[8,40,256]{2,1,0:T(8,128)(2,1)S(1)}, u32[]{:S(2)}, u32[]{:S(2)}) %all-to-all-start) | async-done | bytes 163872 | tf_op jit(solution)/shard_map/all_to_all | solution.py:511
  20.9 13.2 %step.1 = (bf16[64,88,128]{2,1,0:T(8,128)(2,1)S(1)}, bf16[64,88,128]{2,1,0:T(8,128)(2,1)S(1)}) custom-call(s32[2,64]{1,0:T(2,128)} %counts_hbm.1, bf16[8,40,256]{2,1,0:T(8,128)(2,1)S(1)} %all-to-all-done.received_ref, f32[1,256]{1,0:T(1,128)S(1)} %collective-permute-done.1.gain_far_one, f32[1,256]{1,0:T(1,128)S(1)} %collective-permute-done.2.gain_far_two, ...), custom_call_target="tpu_custom_call" | custom-call | tf_op jit(solution)/shard_map/step/pallas_call | solution.py:513
  34.1 0.3 collective-permute-start.7
  34.4 3.2 %collective-permute-done.7 = bf16[64,88,128]{2,1,0:T(8,128)(2,1)S(1)} collective-permute-done((bf16[64,88,128]{2,1,0:T(8,128)(2,1)S(1)}, bf16[64,88,128]{2,1,0:T(8,128)(2,1)S(1)}, u32[]{:S(2)}, u32[]{:S(2)}) %collective-permute-start.7) | collective-permute-done | bytes 1441824 | tf_op jit(solution)/shard_map/ppermute | solution.py:466
  37.6 1.5 %add_convert_fusion = bf16[64,88,128]{2,1,0:T(8,128)(2,1)} fusion(bf16[64,88,128]{2,1,0:T(8,128)(2,1)S(1)} %collective-permute-done.7, bf16[64,88,128]{2,1,0:T(8,128)(2,1)S(1)} %get-tuple-element.22), kind=kLoop, calls=%fused_computation.1 | loop fusion | flops 2883584 | bytes 4325376 | tf_op jit(solution)/shard_map/convert_element_type | solution.py:549
  39.1 9.2 %all-to-all-start.1 = ((bf16[64,88,128]{2,1,0:T(8,128)(2,1)}), bf16[64,88,128]{2,1,0:T(8,128)(2,1)S(1)}, u32[]{:S(2)}, u32[]{:S(2)}) async-start(bf16[64,88,128]{2,1,0:T(8,128)(2,1)} %add_convert_fusion), calls=%async_computation.1 | async-start | bytes 2883584 | tf_op jit(solution)/shard_map/all_to_all | solution.py:550
  48.3 23.5 %all-to-all-done.1 = bf16[64,88,128]{2,1,0:T(8,128)(2,1)S(1)} async-done(((bf16[64,88,128]{2,1,0:T(8,128)(2,1)}), bf16[64,88,128]{2,1,0:T(8,128)(2,1)S(1)}, u32[]{:S(2)}, u32[]{:S(2)}) %all-to-all-start.1) | async-done | bytes 1441824 | tf_op jit(solution)/shard_map/all_to_all | solution.py:550
  71.8 0.2 convert_reduce_fusion
  72.2 0.2 broadcast_in_dim.35
  72.4 26.6 %all_to_all.15.in_ref = bf16[64,88,128]{2,1,0:T(8,128)(2,1)S(1)} all-to-all(bf16[64,88,128]{2,1,0:T(8,128)(2,1)S(1)} %broadcast_in_dim.35), channel_id=1, replica_groups=mesh['pipe'=2,'tok'=64] {'tok'}, dimensions={0} | all-to-all | bytes 2883584 | tf_op jit(solution)/shard_map/all_to_all | solution.py:557
  99.0 1.3 %collective-permute-start.8 = (bf16[13,88,128]{2,1,0:T(8,128)(2,1)S(1)}, bf16[13,88,128]{2,1,0:T(8,128)(2,1)S(1)}, u32[]{:S(2)}, u32[]{:S(2)}) collective-permute-start(bf16[13,88,128]{2,1,0:T(8,128)(2,1)S(1)} %slice.17), channel_id=1, source_target_pairs={{64,0},{65,1},{66,2},{67,3},{68,4},{69,5},{70,6},{71,7},{72,8},{73... | collective-permute-start | bytes 878600 | tf_op jit(solution)/shard_map/ppermute | solution.py:560
  100.3 2.9 %unpack.1 = (f32[1,128]{1,0:T(1,128)}, f32[1,256]{1,0:T(1,128)}, f32[1,256]{1,0:T(1,128)}, f32[1,256,768]{2,1,0:T(8,128)}, f32[1,256,256]{2,1,0:T(8,128)}, /*ind...) custom-call(bf16[64,88,128]{2,1,0:T(8,128)(2,1)S(1)} %all_to_all.15.in_ref, f32[1,256]{1,0:T(1,128)} %bitcast.5), custom_call_target="tpu_custom_call" | custom-call | tf_op jit(solution)/shard_map/unpack/pallas_call | solution.py:561
  103.2 0.9 finish.1
  (14 shorter events, 0.4 us)
Async XLA Ops:
  0.6 20.3 %collective-permute-start.5 = (bf16[1,256,1024]{2,1,0:T(8,128)(2,1)}, bf16[1,256,1024]{2,1,0:T(8,128)(2,1)S(1)}, u32[]{:S(2)}, u32[]{:S(2)}) collective-permute-start(bf16[1,256,1024]{2,1,0:T(8,128)(2,1)} %up_own.1), channel_id=1, source_target_pairs={{0,64},{64,0},{1,65},{65,1},{2,66},{66,2},{3,67},{67,3},{4,68},{68... | collective-permute-start | bytes 1572872 | tf_op jit(solution)/shard_map/ppermute | solution.py:466
  0.7 20.2 %collective-permute-start.6 = (bf16[1,1024,256]{2,1,0:T(8,128)(2,1)}, bf16[1,1024,256]{2,1,0:T(8,128)(2,1)S(1)}, u32[]{:S(2)}, u32[]{:S(2)}) collective-permute-start(bf16[1,1024,256]{2,1,0:T(8,128)(2,1)} %down_own.1), channel_id=1, source_target_pairs={{0,64},{64,0},{1,65},{65,1},{2,66},{66,2},{3,67},{67,3},{4,68},{68... | collective-permute-start | bytes 1572872 | tf_op jit(solution)/shard_map/ppermute | solution.py:466
  1.2 19.7 %collective-permute-start.3 = (bf16[1,256,768]{2,1,0:T(8,128)(2,1)}, bf16[1,256,768]{2,1,0:T(8,128)(2,1)S(1)}, u32[]{:S(2)}, u32[]{:S(2)}) collective-permute-start(bf16[1,256,768]{2,1,0:T(8,128)(2,1)} %qkv_own.1), channel_id=1, source_target_pairs={{0,64},{64,0},{1,65},{65,1},{2,66},{66,2},{3,67},{67,3},{4,68},{68... | collective-permute-start | bytes 1179656 | tf_op jit(solution)/shard_map/ppermute | solution.py:466
  2.0 4.8 %collective-permute-start = (bf16[2,1,256]{2,1,0:T(2,128)(2,1)S(1)}, bf16[2,1,256]{2,1,0:T(2,128)(2,1)S(1)}, u32[]{:S(2)}, u32[]{:S(2)}) collective-permute-start(bf16[2,1,256]{2,1,0:T(2,128)(2,1)S(1)} %slice.12), channel_id=1, source_target_pairs={{0,1},{1,2},{2,3},{3,4},{4,5},{5,6},{6,7},{7,8},{8,9},{9,10},{10,1... | collective-permute-start | bytes 3080 | tf_op jit(solution)/shard_map/ppermute | solution.py:478
  7.7 13.2 %all-to-all-start = ((bf16[8,40,256]{2,1,0:T(8,128)(2,1)}), bf16[8,40,256]{2,1,0:T(8,128)(2,1)S(1)}, u32[]{:S(2)}, u32[]{:S(2)}) async-start(bf16[8,40,256]{2,1,0:T(8,128)(2,1)} %add_rim.1), calls=%async_computation | async-start | bytes 327680 | tf_op jit(solution)/shard_map/all_to_all | solution.py:511
  14.1 2.9 %collective-permute-start.4 = (bf16[1,256,256]{2,1,0:T(8,128)(2,1)}, bf16[1,256,256]{2,1,0:T(8,128)(2,1)S(1)}, u32[]{:S(2)}, u32[]{:S(2)}) collective-permute-start(bf16[1,256,256]{2,1,0:T(8,128)(2,1)} %out_own.1), channel_id=1, source_target_pairs={{0,64},{64,0},{1,65},{65,1},{2,66},{66,2},{3,67},{67,3},{4,68},{68... | collective-permute-start | bytes 393224 | tf_op jit(solution)/shard_map/ppermute | solution.py:466
  14.2 1.5 %collective-permute-start.1 = (f32[1,256]{1,0:T(1,128)}, f32[1,256]{1,0:T(1,128)S(1)}, u32[]{:S(2)}, u32[]{:S(2)}) collective-permute-start(f32[1,256]{1,0:T(1,128)} %gain_own_one_hbm.1), channel_id=1, source_target_pairs={{0,64},{64,0},{1,65},{65,1},{2,66},{66,2},{3,67},{67,3},{4,68},{68... | collective-permute-start | bytes 3080 | tf_op jit(solution)/shard_map/ppermute | solution.py:466
  15.7 1.4 %collective-permute-start.2 = (f32[1,256]{1,0:T(1,128)}, f32[1,256]{1,0:T(1,128)S(1)}, u32[]{:S(2)}, u32[]{:S(2)}) collective-permute-start(f32[1,256]{1,0:T(1,128)} %gain_own_two_hbm.1), channel_id=1, source_target_pairs={{0,64},{64,0},{1,65},{65,1},{2,66},{66,2},{3,67},{67,3},{4,68},{68... | collective-permute-start | bytes 3080 | tf_op jit(solution)/shard_map/ppermute | solution.py:466
  34.1 3.5 %collective-permute-start.7 = (bf16[64,88,128]{2,1,0:T(8,128)(2,1)S(1)}, bf16[64,88,128]{2,1,0:T(8,128)(2,1)S(1)}, u32[]{:S(2)}, u32[]{:S(2)}) collective-permute-start(bf16[64,88,128]{2,1,0:T(8,128)(2,1)S(1)} %get-tuple-element.23), channel_id=1, source_target_pairs={{0,64},{64,0},{1,65},{65,1},{2,66},{66,2},{3,67},{67,3},{4,68},{68... | collective-permute-start | bytes 4325384 | tf_op jit(solution)/shard_map/ppermute | solution.py:466
  39.1 32.7 %all-to-all-start.1 = ((bf16[64,88,128]{2,1,0:T(8,128)(2,1)}), bf16[64,88,128]{2,1,0:T(8,128)(2,1)S(1)}, u32[]{:S(2)}, u32[]{:S(2)}) async-start(bf16[64,88,128]{2,1,0:T(8,128)(2,1)} %add_convert_fusion), calls=%async_computation.1 | async-start | bytes 2883584 | tf_op jit(solution)/shard_map/all_to_all | solution.py:550
  99.0 4.2 %collective-permute-start.8 = (bf16[13,88,128]{2,1,0:T(8,128)(2,1)S(1)}, bf16[13,88,128]{2,1,0:T(8,128)(2,1)S(1)}, u32[]{:S(2)}, u32[]{:S(2)}) collective-permute-start(bf16[13,88,128]{2,1,0:T(8,128)(2,1)S(1)} %slice.17), channel_id=1, source_target_pairs={{64,0},{65,1},{66,2},{67,3},{68,4},{69,5},{70,6},{71,7},{72,8},{73... | collective-permute-start | bytes 878600 | tf_op jit(solution)/shard_map/ppermute | solution.py:560

commit v6 on v5

--- a/solution.py
+++ b/solution.py
@@ -110,48 +110,70 @@
     return nn(high, same_head) + nn(low, same_head)
 
 
-def step_kernel(
-    counts_hbm, received_ref, gain_far_one, gain_far_two, sdf_hbm, gain_own_one_hbm, gain_own_two_hbm,
+def arrange_kernel(
+    gain_far_one, gain_far_two, counts_hbm, sdf_hbm, gain_own_one_hbm, gain_own_two_hbm,
     qkv_own, qkv_far, out_own, out_far, up_own, up_far, down_own, down_far,
-    keep_ref, send_ref,
-    w_qkv, w_out, w_up, w_down,
-    x_buf, inv_one, normed_buf, packed_buf, prob_buf, mixed_buf, after_buf, inv_two,
-    normed_two_buf, slope_buf, hidden_buf, mask_buf, grads, score_buf, dpacked_buf,
-    sdf_ref, gain_own_one, gain_own_two, counts_ref, load_sem, store_sem,
+    w_qkv, w_out, w_up, w_down, mask_ref, fill_ref, rows_ref,
+    sdf_ref, gain_own_one, gain_own_two, counts_ref, load_sem,
 ):
     micro = lax.axis_index("pipe")
     shard = lax.axis_index("tok")
     part = lax.rem(shard, GROUP)
     first = shard - part
-    loads = []
-    for number, (own, far, held) in enumerate(
-        ((qkv_own, qkv_far, w_qkv), (out_own, out_far, w_out), (up_own, up_far, w_up), (down_own, down_far, w_down))
+    moves = [
+        (sdf_hbm, sdf_ref),
+        (gain_own_one_hbm, gain_own_one),
+        (gain_own_two_hbm, gain_own_two),
+        (counts_hbm, counts_ref),
+    ]
+    for own, far, held in (
+        (qkv_own, qkv_far, w_qkv), (out_own, out_far, w_out), (up_own, up_far, w_up), (down_own, down_far, w_down)
     ):
-        loads.append(pltpu.make_async_copy(own.at[0], held.at[micro], load_sem.at[2 * number]))
-        loads.append(pltpu.make_async_copy(far.at[0], held.at[1 - micro], load_sem.at[2 * number + 1]))
-    small = [
-        pltpu.make_async_copy(source, held, load_sem.at[8 + number])
-        for number, (source, held) in enumerate(
-            (
-                (sdf_hbm, sdf_ref),
-                (gain_own_one_hbm, gain_own_one),
-                (gain_own_two_hbm, gain_own_two),
-                (counts_hbm, counts_ref),
-            )
-        )
+        moves += [(own.at[0], held.at[micro]), (far.at[0], held.at[1 - micro])]
+    loads = [
+        pltpu.make_async_copy(source, held, load_sem.at[number]) for number, (source, held) in enumerate(moves)
     ]
-    for load in small + loads:
+    for load in loads:
         load.start()
-    for load in small:
+    for load in loads[:4]:
         load.wait()
-
     own_is_first = micro == 0
+    row = iota((8, WIDTH), 0)
+    rows = jnp.where(row == 4, sdf_ref[...], 0.0)
+    for which, (own, far) in enumerate(((gain_own_one, gain_far_one), (gain_own_two, gain_far_two))):
+        rows = jnp.where(row == which, jnp.where(own_is_first, own[...], far[...]), rows)
+        rows = jnp.where(row == 2 + which, jnp.where(own_is_first, far[...], own[...]), rows)
+    rows_ref[...] = rows
+    key = iota((1, WIDTH), 1) % WIN
+    count_of = [counts_ref[micro, first + s] for s in range(GROUP)]
+    most = functools.reduce(jnp.maximum, count_of)
+    lane_count = jnp.zeros((1, WIDTH), jnp.int32)
+    for s in range(GROUP):
+        lane_count = jnp.where(key // 4 == s, count_of[s], lane_count)
+    for w in range(GROUP):
+        dilated = part * WIN + w * 4 + key % 4 < lane_count
+        plain = part * WIN + key < count_of[w]
+        mask_ref[0, w : w + 1, :] = jnp.where(dilated, 1.0, 0.0)
+        mask_ref[1, w : w + 1, :] = jnp.where(plain, 1.0, 0.0)
+        blank = jnp.zeros((1, WIDTH), F32)
+        fill_ref[0, w : w + 1, :] = jnp.where(part * WIN + w * 4 < most, blank - 1e30, blank)
+        fill_ref[1, w : w + 1, :] = jnp.where(part * WIN < count_of[w], blank - 1e30, blank)
+    for load in loads[4:]:
+        load.wait()
+
+
+def step_kernel(
+    received_ref, w_qkv, w_out, w_up, w_down, mask_buf, fill_buf, rows_ref,
+    keep_ref, send_ref,
+    x_buf, inv_one, normed_buf, packed_buf, prob_buf, mixed_buf, after_buf, inv_two,
+    normed_two_buf, slope_buf, hidden_buf, grads, score_buf, dpacked_buf, store_sem,
+):
+    micro = lax.axis_index("pipe")
+    part = lax.rem(lax.axis_index("tok"), GROUP)
 
     def gain(section, which):
-        own = (gain_own_one, gain_own_two)[which][...]
-        far = (gain_far_one, gain_far_two)[which][...]
-        mine = own_is_first if section == 0 else jnp.logical_not(own_is_first)
-        return jnp.where(mine, own, far)
+        number = 2 * section + which
+        return rows_ref[number : number + 1, :]
 
     row_i = iota((ROWS, WIDTH), 0)
     col_i = iota((ROWS, WIDTH), 1)
@@ -161,22 +183,6 @@
 
     def exchange(value):
         return nn(swap, value).astype(BF)
-
-    lane = iota((1, WIDTH), 1)
-    key = lane % WIN
-    count_of = [counts_ref[micro, first + s] for s in range(GROUP)]
-    lane_count = jnp.zeros((1, WIDTH), jnp.int32)
-    for s in range(GROUP):
-        lane_count = jnp.where(key // 4 == s, count_of[s], lane_count)
-    fills = ([], [])
-    for w in range(GROUP):
-        dilated = part * WIN + w * 4 + key % 4 < lane_count
-        plain = part * WIN + key < count_of[w]
-        mask_buf[0, w : w + 1, :] = jnp.where(dilated, 1.0, 0.0)
-        most = functools.reduce(jnp.maximum, count_of)
-        fills[0].append(jnp.where(part * WIN + w * 4 < most, -1e30, 0.0))
-        fills[1].append(jnp.where(part * WIN < count_of[w], -1e30, 0.0))
-        mask_buf[1, w : w + 1, :] = jnp.where(plain, 1.0, 0.0)
 
     def expand(value):
         return jnp.concatenate([value] * H, axis=0) * same_head
@@ -228,15 +234,12 @@
         inv_one[k] = inv
         normed = (x * inv * gain(k, 0)).astype(BF)
         normed_buf[k] = normed
-        if k == 0:
-            loads[0].wait()
-            loads[1].wait()
         for j in range(3):
             packed_buf[k, j] = nn(normed, w_qkv[k, :, j * WIDTH : (j + 1) * WIDTH]).astype(BF)
         for w in range(GROUP):
             rows = slice(w * WIN, (w + 1) * WIN)
             scores = nt(packed_buf[k, 0, rows, :], expand(packed_buf[k, 1, rows, :]))
-            score_buf[rows, :] = jnp.where(mask_buf[k, w : w + 1, :] > 0.5, scores * HEAD**-0.5, fills[k][w])
+            score_buf[rows, :] = jnp.where(mask_buf[k, w : w + 1, :] > 0.5, scores * HEAD**-0.5, fill_buf[k, w : w + 1, :])
         scores = score_buf[...]
         weights = jnp.exp(scores - group_max(scores, same_head))
         prob = weights / group_sum(weights, same_head)
@@ -245,18 +248,12 @@
         for w in range(GROUP):
             rows = slice(w * WIN, (w + 1) * WIN)
             mixed_buf[k, rows, :] = nn(window(prob_low, w), expand(packed_buf[k, 2, rows, :])).astype(BF)
-        if k == 0:
-            loads[2].wait()
-            loads[3].wait()
         after = x + nn(mixed_buf[k], w_out[k])
         after_buf[k] = after
         inv = lax.rsqrt(jnp.mean(after * after, axis=-1, keepdims=True) + EPS)
         inv_two[k] = inv
         normed_two = (after * inv * gain(k, 1)).astype(BF)
         normed_two_buf[k] = normed_two
-        if k == 0:
-            for load in loads[4:]:
-                load.wait()
         total = after
         for j in range(4):
             cols = slice(j * WIDTH, (j + 1) * WIDTH)
@@ -357,10 +354,12 @@
         line = parts[0:1] + parts[1:2] + parts[2:3]
         chosen = jnp.where(lane_w == part * WIN + row_w, line, 0.0)
         pieces.append(jnp.sum(chosen, axis=-1, keepdims=True))
-        valid_pieces.append(part * WIN + iota((WIN, 1), 0) < count_of[s])
+        valid_pieces.append(
+            jnp.sum(jnp.where(lane_w == row_w, mask_buf[1, s : s + 1, :], 0.0), axis=-1, keepdims=True)
+        )
     target = jnp.concatenate(pieces, axis=0)
-    valid = jnp.concatenate([jnp.where(v, 1.0, 0.0) for v in valid_pieces], axis=0)
-    sdf = sdf_ref[...]
+    valid = jnp.concatenate(valid_pieces, axis=0)
+    sdf = rows_ref[4:5, :]
     predicted = jnp.sum(section_one * sdf, axis=-1, keepdims=True)
     residue = jnp.where(valid > 0.5, predicted - target, 0.0)
     slope = 2.0 * residue / math.sqrt(3 * ROWS * 64 // 4)
@@ -510,16 +509,38 @@
     groups = [[b * GROUP + i for i in range(GROUP)] for b in range(rank_count // GROUP)]
     received = lax.all_to_all(outgoing, "tok", 0, 0, axis_index_groups=groups, tiled=True)
     packet = jax.ShapeDtypeStruct((64, CHUNK_PAD, 128), BF)
+    arranged = pl.pallas_call(
+        arrange_kernel,
+        out_shape=(
+            jax.ShapeDtypeStruct((2, WIDTH, 3 * WIDTH), BF),
+            jax.ShapeDtypeStruct((2, WIDTH, WIDTH), BF),
+            jax.ShapeDtypeStruct((2, WIDTH, FF), BF),
+            jax.ShapeDtypeStruct((2, FF, WIDTH), BF),
+            jax.ShapeDtypeStruct((2, GROUP, WIDTH), F32),
+            jax.ShapeDtypeStruct((2, GROUP, WIDTH), F32),
+            jax.ShapeDtypeStruct((8, WIDTH), F32),
+        ),
+        in_specs=[VMEM] * 2 + [HBM] * 4 + [HBM] * 8,
+        out_specs=(VMEM,) * 7,
+        scratch_shapes=[
+            pltpu.VMEM((1, WIDTH), F32),
+            pltpu.VMEM((1, WIDTH), F32),
+            pltpu.VMEM((1, WIDTH), F32),
+            pltpu.SMEM((2, 64), jnp.int32),
+            pltpu.SemaphoreType.DMA((12,)),
+        ],
+        name="arrange",
+        compiler_params=pltpu.CompilerParams(vmem_limit_bytes=8 * 2**20),
+    )(
+        *gains_far, fix(counts), fix(w_sdf[None]), fix(gain_attn), fix(gain_mlp),
+        fix(w_qkv), fix(qkv_far), fix(w_out), fix(out_far), fix(w_up), fix(up_far), fix(w_down), fix(down_far),
+    )
     keep, send = pl.pallas_call(
         step_kernel,
         out_shape=(packet, packet),
-        in_specs=[HBM] + [VMEM] * 3 + [HBM] * 3 + [HBM, ANY] * 4,
+        in_specs=[VMEM] * 8,
         out_specs=(ANY, ANY),
         scratch_shapes=[
-            pltpu.VMEM((2, WIDTH, 3 * WIDTH), BF),
-            pltpu.VMEM((2, WIDTH, WIDTH), BF),
-            pltpu.VMEM((2, WIDTH, FF), BF),
-            pltpu.VMEM((2, FF, WIDTH), BF),
             pltpu.VMEM((2, ROWS, WIDTH), BF),
             pltpu.VMEM((2, ROWS, 1), F32),
             pltpu.VMEM((2, ROWS, WIDTH), BF),
@@ -531,20 +552,14 @@
             pltpu.VMEM((2, ROWS, WIDTH), BF),
             pltpu.VMEM((2, 4, ROWS, WIDTH), F32),
             pltpu.VMEM((2, 4, ROWS, WIDTH), BF),
-            pltpu.VMEM((2, GROUP, WIDTH), F32),
             pltpu.VMEM((2, 64, CHUNK_PAD, 128), BF),
             pltpu.VMEM((ROWS, WIDTH), F32),
             pltpu.VMEM((3, ROWS, WIDTH), BF),
-            pltpu.VMEM((1, WIDTH), F32),
-            pltpu.VMEM((1, WIDTH), F32),
-            pltpu.VMEM((1, WIDTH), F32),
-            pltpu.SMEM((2, 64), jnp.int32),
-            pltpu.SemaphoreType.DMA((12,)),
             pltpu.SemaphoreType.DMA((5,)),
         ],
         name="step",
-        compiler_params=pltpu.CompilerParams(vmem_limit_bytes=32 * 2**20),
-    )(fix(counts), received, *gains_far, fix(w_sdf[None]), fix(gain_attn), fix(gain_mlp), fix(w_qkv), qkv_far, fix(w_out), out_far, fix(w_up), up_far, fix(w_down), down_far)
+        compiler_params=pltpu.CompilerParams(vmem_limit_bytes=20 * 2**20),
+    )(received, *arranged)
     far = swap_pipe(send)
     total = (keep.astype(F32) + far.astype(F32)).astype(BF)
     shares = lax.all_to_all(total, "tok", 0, 0, tiled=True)

time: 106 us -> 108 us (1.019)
  waiting for transfers between devices: 32.7 us -> 28.9 us
  starting transfers between devices: 22.2 us -> 24.7 us
  local copies, waits for them, and re-layouts: 0.91 us -> 2.63 us
    all_to_all x1, waiting for transfers between devices: 3.82 us -> 0.07 us  [shards(): lax.all_to_all(outgoing, 'tok', 0, 0, axis_index_groups=groups, tiled=True)]
    all_to_all x1, starting transfers between devices: 9.23 us -> 11.5 us  [shards(): shares = lax.all_to_all(total, 'tok', 0, 0, tiled=True)]
    unnamed x0 -> x8, local copies, waits for them, and re-layouts: none -> 1.72 us
    pallas_call x1 -> x2, Pallas kernels: 13.2 us -> 13.9 us  [the longest x1 11.9 us: shards(): pl.pallas_call(step_kernel, out_shape=(packet, packet), in_specs=[VMEM] *...]
  transfers between devices with their start and end apart: 11 -> 11, of which waited for: 6 -> 6; matrix products, arithmetic and copies ran while one was open for 1% -> 1% of each run, Pallas kernels for 5% -> 7%
where the time goes in v6:
time: 108 us; the launch traced here: 106 us
  waiting for transfers between devices  28.9 us (27%)
  blocking collectives  26.9 us (25%)
  starting transfers between devices  24.7 us (23%)
  Pallas kernels  19.8 us (18%)
  local copies, waits for them, and re-layouts  2.63 us (2%)
  other arithmetic  1.85 us (2%)
    all_to_all x1, blocking collectives, shards(): lax.all_to_all(jnp.broadcast_to(summed[None], (rank_count, CHUNK_PAD, 128...  26.9 us
    all_to_all x1, waiting for transfers between devices, shards(): shares = lax.all_to_all(total, 'tok', 0, 0, tiled=True)  23.7 us
    pallas_call x1, Pallas kernels, shards(): pl.pallas_call(step_kernel, out_shape=(packet, packet), in_specs=[VMEM] *...  11.9 us
    all_to_all x1, starting transfers between devices, shards(): shares = lax.all_to_all(total, 'tok', 0, 0, tiled=True)  11.5 us
    all_to_all x1, starting transfers between devices, shards(): lax.all_to_all(outgoing, 'tok', 0, 0, axis_index_groups=groups, tiled=True)  6.44 us
    ppermute x7, waiting for transfers between devices, swap_pipe(): return lax.ppermute(value, 'pipe', [(0, 1), (1, 0)])  5.07 us
    ppermute x1, starting transfers between devices, shards(): lax.ppermute(coarse[:, -1:, :], 'tok', [(i, i + 1) for i in range(rank_co...  3.49 us
    pallas_call x1, Pallas kernels, shards(): pl.pallas_call(unpack_kernel, out_shape=(jax.ShapeDtypeStruct((1, 128), F...  2.9 us
  transfers between devices with their start and end apart: 11, of which 6 were waited for; matrix products, arithmetic and copies ran while one was open for 1% of the time, Pallas kernels for 7%

profile of v6, /device:TPU:0, one launch (start us, length us, event | category | flops | bytes accessed | tf_op | source)
XLA Modules:
  0.0 105.7 jit_solution(7588559921659512515)
XLA Ops:
  0.7 0.5 collective-permute-start.6
  1.3 0.7 slice.12
  2.0 3.5 %collective-permute-start = (bf16[2,1,256]{2,1,0:T(2,128)(2,1)S(1)}, bf16[2,1,256]{2,1,0:T(2,128)(2,1)S(1)}, u32[]{:S(2)}, u32[]{:S(2)}) collective-permute-start(bf16[2,1,256]{2,1,0:T(2,128)(2,1)S(1)} %slice.12), channel_id=1, source_target_pairs={{0,1},{1,2},{2,3},{3,4},{4,5},{5,6},{6,7},{7,8},{8,9},{9,10},{10,1... | collective-permute-start | bytes 3080 | tf_op jit(solution)/shard_map/ppermute | solution.py:477
  5.5 1.2 %embed.1 = (bf16[8,40,256]{2,1,0:T(8,128)(2,1)S(1)}, bf16[16,256]{1,0:T(8,128)(2,1)S(1)}) custom-call(bf16[2,256,256]{2,1,0:T(8,128)(2,1)} %features_hbm.1, bf16[2,64,256]{2,1,0:T(8,128)(2,1)} %coarse_hbm.1, s32[2,256]{1,0:T(2,128)} %parent_hbm.1, f32[2,256]{1,0:T(2,128)} %target_hbm.1), custom_call_target="tpu_custom_call" | custom-call | tf_op jit(solution)/shard_map/embed/pallas_call | solution.py:483
  6.8 0.9 add_rim.1
  7.7 6.4 %all-to-all-start = ((bf16[8,40,256]{2,1,0:T(8,128)(2,1)}), bf16[8,40,256]{2,1,0:T(8,128)(2,1)S(1)}, u32[]{:S(2)}, u32[]{:S(2)}) async-start(bf16[8,40,256]{2,1,0:T(8,128)(2,1)} %add_rim.1), calls=%async_computation | async-start | bytes 327680 | tf_op jit(solution)/shard_map/all_to_all | solution.py:510
  14.2 0.5 collective-permute-start.1
  14.7 1.0 collective-permute-done.1.gain_far_one
  15.7 0.3 collective-permute-start.2
  16.0 1.0 collective-permute-done.2.gain_far_two
  17.1 0.7 copy-done.2
  18.1 0.8 copy-done.1
  18.8 2.0 %arrange.1 = (bf16[2,256,768]{2,1,0:T(8,128)(2,1)S(1)}, bf16[2,256,256]{2,1,0:T(8,128)(2,1)S(1)}, bf16[2,256,1024]{2,1,0:T(8,128)(2,1)S(1)}, bf16[2,1024,256]{2,...) custom-call(f32[1,256]{1,0:T(1,128)S(1)} %collective-permute-done.1.gain_far_one, ...), custom_call_target="tpu_custom_call" | custom-call | tf_op jit(solution)/shard_map/arrange/pallas_call | solution.py:512
  20.9 11.9 %step.1 = (bf16[64,88,128]{2,1,0:T(8,128)(2,1)S(1)}, bf16[64,88,128]{2,1,0:T(8,128)(2,1)S(1)}) custom-call(bf16[8,40,256]{2,1,0:T(8,128)(2,1)S(1)} %all-to-all-done.received_ref, bf16[2,256,768]{2,1,0:T(8,128)(2,1)S(1)} %get-tuple-element.29.w_qkv, bf16[2,256,256]{2,1,0:T(8,128)(2,1)S(1)} %get-tuple-element.30.w_out, ...), custom_call_target="tpu_custom_call" | custom-call | tf_op jit(solution)/shard_map/step/pallas_call | solution.py:538
  32.8 0.5 collective-permute-start.7
  33.3 3.0 %collective-permute-done.7 = bf16[64,88,128]{2,1,0:T(8,128)(2,1)S(1)} collective-permute-done((bf16[64,88,128]{2,1,0:T(8,128)(2,1)S(1)}, bf16[64,88,128]{2,1,0:T(8,128)(2,1)S(1)}, u32[]{:S(2)}, u32[]{:S(2)}) %collective-permute-start.7) | collective-permute-done | bytes 1441824 | tf_op jit(solution)/shard_map/ppermute | solution.py:465
  36.3 1.5 %add_convert_fusion = bf16[64,88,128]{2,1,0:T(8,128)(2,1)} fusion(bf16[64,88,128]{2,1,0:T(8,128)(2,1)S(1)} %collective-permute-done.7, bf16[64,88,128]{2,1,0:T(8,128)(2,1)S(1)} %get-tuple-element.36), kind=kLoop, calls=%fused_computation.1 | loop fusion | flops 2883584 | bytes 4325376 | tf_op jit(solution)/shard_map/convert_element_type | solution.py:564
  37.8 11.5 %all-to-all-start.1 = ((bf16[64,88,128]{2,1,0:T(8,128)(2,1)}), bf16[64,88,128]{2,1,0:T(8,128)(2,1)S(1)}, u32[]{:S(2)}, u32[]{:S(2)}) async-start(bf16[64,88,128]{2,1,0:T(8,128)(2,1)} %add_convert_fusion), calls=%async_computation.1 | async-start | bytes 2883584 | tf_op jit(solution)/shard_map/all_to_all | solution.py:565
  49.3 23.7 %all-to-all-done.1 = bf16[64,88,128]{2,1,0:T(8,128)(2,1)S(1)} async-done(((bf16[64,88,128]{2,1,0:T(8,128)(2,1)}), bf16[64,88,128]{2,1,0:T(8,128)(2,1)S(1)}, u32[]{:S(2)}, u32[]{:S(2)}) %all-to-all-start.1) | async-done | bytes 1441824 | tf_op jit(solution)/shard_map/all_to_all | solution.py:565
  73.0 0.2 convert_reduce_fusion
  73.5 26.9 %all_to_all.15.in_ref = bf16[64,88,128]{2,1,0:T(8,128)(2,1)S(1)} all-to-all(bf16[64,88,128]{2,1,0:T(8,128)(2,1)S(1)} %broadcast_in_dim.35), channel_id=1, replica_groups=mesh['pipe'=2,'tok'=64] {'tok'}, dimensions={0} | all-to-all | bytes 2883584 | tf_op jit(solution)/shard_map/all_to_all | solution.py:572
  100.4 1.3 %collective-permute-start.8 = (bf16[13,88,128]{2,1,0:T(8,128)(2,1)S(1)}, bf16[13,88,128]{2,1,0:T(8,128)(2,1)S(1)}, u32[]{:S(2)}, u32[]{:S(2)}) collective-permute-start(bf16[13,88,128]{2,1,0:T(8,128)(2,1)S(1)} %slice.17), channel_id=1, source_target_pairs={{64,0},{65,1},{66,2},{67,3},{68,4},{69,5},{70,6},{71,7},{72,8},{73... | collective-permute-start | bytes 878600 | tf_op jit(solution)/shard_map/ppermute | solution.py:575
  101.7 2.9 %unpack.1 = (f32[1,128]{1,0:T(1,128)}, f32[1,256]{1,0:T(1,128)}, f32[1,256]{1,0:T(1,128)}, f32[1,256,768]{2,1,0:T(8,128)}, f32[1,256,256]{2,1,0:T(8,128)}, /*ind...) custom-call(bf16[64,88,128]{2,1,0:T(8,128)(2,1)S(1)} %all_to_all.15.in_ref, f32[1,256]{1,0:T(1,128)} %bitcast.5), custom_call_target="tpu_custom_call" | custom-call | tf_op jit(solution)/shard_map/unpack/pallas_call | solution.py:576
  104.7 0.9 finish.1
  (23 shorter events, 0.9 us)
Async XLA Ops:
  0.6 16.5 %collective-permute-start.5 = (bf16[1,256,1024]{2,1,0:T(8,128)(2,1)}, bf16[1,256,1024]{2,1,0:T(8,128)(2,1)S(1)}, u32[]{:S(2)}, u32[]{:S(2)}) collective-permute-start(bf16[1,256,1024]{2,1,0:T(8,128)(2,1)} %up_own.1), channel_id=1, source_target_pairs={{0,64},{64,0},{1,65},{65,1},{2,66},{66,2},{3,67},{67,3},{4,68},{68... | collective-permute-start | bytes 1572872 | tf_op jit(solution)/shard_map/ppermute | solution.py:465
  0.7 16.4 %collective-permute-start.6 = (bf16[1,1024,256]{2,1,0:T(8,128)(2,1)}, bf16[1,1024,256]{2,1,0:T(8,128)(2,1)S(1)}, u32[]{:S(2)}, u32[]{:S(2)}) collective-permute-start(bf16[1,1024,256]{2,1,0:T(8,128)(2,1)} %down_own.1), channel_id=1, source_target_pairs={{0,64},{64,0},{1,65},{65,1},{2,66},{66,2},{3,67},{67,3},{4,68},{68... | collective-permute-start | bytes 1572872 | tf_op jit(solution)/shard_map/ppermute | solution.py:465
  1.2 15.9 %collective-permute-start.3 = (bf16[1,256,768]{2,1,0:T(8,128)(2,1)}, bf16[1,256,768]{2,1,0:T(8,128)(2,1)S(1)}, u32[]{:S(2)}, u32[]{:S(2)}) collective-permute-start(bf16[1,256,768]{2,1,0:T(8,128)(2,1)} %qkv_own.1), channel_id=1, source_target_pairs={{0,64},{64,0},{1,65},{65,1},{2,66},{66,2},{3,67},{67,3},{4,68},{68... | collective-permute-start | bytes 1179656 | tf_op jit(solution)/shard_map/ppermute | solution.py:465
  2.0 4.8 %collective-permute-start = (bf16[2,1,256]{2,1,0:T(2,128)(2,1)S(1)}, bf16[2,1,256]{2,1,0:T(2,128)(2,1)S(1)}, u32[]{:S(2)}, u32[]{:S(2)}) collective-permute-start(bf16[2,1,256]{2,1,0:T(2,128)(2,1)S(1)} %slice.12), channel_id=1, source_target_pairs={{0,1},{1,2},{2,3},{3,4},{4,5},{5,6},{6,7},{7,8},{8,9},{9,10},{10,1... | collective-permute-start | bytes 3080 | tf_op jit(solution)/shard_map/ppermute | solution.py:477
  7.7 13.2 %all-to-all-start = ((bf16[8,40,256]{2,1,0:T(8,128)(2,1)}), bf16[8,40,256]{2,1,0:T(8,128)(2,1)S(1)}, u32[]{:S(2)}, u32[]{:S(2)}) async-start(bf16[8,40,256]{2,1,0:T(8,128)(2,1)} %add_rim.1), calls=%async_computation | async-start | bytes 327680 | tf_op jit(solution)/shard_map/all_to_all | solution.py:510
  14.1 2.9 %collective-permute-start.4 = (bf16[1,256,256]{2,1,0:T(8,128)(2,1)}, bf16[1,256,256]{2,1,0:T(8,128)(2,1)S(1)}, u32[]{:S(2)}, u32[]{:S(2)}) collective-permute-start(bf16[1,256,256]{2,1,0:T(8,128)(2,1)} %out_own.1), channel_id=1, source_target_pairs={{0,64},{64,0},{1,65},{65,1},{2,66},{66,2},{3,67},{67,3},{4,68},{68... | collective-permute-start | bytes 393224 | tf_op jit(solution)/shard_map/ppermute | solution.py:465
  14.2 1.5 %collective-permute-start.1 = (f32[1,256]{1,0:T(1,128)}, f32[1,256]{1,0:T(1,128)S(1)}, u32[]{:S(2)}, u32[]{:S(2)}) collective-permute-start(f32[1,256]{1,0:T(1,128)} %gain_own_one_hbm.1), channel_id=1, source_target_pairs={{0,64},{64,0},{1,65},{65,1},{2,66},{66,2},{3,67},{67,3},{4,68},{68... | collective-permute-start | bytes 3080 | tf_op jit(solution)/shard_map/ppermute | solution.py:465
  15.7 1.4 %collective-permute-start.2 = (f32[1,256]{1,0:T(1,128)}, f32[1,256]{1,0:T(1,128)S(1)}, u32[]{:S(2)}, u32[]{:S(2)}) collective-permute-start(f32[1,256]{1,0:T(1,128)} %gain_own_two_hbm.1), channel_id=1, source_target_pairs={{0,64},{64,0},{1,65},{65,1},{2,66},{66,2},{3,67},{67,3},{4,68},{68... | collective-permute-start | bytes 3080 | tf_op jit(solution)/shard_map/ppermute | solution.py:465
  17.1 1.8 %copy-start.3 = (bf16[1,256,256]{2,1,0:T(8,128)(2,1)}, bf16[1,256,256]{2,1,0:T(8,128)(2,1)S(1)}, u32[]{:S(2)}) copy-start(bf16[1,256,256]{2,1,0:T(8,128)(2,1)S(1)} %collective-permute-done.4.out_far) | copy-start | bytes 393220
  17.1 0.8 copy-start.2
  17.1 0.9 copy-start
  18.1 0.8 copy-start.1
  32.8 3.5 %collective-permute-start.7 = (bf16[64,88,128]{2,1,0:T(8,128)(2,1)S(1)}, bf16[64,88,128]{2,1,0:T(8,128)(2,1)S(1)}, u32[]{:S(2)}, u32[]{:S(2)}) collective-permute-start(bf16[64,88,128]{2,1,0:T(8,128)(2,1)S(1)} %get-tuple-element.37), channel_id=1, source_target_pairs={{0,64},{64,0},{1,65},{65,1},{2,66},{66,2},{3,67},{67,3},{4,68},{68... | collective-permute-start | bytes 4325384 | tf_op jit(solution)/shard_map/ppermute | solution.py:465
  37.8 35.2 %all-to-all-start.1 = ((bf16[64,88,128]{2,1,0:T(8,128)(2,1)}), bf16[64,88,128]{2,1,0:T(8,128)(2,1)S(1)}, u32[]{:S(2)}, u32[]{:S(2)}) async-start(bf16[64,88,128]{2,1,0:T(8,128)(2,1)} %add_convert_fusion), calls=%async_computation.1 | async-start | bytes 2883584 | tf_op jit(solution)/shard_map/all_to_all | solution.py:565
  100.4 4.2 %collective-permute-start.8 = (bf16[13,88,128]{2,1,0:T(8,128)(2,1)S(1)}, bf16[13,88,128]{2,1,0:T(8,128)(2,1)S(1)}, u32[]{:S(2)}, u32[]{:S(2)}) collective-permute-start(bf16[13,88,128]{2,1,0:T(8,128)(2,1)S(1)} %slice.17), channel_id=1, source_target_pairs={{64,0},{65,1},{66,2},{67,3},{68,4},{69,5},{70,6},{71,7},{72,8},{73... | collective-permute-start | bytes 878600 | tf_op jit(solution)/shard_map/ppermute | solution.py:575

commit v7 on v6

--- a/solution.py
+++ b/solution.py
@@ -395,8 +395,8 @@
 
 
 def unpack_kernel(
-    in_ref, sdf_row_ref, loss_ref, sdf_ref, gain_one_ref, qkv_hbm, out_hbm, gain_two_ref, up_hbm, down_hbm,
-    qkv_ref, out_ref, up_ref, down_ref, store_sem,
+    in_ref, sdf_hbm, loss_ref, sdf_ref, gain_one_ref, qkv_hbm, out_hbm, gain_two_ref, up_hbm, down_hbm,
+    qkv_ref, out_ref, up_ref, down_ref, sdf_row_ref, store_sem, load_sem,
 ):
     micro = lax.axis_index("pipe")
     stores = []
@@ -406,6 +406,14 @@
         copy.start()
         stores.append(copy)
 
+    load = pltpu.make_async_copy(sdf_hbm, sdf_row_ref, load_sem.at[0])
+    load.start()
+    for ref, target, place, count in ((up_ref, up_hbm, 0, 4), (out_ref, out_hbm, 8, 1), (qkv_ref, qkv_hbm, 10, 3)):
+        for quarter in range(4):
+            for j in range(count):
+                wide(in_ref, 0, place + 2 * j, ref, 0, j * WIDTH, range(4 * quarter, 4 * quarter + 4))
+            rows = pl.ds(quarter * 64, 64)
+            store(ref.at[rows], target.at[0, rows])
     lines = []
     for c in range(15):
         pair = in_ref[STAT_AT + c, CHUNK:CHUNK_PAD, :].astype(F32)
@@ -415,6 +423,8 @@
         ref[0:1, 128:256] = lines[c + 1]
     loss_ref[0:1, :] = lines[6] / (2 * 12288)
 
+    load.wait()
+
     @pl.when(micro == 0)
     def _():
         for j in range(2):
@@ -431,12 +441,6 @@
     rows = pl.ds(2 * WIDTH, 2 * WIDTH)
     last = pltpu.make_async_copy(down_ref.at[rows], down_hbm.at[0, rows], store_sem.at[13])
     pl.when(micro == 1)(last.start)
-    for ref, target, place, count in ((up_ref, up_hbm, 0, 4), (out_ref, out_hbm, 8, 1), (qkv_ref, qkv_hbm, 10, 3)):
-        for quarter in range(4):
-            for j in range(count):
-                wide(in_ref, 0, place + 2 * j, ref, 0, j * WIDTH, range(4 * quarter, 4 * quarter + 4))
-            rows = pl.ds(quarter * 64, 64)
-            store(ref.at[rows], target.at[0, rows])
     pl.when(micro == 1)(last.wait)
     for copy in stores:
         copy.wait()
@@ -585,14 +589,16 @@
             jax.ShapeDtypeStruct((1, WIDTH, FF), F32),
             jax.ShapeDtypeStruct((1, FF, WIDTH), F32),
         ),
-        in_specs=[VMEM, VMEM],
+        in_specs=[VMEM, HBM],
         out_specs=(VMEM, VMEM, VMEM, HBM, HBM, VMEM, HBM, HBM),
         scratch_shapes=[
             pltpu.VMEM((WIDTH, 3 * WIDTH), F32),
             pltpu.VMEM((WIDTH, WIDTH), F32),
             pltpu.VMEM((WIDTH, FF), F32),
             pltpu.VMEM((FF, WIDTH), F32),
+            pltpu.VMEM((1, WIDTH), F32),
             pltpu.SemaphoreType.DMA((14,)),
+            pltpu.SemaphoreType.DMA((1,)),
         ],
         name="unpack",
         compiler_params=pltpu.CompilerParams(vmem_limit_bytes=16 * 2**20),

time: 108 us -> 107 us (level)
  transfers between devices with their start and end apart: 11 -> 11, of which waited for: 6 -> 6; matrix products, arithmetic and copies ran while one was open for 1% -> 1% of each run, Pallas kernels for 7% -> 6%
where the time goes in v7:
time: 107 us; the launch traced here: 105 us
  waiting for transfers between devices  28.9 us (27%)
  blocking collectives  26.9 us (25%)
  starting transfers between devices  24.7 us (23%)
  Pallas kernels  19.1 us (18%)
  local copies, waits for them, and re-layouts  2.63 us (2%)
  other arithmetic  1.85 us (2%)
    all_to_all x1, blocking collectives, shards(): lax.all_to_all(jnp.broadcast_to(summed[None], (rank_count, CHUNK_PAD, 128...  26.9 us
    all_to_all x1, waiting for transfers between devices, shards(): shares = lax.all_to_all(total, 'tok', 0, 0, tiled=True)  23.7 us
    pallas_call x1, Pallas kernels, shards(): pl.pallas_call(step_kernel, out_shape=(packet, packet), in_specs=[VMEM] *...  11.9 us
    all_to_all x1, starting transfers between devices, shards(): shares = lax.all_to_all(total, 'tok', 0, 0, tiled=True)  11.5 us
    all_to_all x1, starting transfers between devices, shards(): lax.all_to_all(outgoing, 'tok', 0, 0, axis_index_groups=groups, tiled=True)  6.44 us
    ppermute x7, waiting for transfers between devices, swap_pipe(): return lax.ppermute(value, 'pipe', [(0, 1), (1, 0)])  5.07 us
    ppermute x1, starting transfers between devices, shards(): lax.ppermute(coarse[:, -1:, :], 'tok', [(i, i + 1) for i in range(rank_co...  3.49 us
    pallas_call x1, Pallas kernels, shards(): pl.pallas_call(unpack_kernel, out_shape=(jax.ShapeDtypeStruct((1, 128), F...  2.22 us
  transfers between devices with their start and end apart: 11, of which 6 were waited for; matrix products, arithmetic and copies ran while one was open for 1% of the time, Pallas kernels for 6%

profile of v7, /device:TPU:0, one launch (start us, length us, event | category | flops | bytes accessed | tf_op | source)
XLA Modules:
  0.0 105.1 jit_solution(16096611815525205153)
XLA Ops:
  0.7 0.5 collective-permute-start.6
  1.3 0.7 slice.12
  2.0 3.5 %collective-permute-start = (bf16[2,1,256]{2,1,0:T(2,128)(2,1)S(1)}, bf16[2,1,256]{2,1,0:T(2,128)(2,1)S(1)}, u32[]{:S(2)}, u32[]{:S(2)}) collective-permute-start(bf16[2,1,256]{2,1,0:T(2,128)(2,1)S(1)} %slice.12), channel_id=1, source_target_pairs={{0,1},{1,2},{2,3},{3,4},{4,5},{5,6},{6,7},{7,8},{8,9},{9,10},{10,1... | collective-permute-start | bytes 3080 | tf_op jit(solution)/shard_map/ppermute | solution.py:481
  5.5 1.2 %embed.1 = (bf16[8,40,256]{2,1,0:T(8,128)(2,1)S(1)}, bf16[16,256]{1,0:T(8,128)(2,1)S(1)}) custom-call(bf16[2,256,256]{2,1,0:T(8,128)(2,1)} %features_hbm.1, bf16[2,64,256]{2,1,0:T(8,128)(2,1)} %coarse_hbm.1, s32[2,256]{1,0:T(2,128)} %parent_hbm.1, f32[2,256]{1,0:T(2,128)} %target_hbm.1), custom_call_target="tpu_custom_call" | custom-call | tf_op jit(solution)/shard_map/embed/pallas_call | solution.py:487
  6.8 0.9 add_rim.1
  7.7 6.4 %all-to-all-start = ((bf16[8,40,256]{2,1,0:T(8,128)(2,1)}), bf16[8,40,256]{2,1,0:T(8,128)(2,1)S(1)}, u32[]{:S(2)}, u32[]{:S(2)}) async-start(bf16[8,40,256]{2,1,0:T(8,128)(2,1)} %add_rim.1), calls=%async_computation | async-start | bytes 327680 | tf_op jit(solution)/shard_map/all_to_all | solution.py:514
  14.2 0.5 collective-permute-start.1
  14.7 1.0 collective-permute-done.1.gain_far_one
  15.7 0.3 collective-permute-start.2
  16.0 1.0 collective-permute-done.2.gain_far_two
  17.1 0.7 copy-done.2
  18.1 0.8 copy-done.1
  18.8 2.0 %arrange.1 = (bf16[2,256,768]{2,1,0:T(8,128)(2,1)S(1)}, bf16[2,256,256]{2,1,0:T(8,128)(2,1)S(1)}, bf16[2,256,1024]{2,1,0:T(8,128)(2,1)S(1)}, bf16[2,1024,256]{2,...) custom-call(f32[1,256]{1,0:T(1,128)S(1)} %collective-permute-done.1.gain_far_one, ...), custom_call_target="tpu_custom_call" | custom-call | tf_op jit(solution)/shard_map/arrange/pallas_call | solution.py:516
  20.9 11.9 %step.1 = (bf16[64,88,128]{2,1,0:T(8,128)(2,1)S(1)}, bf16[64,88,128]{2,1,0:T(8,128)(2,1)S(1)}) custom-call(bf16[8,40,256]{2,1,0:T(8,128)(2,1)S(1)} %all-to-all-done.received_ref, bf16[2,256,768]{2,1,0:T(8,128)(2,1)S(1)} %get-tuple-element.29.w_qkv, bf16[2,256,256]{2,1,0:T(8,128)(2,1)S(1)} %get-tuple-element.30.w_out, ...), custom_call_target="tpu_custom_call" | custom-call | tf_op jit(solution)/shard_map/step/pallas_call | solution.py:542
  32.8 0.5 collective-permute-start.7
  33.3 3.0 %collective-permute-done.7 = bf16[64,88,128]{2,1,0:T(8,128)(2,1)S(1)} collective-permute-done((bf16[64,88,128]{2,1,0:T(8,128)(2,1)S(1)}, bf16[64,88,128]{2,1,0:T(8,128)(2,1)S(1)}, u32[]{:S(2)}, u32[]{:S(2)}) %collective-permute-start.7) | collective-permute-done | bytes 1441824 | tf_op jit(solution)/shard_map/ppermute | solution.py:469
  36.3 1.5 %add_convert_fusion = bf16[64,88,128]{2,1,0:T(8,128)(2,1)} fusion(bf16[64,88,128]{2,1,0:T(8,128)(2,1)S(1)} %collective-permute-done.7, bf16[64,88,128]{2,1,0:T(8,128)(2,1)S(1)} %get-tuple-element.36), kind=kLoop, calls=%fused_computation.1 | loop fusion | flops 2883584 | bytes 4325376 | tf_op jit(solution)/shard_map/convert_element_type | solution.py:568
  37.8 11.5 %all-to-all-start.1 = ((bf16[64,88,128]{2,1,0:T(8,128)(2,1)}), bf16[64,88,128]{2,1,0:T(8,128)(2,1)S(1)}, u32[]{:S(2)}, u32[]{:S(2)}) async-start(bf16[64,88,128]{2,1,0:T(8,128)(2,1)} %add_convert_fusion), calls=%async_computation.1 | async-start | bytes 2883584 | tf_op jit(solution)/shard_map/all_to_all | solution.py:569
  49.3 23.7 %all-to-all-done.1 = bf16[64,88,128]{2,1,0:T(8,128)(2,1)S(1)} async-done(((bf16[64,88,128]{2,1,0:T(8,128)(2,1)}), bf16[64,88,128]{2,1,0:T(8,128)(2,1)S(1)}, u32[]{:S(2)}, u32[]{:S(2)}) %all-to-all-start.1) | async-done | bytes 1441824 | tf_op jit(solution)/shard_map/all_to_all | solution.py:569
  73.0 0.2 convert_reduce_fusion
  73.5 26.9 %all_to_all.15.in_ref = bf16[64,88,128]{2,1,0:T(8,128)(2,1)S(1)} all-to-all(bf16[64,88,128]{2,1,0:T(8,128)(2,1)S(1)} %broadcast_in_dim.35), channel_id=1, replica_groups=mesh['pipe'=2,'tok'=64] {'tok'}, dimensions={0} | all-to-all | bytes 2883584 | tf_op jit(solution)/shard_map/all_to_all | solution.py:576
  100.4 1.3 %collective-permute-start.8 = (bf16[13,88,128]{2,1,0:T(8,128)(2,1)S(1)}, bf16[13,88,128]{2,1,0:T(8,128)(2,1)S(1)}, u32[]{:S(2)}, u32[]{:S(2)}) collective-permute-start(bf16[13,88,128]{2,1,0:T(8,128)(2,1)S(1)} %slice.17), channel_id=1, source_target_pairs={{64,0},{65,1},{66,2},{67,3},{68,4},{69,5},{70,6},{71,7},{72,8},{73... | collective-permute-start | bytes 878600 | tf_op jit(solution)/shard_map/ppermute | solution.py:579
  101.7 2.2 %unpack.1 = (f32[1,128]{1,0:T(1,128)}, f32[1,256]{1,0:T(1,128)}, f32[1,256]{1,0:T(1,128)}, f32[1,256,768]{2,1,0:T(8,128)}, f32[1,256,256]{2,1,0:T(8,128)}, /*ind...) custom-call(bf16[64,88,128]{2,1,0:T(8,128)(2,1)S(1)} %all_to_all.15.in_ref, f32[1,256]{1,0:T(1,128)} %bitcast.5), custom_call_target="tpu_custom_call" | custom-call | tf_op jit(solution)/shard_map/unpack/pallas_call | solution.py:580
  104.0 0.9 finish.1
  (23 shorter events, 0.9 us)
Async XLA Ops:
  0.6 16.5 %collective-permute-start.5 = (bf16[1,256,1024]{2,1,0:T(8,128)(2,1)}, bf16[1,256,1024]{2,1,0:T(8,128)(2,1)S(1)}, u32[]{:S(2)}, u32[]{:S(2)}) collective-permute-start(bf16[1,256,1024]{2,1,0:T(8,128)(2,1)} %up_own.1), channel_id=1, source_target_pairs={{0,64},{64,0},{1,65},{65,1},{2,66},{66,2},{3,67},{67,3},{4,68},{68... | collective-permute-start | bytes 1572872 | tf_op jit(solution)/shard_map/ppermute | solution.py:469
  0.7 16.4 %collective-permute-start.6 = (bf16[1,1024,256]{2,1,0:T(8,128)(2,1)}, bf16[1,1024,256]{2,1,0:T(8,128)(2,1)S(1)}, u32[]{:S(2)}, u32[]{:S(2)}) collective-permute-start(bf16[1,1024,256]{2,1,0:T(8,128)(2,1)} %down_own.1), channel_id=1, source_target_pairs={{0,64},{64,0},{1,65},{65,1},{2,66},{66,2},{3,67},{67,3},{4,68},{68... | collective-permute-start | bytes 1572872 | tf_op jit(solution)/shard_map/ppermute | solution.py:469
  1.2 15.9 %collective-permute-start.3 = (bf16[1,256,768]{2,1,0:T(8,128)(2,1)}, bf16[1,256,768]{2,1,0:T(8,128)(2,1)S(1)}, u32[]{:S(2)}, u32[]{:S(2)}) collective-permute-start(bf16[1,256,768]{2,1,0:T(8,128)(2,1)} %qkv_own.1), channel_id=1, source_target_pairs={{0,64},{64,0},{1,65},{65,1},{2,66},{66,2},{3,67},{67,3},{4,68},{68... | collective-permute-start | bytes 1179656 | tf_op jit(solution)/shard_map/ppermute | solution.py:469
  2.0 4.8 %collective-permute-start = (bf16[2,1,256]{2,1,0:T(2,128)(2,1)S(1)}, bf16[2,1,256]{2,1,0:T(2,128)(2,1)S(1)}, u32[]{:S(2)}, u32[]{:S(2)}) collective-permute-start(bf16[2,1,256]{2,1,0:T(2,128)(2,1)S(1)} %slice.12), channel_id=1, source_target_pairs={{0,1},{1,2},{2,3},{3,4},{4,5},{5,6},{6,7},{7,8},{8,9},{9,10},{10,1... | collective-permute-start | bytes 3080 | tf_op jit(solution)/shard_map/ppermute | solution.py:481
  7.7 13.2 %all-to-all-start = ((bf16[8,40,256]{2,1,0:T(8,128)(2,1)}), bf16[8,40,256]{2,1,0:T(8,128)(2,1)S(1)}, u32[]{:S(2)}, u32[]{:S(2)}) async-start(bf16[8,40,256]{2,1,0:T(8,128)(2,1)} %add_rim.1), calls=%async_computation | async-start | bytes 327680 | tf_op jit(solution)/shard_map/all_to_all | solution.py:514
  14.1 2.9 %collective-permute-start.4 = (bf16[1,256,256]{2,1,0:T(8,128)(2,1)}, bf16[1,256,256]{2,1,0:T(8,128)(2,1)S(1)}, u32[]{:S(2)}, u32[]{:S(2)}) collective-permute-start(bf16[1,256,256]{2,1,0:T(8,128)(2,1)} %out_own.1), channel_id=1, source_target_pairs={{0,64},{64,0},{1,65},{65,1},{2,66},{66,2},{3,67},{67,3},{4,68},{68... | collective-permute-start | bytes 393224 | tf_op jit(solution)/shard_map/ppermute | solution.py:469
  14.2 1.5 %collective-permute-start.1 = (f32[1,256]{1,0:T(1,128)}, f32[1,256]{1,0:T(1,128)S(1)}, u32[]{:S(2)}, u32[]{:S(2)}) collective-permute-start(f32[1,256]{1,0:T(1,128)} %gain_own_one_hbm.1), channel_id=1, source_target_pairs={{0,64},{64,0},{1,65},{65,1},{2,66},{66,2},{3,67},{67,3},{4,68},{68... | collective-permute-start | bytes 3080 | tf_op jit(solution)/shard_map/ppermute | solution.py:469
  15.7 1.4 %collective-permute-start.2 = (f32[1,256]{1,0:T(1,128)}, f32[1,256]{1,0:T(1,128)S(1)}, u32[]{:S(2)}, u32[]{:S(2)}) collective-permute-start(f32[1,256]{1,0:T(1,128)} %gain_own_two_hbm.1), channel_id=1, source_target_pairs={{0,64},{64,0},{1,65},{65,1},{2,66},{66,2},{3,67},{67,3},{4,68},{68... | collective-permute-start | bytes 3080 | tf_op jit(solution)/shard_map/ppermute | solution.py:469
  17.1 1.8 %copy-start.3 = (bf16[1,256,256]{2,1,0:T(8,128)(2,1)}, bf16[1,256,256]{2,1,0:T(8,128)(2,1)S(1)}, u32[]{:S(2)}) copy-start(bf16[1,256,256]{2,1,0:T(8,128)(2,1)S(1)} %collective-permute-done.4.out_far) | copy-start | bytes 393220
  17.1 0.8 copy-start.2
  17.1 0.9 copy-start
  18.1 0.8 copy-start.1
  32.8 3.5 %collective-permute-start.7 = (bf16[64,88,128]{2,1,0:T(8,128)(2,1)S(1)}, bf16[64,88,128]{2,1,0:T(8,128)(2,1)S(1)}, u32[]{:S(2)}, u32[]{:S(2)}) collective-permute-start(bf16[64,88,128]{2,1,0:T(8,128)(2,1)S(1)} %get-tuple-element.37), channel_id=1, source_target_pairs={{0,64},{64,0},{1,65},{65,1},{2,66},{66,2},{3,67},{67,3},{4,68},{68... | collective-permute-start | bytes 4325384 | tf_op jit(solution)/shard_map/ppermute | solution.py:469
  37.8 35.2 %all-to-all-start.1 = ((bf16[64,88,128]{2,1,0:T(8,128)(2,1)}), bf16[64,88,128]{2,1,0:T(8,128)(2,1)S(1)}, u32[]{:S(2)}, u32[]{:S(2)}) async-start(bf16[64,88,128]{2,1,0:T(8,128)(2,1)} %add_convert_fusion), calls=%async_computation.1 | async-start | bytes 2883584 | tf_op jit(solution)/shard_map/all_to_all | solution.py:569
  100.4 3.5 %collective-permute-start.8 = (bf16[13,88,128]{2,1,0:T(8,128)(2,1)S(1)}, bf16[13,88,128]{2,1,0:T(8,128)(2,1)S(1)}, u32[]{:S(2)}, u32[]{:S(2)}) collective-permute-start(bf16[13,88,128]{2,1,0:T(8,128)(2,1)S(1)} %slice.17), channel_id=1, source_target_pairs={{64,0},{65,1},{66,2},{67,3},{68,4},{69,5},{70,6},{71,7},{72,8},{73... | collective-permute-start | bytes 878600 | tf_op jit(solution)/shard_map/ppermute | solution.py:579
